TPU v7x, 128 devices: a whole 4x4x4 slice. The times are simulated.
128 devices in a mesh: view: 8 (over y, core), space: 16 (over z, x).
Axes of the slice: x: 4, y: 4, z: 4, core: 2. Of those that a mesh axis runs over, the one named last changes fastest.
Arguments:
- brick_feats: bfloat16 [8192, 512, 32], P(('view', 'space')), may hold values from -6 to 6
- interp_weights: bfloat16 [16384, 128, 512], P(('view', 'space')), may hold values from 0 to 0.099609375
- block_owner: int32 [16384, 1], P(('view', 'space')), may hold values from 0 to 127; in each aligned block of 128 rows (0 to 127, 128 to 255, ...) at most 2 rows name the same one
- block_brick: int32 [16384, 1], P(('view', 'space')), may hold values from 0 to 63
- sample_count: int32 [65536], P(('view', 'space')), may hold values from 1 to 32
- target: float32 [3, 65536], P(None, ('view', 'space')), may hold values from 0 to 1
- w_in: bfloat16 [32, 256], replicated, may hold values from -1 to 1
- b_in: float32 [256], replicated, may hold values from -3 to 3
- w_hid: bfloat16 [256, 256], replicated, may hold values from -0.5 to 0.5
- b_hid: float32 [256], replicated, may hold values from -3 to 3
- w_out: bfloat16 [4, 256], replicated, may hold values from -0.5 to 0.5
- b_out: float32 [4], replicated, may hold values from -2 to 2
Outputs:
- brick_grad: float32 [8192, 512, 32], P(('view', 'space'))
- color: float32 [3, 65536], P(None, ('view', 'space'))
- g_w_in: float32 [32, 256], replicated
- g_b_in: float32 [256], replicated
- g_w_hid: float32 [256, 256], replicated
- g_b_hid: float32 [256], replicated
- g_w_out: float32 [4, 256], replicated
- g_b_out: float32 [4], replicated
Inputs may be any that keep to these rules, and one draw needn't show every extreme that they name: `block_owner`: among the 128 rows of one device no owner appears more than 2 times, and some owner appears exactly 2 times in some devices' rows.
All inputs are finite; a program needn't handle non-finite values.
Results may differ from a plain program's by a relative error of at most 0.0065.
The roundings to bfloat16 on the way count: a program that leaves them out, or rounds other values in their place, can miss the bound.
Values may be sent and summed in bfloat16 or wider, within the bound.
No kernel may reach another device: no remote copies, remote signals or barrier semaphores. Data moves between devices by JAX's collectives and lax.ppermute only.
A program may use at most 256 MiB of HBM per device.

v0:
```python
import jax
import jax.numpy as jnp
from jax import lax
from jax.sharding import PartitionSpec as P

FEAT = 32
VOX = 512
BLOCK = 128
RAY_LEN = 32


step_len = 0.05


def contract_rows(left, right):
    return lax.dot_general(
        left, right, (((0,), (0,)), ((), ())), preferred_element_type=jnp.float32
    )


def contract_cols(left, right):
    return lax.dot_general(
        left, right, (((1,), (1,)), ((), ())), preferred_element_type=jnp.float32
    )


def composite(raw_out, counts, goal_rgb):
    ray_count = counts.shape[0]
    shaped = raw_out.reshape(ray_count, RAY_LEN, 4)
    sigma = jax.nn.softplus(shaped[:, :, 0])
    shades = jax.nn.sigmoid(shaped[:, :, 1:])
    places = lax.broadcasted_iota(jnp.int32, (ray_count, RAY_LEN), 1)
    is_live = (places < counts[:, None]).astype(jnp.float32)
    depth = step_len * sigma * is_live
    alpha = 1.0 - jnp.exp(-depth)
    trans = jnp.exp(depth - jnp.cumsum(depth, axis=1))
    weight = trans * alpha
    rendered = jnp.sum(weight[:, :, None] * shades, axis=1).T
    loss = 0.5 * jnp.sum(jnp.square(rendered - goal_rgb))
    return (loss, rendered)


def network_pass(feats, counts, goal_rgb, w_in, b_in, w_hid, b_hid, w_out, b_out):
    pre_one = jnp.dot(feats, w_in, preferred_element_type=jnp.float32) + b_in
    act_one = jnp.maximum(pre_one, 0.0).astype(jnp.bfloat16)
    pre_two = jnp.dot(act_one, w_hid, preferred_element_type=jnp.float32) + b_hid
    act_two = jnp.maximum(pre_two, 0.0).astype(jnp.bfloat16)
    raw_out = contract_cols(act_two, w_out) + b_out

    def render_loss(values):
        return composite(values, counts, goal_rgb)

    loss, pullback, rendered = jax.vjp(render_loss, raw_out, has_aux=True)
    d_raw = pullback(jnp.ones((), jnp.float32))[0]
    d_raw_b = d_raw.astype(jnp.bfloat16)
    g_w_out = contract_rows(d_raw_b, act_two)
    g_b_out = jnp.sum(d_raw, axis=0)
    d_two = jnp.dot(d_raw_b, w_out, preferred_element_type=jnp.float32) * (pre_two > 0.0)
    d_two_b = d_two.astype(jnp.bfloat16)
    g_w_hid = contract_rows(act_one, d_two_b)
    g_b_hid = jnp.sum(d_two, axis=0)
    d_one = contract_cols(d_two_b, w_hid) * (pre_one > 0.0)
    d_one_b = d_one.astype(jnp.bfloat16)
    g_w_in = contract_rows(feats, d_one_b)
    g_b_in = jnp.sum(d_one, axis=0)
    d_feats = contract_cols(d_one_b, w_in).astype(jnp.bfloat16)
    return (rendered, d_feats, (g_w_in, g_b_in, g_w_hid, g_b_hid, g_w_out, g_b_out))


def body(
    brick_feats,
    interp_weights,
    block_owner,
    block_brick,
    sample_count,
    target,
    w_in,
    b_in,
    w_hid,
    b_hid,
    w_out,
    b_out,
):
    own_blocks = interp_weights.shape[0]
    own_bricks = brick_feats.shape[0]
    dev_count = lax.axis_size(("view", "space"))
    capacity = max(2, 2 * own_blocks // dev_count)
    owners = block_owner[:, 0]
    local_ids = block_brick[:, 0]
    row_index = lax.broadcasted_iota(jnp.int32, (own_blocks, own_blocks), 0)
    col_index = lax.broadcasted_iota(jnp.int32, (own_blocks, own_blocks), 1)
    matches = (owners[:, None] == owners[None, :]) & (col_index < row_index)
    ranks = jnp.sum(matches.astype(jnp.int32), axis=1)
    slots = owners * capacity + ranks
    requested = jnp.full((dev_count * capacity,), -1, jnp.int32).at[slots].set(local_ids)
    requested = requested.reshape(dev_count, capacity)
    wanted = lax.all_to_all(requested, ("view", "space"), split_axis=0, concat_axis=0, tiled=True)
    picked = jnp.maximum(wanted, 0)
    located = brick_feats[picked]
    filled = jnp.where((wanted >= 0)[:, :, None, None], located, jnp.zeros_like(located))
    fetched = lax.all_to_all(filled, ("view", "space"), split_axis=0, concat_axis=0, tiled=True)
    fetched_rows = fetched.reshape(dev_count * capacity, VOX, FEAT)[slots]
    feats = jnp.einsum(
        "bsv,bvf->bsf", interp_weights, fetched_rows, preferred_element_type=jnp.float32
    )
    feats = feats.astype(jnp.bfloat16).reshape(own_blocks * BLOCK, FEAT)
    rendered, d_feats, param_sums = network_pass(
        feats, sample_count, target, w_in, b_in, w_hid, b_hid, w_out, b_out
    )
    block_grad = jnp.einsum(
        "bsv,bsf->bvf",
        interp_weights,
        d_feats.reshape(own_blocks, BLOCK, FEAT),
        preferred_element_type=jnp.float32,
    )
    outgoing = jnp.zeros((dev_count * capacity, VOX, FEAT), jnp.float32).at[slots].set(block_grad)
    outgoing = outgoing.reshape(dev_count, capacity, VOX, FEAT)
    returned = lax.all_to_all(outgoing, ("view", "space"), split_axis=0, concat_axis=0, tiled=True)
    returned = returned.reshape(dev_count * capacity, VOX, FEAT)
    flat_ids = wanted.reshape(dev_count * capacity)
    target_rows = jnp.where(flat_ids >= 0, flat_ids, own_bricks)
    brick_grad = (
        jnp.zeros((own_bricks, VOX, FEAT), jnp.float32).at[target_rows].add(returned, mode="drop")
    )
    totals = lax.psum(
        (param_sums[0], param_sums[1], param_sums[2], param_sums[3], param_sums[4], param_sums[5]),
        ("view", "space"),
    )
    ray_total = sample_count.shape[0] * dev_count
    scaled = tuple((total / ray_total for total in totals))
    return (brick_grad, rendered, scaled[0], scaled[1], scaled[2], scaled[3], scaled[4], scaled[5])


def solution(mesh):
    return jax.shard_map(
        body,
        mesh=mesh,
        in_specs=(
            P(("view", "space"), None, None),
            P(("view", "space"), None, None),
            P(("view", "space"), None),
            P(("view", "space"), None),
            P(("view", "space")),
            P(None, ("view", "space")),
            P(),
            P(),
            P(),
            P(),
            P(),
            P(),
        ),
        out_specs=(
            P(("view", "space"), None, None),
            P(None, ("view", "space")),
            P(),
            P(),
            P(),
            P(),
            P(),
            P(),
        ),
        check_vma=False,
    )
```

profile of v0, /device:TPU:1, one launch (start us, length us, event | category | flops | bytes accessed | tf_op | source)
XLA Modules:
  0.0 663.0 jit_solution(6460754837386347434)
XLA Ops:
  7.2 1.0 convert_reduce_fusion
  8.2 0.7 fusion.32
  8.8 1.1 scatter_custom_fusion
  10.0 0.1 all_to_all.12
  10.1 21.1 %all_to_all.19 = s32[128,1,2]{2,1,0:T(1,128)S(1)} all-to-all(s32[128,1,2]{2,1,0:T(1,128)S(1)} %bitcast.80), channel_id=1, replica_groups=mesh['view'=8,'space'=16] {'view','space'}, dimensions={0} | all-to-all | bytes 2048 | tf_op jit(solution)/shard_map/all_to_all | solution.py:97
  31.2 0.5 broadcast.210
  31.7 1.0 maximum_reduce_fusion
  32.7 0.1 reshape.163
  33.0 0.1 copy.43
  33.0 0.1 copy.44
  33.2 8.4 %gather_fusion = bf16[256,512,32]{1,2,0:T(8,128)(2,1)} fusion(bf16[64,512,32]{1,2,0:T(8,128)(2,1)S(1)} %copy-done, s32[1024]{0:T(1024)S(1)} %pad_clamp_fusion.1), kind=kCustom, calls=%fused_computation | custom fusion | bytes 16778240 | tf_op jit(solution)/shard_map/gather | solution.py:99
  41.6 7.3 %broadcast_select_fusion = bf16[128,2,512,32]{2,3,1,0:T(8,128)(2,1)} fusion(bf16[128,2,512,32]{2,3,1,0:T(8,128)(2,1)} %bitcast.78, pred[128,2]{1,0:T(8,128)(4,1)S(1)} %copy.44), kind=kLoop, calls=%fused_computation.13 | loop fusion | flops 4194304 | bytes 16777472 | tf_op jit(solution)/shard_map/jit(_where)/select_n | solution.py:100
  48.9 5.4 all-to-all-start.1
  54.3 98.4 %all-to-all-done.1 = bf16[128,2,512,32]{2,3,1,0:T(8,128)(2,1)} async-done(((bf16[128,2,512,32]{2,3,1,0:T(8,128)(2,1)}), bf16[128,2,512,32]{2,3,1,0:T(8,128)(2,1)}, u32[]{:S(2)}, u32[]{:S(2)}) %all-to-all-start.1) | async-done | bytes 8388640 | tf_op jit(solution)/shard_map/all_to_all | solution.py:101
  152.7 6.2 gather_fusion.1
  158.9 12.7 %fusion.10 = bf16[128,4,8,128]{3,2,1,0:T(8,128)(2,1)S(1)} fusion(bf16[128,512,32]{1,2,0:T(8,128)(2,1)} %gather_fusion.1, bf16[128,128,512]{2,1,0:T(8,128)(2,1)} %param.13), kind=kOutput, calls=%fused_computation.24 | convolution fusion | flops 537395200 | bytes 22020096 | tf_op jit(solution)/shard_map/bsv,bvf->bsf/dot_general | solution.py:103
  171.7 8.1 %convolution_add_fusion = f32[16384,256]{1,0:T(8,128)} fusion(bf16[32,256]{1,0:T(8,128)(2,1)S(1)} %copy-done.3, f32[256]{0:T(256)S(1)} %copy-done.8, bf16[128,4,8,128]{3,2,1,0:T(8,128)(2,1)S(1)} %fusion.10), kind=kOutput, calls=%fused_computation.5 | convolution fusion | flops 272629760 | bytes 17843200 | tf_op jit(solution)/shard_map/dot_general | solution.py:44
  179.8 13.9 %convolution_add_fusion.1 = f32[16384,256]{1,0:T(8,128)} fusion(bf16[256,256]{1,0:T(8,128)(2,1)S(1)} %copy-done.2, f32[256]{0:T(256)S(1)} %copy-done.9, f32[16384,256]{1,0:T(8,128)} %convolution_add_fusion), kind=kOutput, calls=%fused_computation.7 | convolution fusion | flops 2160066560 | bytes 33686528 | tf_op jit(solution)/shard_map/dot_general | solution.py:46
  193.6 8.1 %convolution_add_fusion.2 = f32[16384,4]{0,1:T(4,128)S(1)} fusion(bf16[4,256]{1,0:T(4,128)(2,1)S(1)} %copy-done.6, f32[16384,256]{1,0:T(8,128)} %convolution_add_fusion.1, f32[4]{0:T(128)S(1)} %copy-done.10), kind=kOutput, calls=%fused_computation.10 | convolution fusion | flops 42008576 | bytes 17041424 | tf_op jit(solution)/shard_map/dot_general | solution.py:22
  201.7 0.4 reshape.157
  202.2 0.1 copy.50
  202.5 0.2 copy.51
  202.8 0.1 fusion.19
  203.0 0.3 reduce_window_sum.23
  203.3 0.1 fusion.22
  203.4 0.1 fusion.17
  203.6 0.3 copy.48
  203.9 0.6 convert_element_type.39
  204.4 9.7 %fusion.40 = (f32[256]{0:T(256)S(1)}, bf16[16384,256]{1,0:T(8,128)(2,1)}) fusion(bf16[16384,4]{0,1:T(4,128)(2,1)S(1)} %convert_element_type.39, bf16[4,256]{1,0:T(4,128)(2,1)S(1)} %copy-done.6, f32[16384,256]{1,0:T(8,128)} %convolution_add_fusion.1), kind=kOutput, calls=%fused_computation.86 | convolution fusion | flops 50331392 | bytes 25299968 | tf_op jit(solution)/shard_map/dot_general | solution.py:58
  214.2 14.6 %fusion.39 = (f32[256]{0:T(256)S(1)}, bf16[16384,256]{1,0:T(8,128)(2,1)}) fusion(bf16[256,256]{1,0:T(8,128)(2,1)S(1)} %copy-done.2, bf16[16384,256]{1,0:T(8,128)(2,1)} %get-tuple-element.22, f32[16384,256]{1,0:T(8,128)} %convolution_add_fusion), kind=kOutput, calls=%fused_computation.85 | convolution fusion | flops 2164260608 | bytes 33686528 | tf_op jit(solution)/shard_map/dot_general | solution.py:22
  228.8 5.9 fusion.7
  234.7 11.3 %convolution_bitcast_fusion = f32[128,512,32]{1,2,0:T(8,128)} fusion(bf16[128,128,512]{2,1,0:T(8,128)(2,1)} %param.13, bf16[4,128,8,128]{3,2,1,0:T(8,128)(2,1)S(1)} %fusion.7), kind=kOutput, calls=%fused_computation.20 | convolution fusion | flops 536870912 | bytes 26214400 | tf_op jit(solution)/shard_map/bsv,bsf->bvf/dot_general | solution.py:110
  246.0 7.9 %broadcast_in_dim.24 = f32[256,512,32]{1,2,0:T(8,128)} broadcast(f32[]{:T(128)} %constant.18.clone.1), dimensions={} | broadcast | bytes 16777220 | tf_op jit(solution)/shard_map/broadcast_in_dim | solution.py:116
  253.8 23.3 %scatter_fusion = f32[256,512,32]{1,2,0:T(8,128)} fusion(f32[256,512,32]{1,2,0:T(8,128)} %broadcast_in_dim.24, s32[128]{0:T(128)S(1)} %fusion.32, f32[128,512,32]{1,2,0:T(8,128)} %convolution_bitcast_fusion), kind=kCustom, calls=%fused_computation.3 | custom fusion | bytes 25166336 | tf_op jit(solution)/shard_map/scatter | solution.py:116
  277.2 17.8 %all-to-all-start.2 = ((f32[128,2,512,32]{2,3,1,0:T(8,128)}), f32[128,2,512,32]{2,3,1,0:T(8,128)}, u32[]{:S(2)}, u32[]{:S(2)}) async-start(f32[128,2,512,32]{2,3,1,0:T(8,128)} %bitcast.79), calls=%async_computation.2 | async-start | bytes 33554432 | tf_op jit(solution)/shard_map/all_to_all | solution.py:118
  294.9 0.3 all-reduce.5.cloned.1.call-start
  295.3 0.1 reshape.154
  295.4 11.2 %fusion.3 = f32[256,256]{1,0:T(8,128)} fusion(bf16[16384,256]{1,0:T(8,128)(2,1)} %get-tuple-element.22, f32[16384,256]{1,0:T(8,128)} %convolution_add_fusion), kind=kOutput, calls=%fused_computation.17 | convolution fusion | flops 2155872256 | bytes 25427968 | tf_op jit(solution)/shard_map/dot_general | solution.py:16
  306.6 4.9 fusion
  311.6 7.0 %fusion.6 = f32[4,256]{1,0:T(4,128)S(1)} fusion(bf16[16384,4]{0,1:T(4,128)(2,1)S(1)} %convert_element_type.39, f32[16384,256]{1,0:T(8,128)} %convolution_add_fusion.1), kind=kOutput, calls=%fused_computation.21 | convolution fusion | flops 41943040 | bytes 16912384 | tf_op jit(solution)/shard_map/dot_general | solution.py:16
  318.6 280.6 %all-reduce.2 = (f32[32,256]{1,0:T(8,128)S(1)}, f32[256]{0:T(256)S(1)}, f32[256]{0:T(256)S(1)}, f32[4,256]{1,0:T(4,128)S(1)}, f32[4]{0:T(128)S(1)}) all-reduce(f32[32,256]{1,0:T(8,128)S(1)} %fusion, f32[256]{0:T(256)S(1)} %get-tuple-element.19, f32[256]{0:T(256)S(1)} %get-tuple-element.21, ...), channel_id=1, replica_groups=mesh['view'=8,'space'=16] {'view','space'}, use_global_device_ids=true, to_apply=%region_8.9 | all-reduce | flops 9732 | bytes 77856 | tf_op jit(solution)/shard_map/psum | solution.py:125
  599.1 0.6 broadcast_multiply_fusion.3
  599.7 0.6 broadcast_multiply_fusion.2
  600.3 0.6 broadcast_multiply_fusion.1
  600.9 0.5 broadcast_multiply_fusion.5
  601.4 1.7 broadcast_multiply_fusion
  603.1 2.5 broadcast_in_dim.21
  605.6 50.5 %scatter_fusion.1 = f32[64,512,32]{1,2,0:T(8,128)} fusion(f32[64,512,32]{1,2,0:T(8,128)} %broadcast_in_dim.21, s32[256]{0:T(256)S(1)} %bitcast.82, f32[256,512,32]{1,2,0:T(8,128)} %bitcast.16), kind=kCustom, calls=%fused_computation.4 | custom fusion | flops 4194304 | bytes 50332672 | tf_op jit(solution)/shard_map/scatter-add | solution.py:123
  (37 shorter events, 0.6 us)
Async XLA Ops:
  7.2 26.0 %copy-start = (bf16[64,512,32]{1,2,0:T(8,128)(2,1)S(1)}, bf16[64,512,32]{1,2,0:T(8,128)(2,1)}, u32[]{:S(2)}) copy-start(bf16[64,512,32]{1,2,0:T(8,128)(2,1)} %param.12) | copy-start | bytes 6291460
  48.9 103.8 %all-to-all-start.1 = ((bf16[128,2,512,32]{2,3,1,0:T(8,128)(2,1)}), bf16[128,2,512,32]{2,3,1,0:T(8,128)(2,1)}, u32[]{:S(2)}, u32[]{:S(2)}) async-start(bf16[128,2,512,32]{2,3,1,0:T(8,128)(2,1)} %broadcast_select_fusion), calls=%async_computation.1 | async-start | bytes 16777216 | tf_op jit(solution)/shard_map/all_to_all | solution.py:101
  158.9 12.7 %copy-start.3 = (bf16[32,256]{1,0:T(8,128)(2,1)S(1)}, bf16[32,256]{1,0:T(8,128)(2,1)}, u32[]{:S(2)}) copy-start(bf16[32,256]{1,0:T(8,128)(2,1)} %param.18) | copy-start | bytes 49156
  158.9 12.7 %copy-start.8 = (f32[256]{0:T(256)S(1)}, f32[256]{0:T(256)}, u32[]{:S(2)}) copy-start(f32[256]{0:T(256)} %param.19) | copy-start | bytes 3076
  158.9 20.9 %copy-start.2 = (bf16[256,256]{1,0:T(8,128)(2,1)S(1)}, bf16[256,256]{1,0:T(8,128)(2,1)}, u32[]{:S(2)}) copy-start(bf16[256,256]{1,0:T(8,128)(2,1)} %param.20) | copy-start | bytes 393220
  158.9 20.9 %copy-start.9 = (f32[256]{0:T(256)S(1)}, f32[256]{0:T(256)}, u32[]{:S(2)}) copy-start(f32[256]{0:T(256)} %param.21) | copy-start | bytes 3076
  179.8 13.9 %copy-start.6 = (bf16[4,256]{1,0:T(4,128)(2,1)S(1)}, bf16[4,256]{1,0:T(4,128)(2,1)}, u32[]{:S(2)}) copy-start(bf16[4,256]{1,0:T(4,128)(2,1)} %param.22) | copy-start | bytes 6148
  179.8 13.9 %copy-start.10 = (f32[4]{0:T(128)S(1)}, f32[4]{0:T(128)}, u32[]{:S(2)}) copy-start(f32[4]{0:T(128)} %param.23) | copy-start | bytes 52
  193.6 8.6 %copy-start.4 = (s32[512]{0:T(512)S(1)}, s32[512]{0:T(512)}, u32[]{:S(2)}) copy-start(s32[512]{0:T(512)} %param.16) | copy-start | bytes 6148
  193.6 9.2 %copy-start.7 = (f32[3,512]{1,0:T(4,128)S(1)}, f32[3,512]{1,0:T(4,128)}, u32[]{:S(2)}) copy-start(f32[3,512]{1,0:T(4,128)} %param.17) | copy-start | bytes 18436
  202.8 25.9 %copy-start.5 = (f32[512,3]{0,1:T(4,128)}, f32[512,3]{0,1:T(4,128)S(1)}, u32[]{:S(2)}) copy-start(f32[512,3]{0,1:T(4,128)S(1)} %multiply_reduce_fusion.1) | copy-start | bytes 18436
  277.2 325.9 %all-to-all-start.2 = ((f32[128,2,512,32]{2,3,1,0:T(8,128)}), f32[128,2,512,32]{2,3,1,0:T(8,128)}, u32[]{:S(2)}, u32[]{:S(2)}) async-start(f32[128,2,512,32]{2,3,1,0:T(8,128)} %bitcast.79), calls=%async_computation.2 | async-start | bytes 33554432 | tf_op jit(solution)/shard_map/all_to_all | solution.py:118
  294.9 306.5 %all-reduce.5.cloned.1.call-start = ((), (), s32[]{:S(2)}) async-start(), calls=%async_computation.3 | async-start | bytes 524288 | tf_op jit(solution)/shard_map/psum | solution.py:125
  605.6 50.5 %copy-start.1 = (bf16[64,512,32]{1,2,0:T(8,128)(2,1)S(1)}, bf16[64,512,32]{1,2,0:T(8,128)(2,1)}, u32[]{:S(2)}) copy-start(bf16[64,512,32]{1,2,0:T(8,128)(2,1)} %param.12) | copy-start | bytes 6291460
Sparse Core Ops, SparseCore 0:
  306.8 283.9 all-reduce.4
where the time goes:
time: 665 us; the launch traced here: 663 us
  blocking collectives  302 us (45%)
  matrix products  107 us (16%)
  waiting for transfers between devices  98.4 us (15%)
  other arithmetic  65.5 us (10%)
  local copies, waits for them, and re-layouts  52.3 us (8%)
  starting transfers between devices  23.5 us (4%)
  between operations  14.3 us (2%)
    psum x1, blocking collectives, body(): lax.psum((param_sums[0], param_sums[1], param_sums[2], param_sums[3], par...  281 us
    all_to_all x1, waiting for transfers between devices, body(): lax.all_to_all(filled, ('view', 'space'), split_axis=0, concat_axis=0, ti...  98.4 us
    scatter-add x1, other arithmetic, body(): jnp.zeros((own_bricks, VOX, FEAT), jnp.float32).at[target_rows]  50.5 us
    dot_general x3, matrix products, contract_cols(): lax.dot_general(left, right, (((1,), (1,)), ((), ())), preferred_element_...  28.6 us
    scatter x1, local copies, waits for them, and re-layouts, body(): jnp.zeros((dev_count * capacity, VOX, FEAT), jnp.float32).at[slots]  23.3 us
    dot_general x3, matrix products, contract_rows(): lax.dot_general(left, right, (((0,), (0,)), ((), ())), preferred_element_...  23.1 us
    all_to_all x1, blocking collectives, body(): lax.all_to_all(requested, ('view', 'space'), split_axis=0, concat_axis=0,...  21.1 us
    all_to_all x1, starting transfers between devices, body(): lax.all_to_all(outgoing, ('view', 'space'), split_axis=0, concat_axis=0,...  17.8 us
  transfers between devices with their start and end apart: 3, of which 1 were waited for; matrix products, arithmetic and copies ran while one was open for 4% of the time, Pallas kernels for 0%

commit v1 on v0

v1 whole, which is shorter than its diff:
```python
import functools

import jax
import jax.numpy as jnp
from jax import lax
from jax.experimental import pallas as pl
from jax.experimental.pallas import tpu as pltpu
from jax.sharding import PartitionSpec as P

FEAT = 32
VOX = 512
WIDTH = 256
BLOCK = 128
RAY_LEN = 32
GROUP = 8
GRAD_ROWS = 1024

AXES = ("view", "space")
step_len = 0.05
F32 = jnp.float32
BF16 = jnp.bfloat16


def dot_nn(left, right, precision=None):
    return lax.dot_general(
        left, right, (((1,), (0,)), ((), ())), precision=precision, preferred_element_type=F32
    )


def dot_nt(left, right, precision=None):
    return lax.dot_general(
        left, right, (((1,), (1,)), ((), ())), precision=precision, preferred_element_type=F32
    )


def lane_sums(values, matrix):
    return dot_nn(values, matrix, precision=lax.Precision.HIGHEST)


def render_grad(raw, live, goal, before, within, after):
    rows = live.shape[0]
    small = jnp.exp(-jnp.abs(raw[0]))
    sigma = jnp.maximum(raw[0], 0.0) + jnp.log1p(small)
    slope = jnp.where(raw[0] >= 0.0, 1.0, small) / (1.0 + small)
    shades = [jax.nn.sigmoid(channel) for channel in raw[1:]]
    depth = step_len * sigma * live
    faded = jnp.exp(-depth)
    trans = jnp.exp(depth - lane_sums(depth, before))
    weight = trans * (1.0 - faded)
    stacked = jnp.concatenate([weight * shade for shade in shades], axis=0)
    color = lane_sums(stacked, within)
    colors = [color[c * rows : (c + 1) * rows] for c in range(3)]
    miss = [colors[c] - goal[c] for c in range(3)]
    d_weight = miss[0] * shades[0] + miss[1] * shades[1] + miss[2] * shades[2]
    d_depth = d_weight * (trans * faded) - lane_sums(d_weight * weight, after)
    d_raw = [step_len * live * d_depth * slope]
    for c in range(3):
        d_raw.append(weight * miss[c] * shades[c] * (1.0 - shades[c]))
    return colors, d_raw


def lane_matrices():
    row = lax.broadcasted_iota(jnp.int32, (BLOCK, BLOCK), 0)
    col = lax.broadcasted_iota(jnp.int32, (BLOCK, BLOCK), 1)
    same = (row // RAY_LEN) == (col // RAY_LEN)
    before = (same & (row <= col)).astype(F32)
    after = (same & (row > col)).astype(F32)
    return before, same.astype(F32), after


def step_kernel(
    first,
    count_ref,
    block_ref,
    slot_ref,
    weights_hbm,
    bricks_hbm,
    samples_ref,
    goal_ref,
    w_in_ref,
    w_in_t_ref,
    b_in_ref,
    w_hid_ref,
    w_hid_t_ref,
    b_hid_ref,
    w_out_ref,
    w_out_t_ref,
    b_out_ref,
    lanes_ref,
    carried_ref,
    _,
    grads_hbm,
    color_ref,
    sums_ref,
    weights_buf,
    bricks_buf,
    grads_buf,
    raw_buf,
    d_raw_buf,
    live_buf,
    goal_buf,
    acc_hid,
    acc_in,
    acc_out,
    acc_b_hid,
    acc_b_in,
    acc_b_out,
    weights_sem,
    bricks_sem,
    grads_sem,
):
    total = count_ref[0]
    steps = (total + GROUP - 1) // GROUP
    width = GROUP * BLOCK

    def fetch(step, side):
        for k in range(GROUP):
            at = step * GROUP + k
            pltpu.make_async_copy(
                weights_hbm.at[block_ref[at]], weights_buf.at[side, k], weights_sem.at[side, k]
            ).start()
            pltpu.make_async_copy(
                bricks_hbm.at[slot_ref[at]], bricks_buf.at[side, k], bricks_sem.at[side, k]
            ).start()

    def arrive(side):
        for k in range(GROUP):
            pltpu.make_async_copy(
                weights_hbm.at[0], weights_buf.at[side, k], weights_sem.at[side, k]
            ).wait()
            pltpu.make_async_copy(
                bricks_hbm.at[0], bricks_buf.at[side, k], bricks_sem.at[side, k]
            ).wait()

    def send(step, side):
        for k in range(GROUP):
            at = step * GROUP + k

            @pl.when(at < total)
            def _():
                pltpu.make_async_copy(
                    grads_buf.at[side, k],
                    grads_hbm.at[slot_ref[at], 0 if first else 1],
                    grads_sem.at[side, k],
                ).start()

    def settle(step, side):
        for k in range(GROUP):
            at = step * GROUP + k

            @pl.when((step >= 0) & (at < total))
            def _():
                pltpu.make_async_copy(
                    grads_buf.at[side, k], grads_hbm.at[0, 0], grads_sem.at[side, k]
                ).wait()

    @pl.when(steps > 0)
    def _():
        fetch(0, 0)

    for ref in (acc_hid, acc_in, acc_out, acc_b_hid, acc_b_in, acc_b_out, color_ref):
        ref[...] = jnp.zeros_like(ref)

    def one_step(step, state):
        side = step % 2
        arrive(side)

        @pl.when(step + 1 < steps)
        def _():
            fetch(step + 1, 1 - side)

        for k in range(GROUP):
            at = step * GROUP + k
            block = block_ref[at]
            used = jnp.where(at < total, samples_ref[pl.ds(block, 1), :], 0)
            live_buf[pl.ds(k, 1), :] = used
            for c in range(3):
                goal_buf[c, pl.ds(k, 1), :] = goal_ref[c, pl.ds(block, 1), :]
        place = lax.broadcasted_iota(jnp.int32, (GROUP, BLOCK), 1) % RAY_LEN
        live = (place < live_buf[...]).astype(F32)

        feats = jnp.concatenate(
            [dot_nt(bricks_buf[side, k], weights_buf[side, k]) for k in range(GROUP)], axis=1
        ).astype(BF16)
        pre_one = dot_nn(w_in_t_ref[...], feats) + b_in_ref[...]
        act_one = jnp.maximum(pre_one, 0.0).astype(BF16)
        pre_two = dot_nn(w_hid_t_ref[...], act_one) + b_hid_ref[...]
        act_two = jnp.maximum(pre_two, 0.0).astype(BF16)
        raw = dot_nn(w_out_ref[...], act_two) + b_out_ref[...]
        for k in range(GROUP):
            for c in range(4):
                raw_buf[c, k : k + 1, :] = raw[c : c + 1, k * BLOCK : (k + 1) * BLOCK]
        colors, d_raw = render_grad(
            [raw_buf[c] for c in range(4)],
            live,
            [goal_buf[c] for c in range(3)],
            lanes_ref[0],
            lanes_ref[1],
            lanes_ref[2],
        )
        for k in range(GROUP):
            at = step * GROUP + k
            row = jnp.where(at < total, block_ref[at], BLOCK)
            for c in range(3):
                color_ref[c, pl.ds(row, 1), :] = colors[c][k : k + 1]
            for c in range(4):
                d_raw_buf[c : c + 1, k * BLOCK : (k + 1) * BLOCK] = d_raw[c][k : k + 1]
        for c in range(4):
            acc_b_out[c] += d_raw[c]
        d_raw_b = d_raw_buf[...].astype(BF16)
        acc_out[...] += dot_nt(d_raw_b, act_two)
        d_two = jnp.where(pre_two > 0.0, dot_nn(w_out_t_ref[...], d_raw_b), 0.0)
        d_two_b = d_two.astype(BF16)
        acc_hid[...] += dot_nt(act_one, d_two_b)
        d_one = jnp.where(pre_one > 0.0, dot_nn(w_hid_ref[...], d_two_b), 0.0)
        d_one_b = d_one.astype(BF16)
        acc_in[...] += dot_nt(feats, d_one_b)
        b_two = acc_b_hid[...]
        b_one = acc_b_in[...]
        for k in range(GROUP):
            b_two += d_two[:, k * BLOCK : (k + 1) * BLOCK]
            b_one += d_one[:, k * BLOCK : (k + 1) * BLOCK]
        acc_b_hid[...] = b_two
        acc_b_in[...] = b_one
        d_feats = dot_nn(w_in_ref[...], d_one_b).astype(BF16)
        settle(step - 2, side)
        for k in range(GROUP):
            grads_buf[side, k] = dot_nn(
                d_feats[:, k * BLOCK : (k + 1) * BLOCK], weights_buf[side, k]
            ).astype(BF16)
        send(step, side)
        return state

    lax.fori_loop(0, steps, one_step, 0)

    settle(steps - 2, steps % 2)
    settle(steps - 1, (steps + 1) % 2)

    ones = jnp.ones((8, BLOCK), F32)

    def over_lanes(values):
        return dot_nt(ones, values, precision=lax.Precision.HIGHEST)

    half = WIDTH // 2
    sums_ref[0:256, :] = acc_hid[:, :half]
    sums_ref[256:512, :] = acc_hid[:, half:]
    sums_ref[512:544, :] = acc_in[:, :half]
    sums_ref[544:576, :] = acc_in[:, half:]
    sums_ref[576:584, :] = acc_out[:, :half]
    sums_ref[584:592, :] = acc_out[:, half:]
    b_hid_row = over_lanes(acc_b_hid[...])
    b_in_row = over_lanes(acc_b_in[...])
    sums_ref[592:600, :] = b_hid_row[:, :half]
    sums_ref[600:608, :] = b_hid_row[:, half:]
    sums_ref[608:616, :] = b_in_row[:, :half]
    sums_ref[616:624, :] = b_in_row[:, half:]
    sums_ref[624:632, :] = jnp.zeros((8, BLOCK), F32)
    for c in range(4):
        sums_ref[624 + c : 625 + c, :] = jnp.sum(acc_b_out[c], axis=0, keepdims=True)
    sums_ref[632:GRAD_ROWS, :] = jnp.zeros((GRAD_ROWS - 632, BLOCK), F32)
    if not first:
        sums_ref[...] += carried_ref[...]


def run_blocks(first, total, blocks, slots, weights, bricks, samples, goal, params, carried, grads):
    vmem = pl.BlockSpec(memory_space=pltpu.VMEM)
    smem = pl.BlockSpec(memory_space=pltpu.SMEM)
    hbm = pl.BlockSpec(memory_space=pltpu.MemorySpace.HBM)
    amount = blocks.shape[0] if first else blocks.shape[0] // 8
    cost = pl.CostEstimate(
        flops=amount * 70_000_000, bytes_accessed=amount * 200_000, transcendentals=amount * 1000
    )
    return pl.pallas_call(
        functools.partial(step_kernel, first),
        out_shape=(
            jax.ShapeDtypeStruct((bricks.shape[0], 2, FEAT, VOX), BF16),
            jax.ShapeDtypeStruct((3, BLOCK + 8, BLOCK), F32),
            jax.ShapeDtypeStruct((GRAD_ROWS, BLOCK), F32),
        ),
        in_specs=[smem, smem, smem, hbm, hbm] + [vmem] * 13 + [hbm],
        out_specs=(hbm, vmem, vmem),
        scratch_shapes=[
            pltpu.VMEM((2, GROUP, BLOCK, VOX), BF16),
            pltpu.VMEM((2, GROUP, FEAT, VOX), BF16),
            pltpu.VMEM((2, GROUP, FEAT, VOX), BF16),
            pltpu.VMEM((4, GROUP, BLOCK), F32),
            pltpu.VMEM((8, GROUP * BLOCK), F32),
            pltpu.VMEM((GROUP, BLOCK), jnp.int32),
            pltpu.VMEM((3, GROUP, BLOCK), F32),
            pltpu.VMEM((WIDTH, WIDTH), F32),
            pltpu.VMEM((FEAT, WIDTH), F32),
            pltpu.VMEM((8, WIDTH), F32),
            pltpu.VMEM((WIDTH, BLOCK), F32),
            pltpu.VMEM((WIDTH, BLOCK), F32),
            pltpu.VMEM((4, GROUP, BLOCK), F32),
            pltpu.SemaphoreType.DMA((2, GROUP)),
            pltpu.SemaphoreType.DMA((2, GROUP)),
            pltpu.SemaphoreType.DMA((2, GROUP)),
        ],
        compiler_params=pltpu.CompilerParams(vmem_limit_bytes=60 << 20),
        input_output_aliases={} if first else {18: 0},
        cost_estimate=cost,
        name="blocks_first" if first else "blocks_second",
    )(total, blocks, slots, weights, bricks, samples, goal, *params, carried, grads)


TAKE = 8


def collect_kernel(ids_ref, grads_ref, out_ref):
    step = pl.program_id(0)

    @pl.when(step == 0)
    def _():
        out_ref[...] = jnp.zeros_like(out_ref)

    for k in range(TAKE):
        for r in range(2):
            brick = ids_ref[2 * (step * TAKE + k) + r]

            @pl.when(brick >= 0)
            def _():
                out_ref[brick] += grads_ref[k, r].astype(F32)


def collect(ids, grads, own):
    amount = grads.shape[0]
    return pl.pallas_call(
        collect_kernel,
        out_shape=jax.ShapeDtypeStruct((own, FEAT, VOX), F32),
        grid_spec=pltpu.PrefetchScalarGridSpec(
            num_scalar_prefetch=1,
            grid=(amount // TAKE,),
            in_specs=[pl.BlockSpec((TAKE, 2, FEAT, VOX), lambda i, ids: (i, 0, 0, 0))],
            out_specs=pl.BlockSpec((own, FEAT, VOX), lambda i, ids: (0, 0, 0)),
        ),
        compiler_params=pltpu.CompilerParams(vmem_limit_bytes=60 << 20),
        cost_estimate=pl.CostEstimate(
            flops=amount * FEAT * VOX, bytes_accessed=amount * FEAT * VOX * 2, transcendentals=0
        ),
        name="collect",
    )(ids, grads)


def exchange(values):
    return lax.all_to_all(values, AXES, split_axis=0, concat_axis=0, tiled=True)


def scatter_sum(parts, axis):
    size = parts.shape[0]
    me = lax.axis_index(axis)
    pieces = [lax.dynamic_index_in_dim(parts, me, keepdims=False)]
    for shift in range(1, size):
        piece = lax.dynamic_index_in_dim(parts, (me + shift) % size, keepdims=False)
        pieces.append(lax.ppermute(piece, axis, [(i, (i + shift) % size) for i in range(size)]))
    return functools.reduce(jnp.add, pieces)


def gather_all(part, axis, size):
    me = lax.axis_index(axis)
    pieces = [part]
    for shift in range(1, size):
        pieces.append(lax.ppermute(part, axis, [((i + shift) % size, i) for i in range(size)]))
    twice = jnp.concatenate(pieces + pieces)
    rows = part.shape[0]
    return lax.dynamic_slice_in_dim(twice, (size - me) % size * rows, size * rows)


def sum_over_devices(sums):
    space, view = lax.axis_size("space"), lax.axis_size("view")
    part = scatter_sum(sums.reshape(space, GRAD_ROWS // space, BLOCK), "space")
    part = scatter_sum(part.reshape(view, GRAD_ROWS // (space * view), BLOCK), "view")
    return gather_all(gather_all(part, "view", view), "space", space)


def network_params(w_in, b_in, w_hid, b_hid, w_out, b_out):
    w_out_rows = jnp.pad(w_out, ((0, 4), (0, 0)))
    return (
        w_in,
        w_in.T,
        b_in[:, None],
        w_hid,
        w_hid.T,
        b_hid[:, None],
        w_out_rows,
        w_out_rows.T,
        jnp.pad(b_out, (0, 4))[:, None],
        jnp.stack(lane_matrices()),
    )


def body(
    brick_feats,
    interp_weights,
    block_owner,
    block_brick,
    sample_count,
    target,
    w_in,
    b_in,
    w_hid,
    b_hid,
    w_out,
    b_out,
):
    own_blocks = interp_weights.shape[0]
    own_bricks = brick_feats.shape[0]
    dev_count = lax.axis_size(AXES)
    owners = block_owner[:, 0]
    local_ids = block_brick[:, 0]
    row_index = lax.broadcasted_iota(jnp.int32, (own_blocks, own_blocks), 0)
    col_index = lax.broadcasted_iota(jnp.int32, (own_blocks, own_blocks), 1)
    same = owners[:, None] == owners[None, :]
    ranks = jnp.sum((same & (col_index < row_index)).astype(jnp.int32), axis=1)
    ranks_c = jnp.sum((same & (row_index < col_index)).astype(jnp.int32), axis=0)

    owner_row = row_index == owners[None, :]
    wish = [
        jnp.max(jnp.where(owner_row & (ranks_c == r)[None, :], local_ids[None, :], -1), axis=1)
        for r in range(2)
    ]
    asked = exchange(jnp.stack(wish, axis=1).reshape(dev_count, 1, 2)).reshape(dev_count, 2)

    lists = []
    for r in range(2):
        mine = ranks == r
        place = jnp.sum(((col_index < row_index) & (ranks_c == r)[None, :]).astype(jnp.int32), axis=1)
        total = jnp.sum(mine.astype(jnp.int32))
        hit = (place[:, None] == col_index) & mine[:, None]
        blocks = jnp.sum(jnp.where(hit, row_index, 0), axis=0)
        slots = jnp.sum(jnp.where(hit, owners[:, None], 0), axis=0)
        last = jnp.max(jnp.where(mine, row_index[:, 0], 0))
        last_slot = jnp.sum(jnp.where(mine & (row_index[:, 0] == last), owners, 0))
        empty = col_index[0] >= total
        blocks = jnp.where(empty, last, blocks)
        slots = jnp.where(empty, last_slot, slots)
        lists.append((total[None], blocks, slots))

    bricks_t = jnp.swapaxes(brick_feats, 1, 2)
    fetched = [exchange(bricks_t[jnp.maximum(asked[:, r], 0)]) for r in range(2)]

    samples = jnp.repeat(sample_count, RAY_LEN).reshape(own_blocks, BLOCK)
    goal = jnp.repeat(target, RAY_LEN, axis=1).reshape(3, own_blocks, BLOCK)
    params = network_params(w_in, b_in, w_hid, b_hid, w_out, b_out)
    nothing = jnp.zeros((8, BLOCK), F32)
    grads, color_0, sums = run_blocks(
        True, *lists[0], interp_weights, fetched[0], samples, goal, params, nothing, nothing
    )
    grads, color_1, sums = run_blocks(
        False, *lists[1], interp_weights, fetched[1], samples, goal, params, sums, grads
    )
    brick_grad = collect(asked.reshape(-1), exchange(grads), own_bricks)
    brick_grad = jnp.swapaxes(brick_grad, 1, 2)

    totals = sum_over_devices(sums) / (sample_count.shape[0] * dev_count)
    half = WIDTH // 2

    def joined(start, rows):
        return jnp.concatenate([totals[start : start + rows], totals[start + rows : start + 2 * rows]], axis=1)

    g_w_hid = joined(0, WIDTH)
    g_w_in = joined(2 * WIDTH, FEAT)
    g_w_out = joined(576, 8)[:4]
    g_b_hid = joined(592, 8)[0]
    g_b_in = joined(608, 8)[0]
    g_b_out = jnp.sum(totals[624:628], axis=1)
    color = (color_0 + color_1)[:, :own_blocks, ::RAY_LEN].reshape(3, -1)
    return (brick_grad, color, g_w_in, g_b_in, g_w_hid, g_b_hid, g_w_out, g_b_out)


def solution(mesh):
    shared = P(AXES, None, None)
    return jax.shard_map(
        body,
        mesh=mesh,
        in_specs=(
            shared,
            shared,
            P(AXES, None),
            P(AXES, None),
            P(AXES),
            P(None, AXES),
            P(),
            P(),
            P(),
            P(),
            P(),
            P(),
        ),
        out_specs=(shared, P(None, AXES), P(), P(), P(), P(), P(), P()),
        check_vma=False,
    )
```

time: 665 us -> 402 us (0.60)
  blocking collectives: 302 us -> 21.1 us
  matrix products: 107 us -> 0 us
  starting transfers between devices: 23.5 us -> 97 us
  Pallas kernels: 0 us -> 73.1 us
  waiting for transfers between devices: 98.4 us -> 149 us
  other arithmetic: 65.5 us -> 19.5 us
  local copies, waits for them, and re-layouts: 52.3 us -> 36.7 us
  between operations: 14.3 us -> 1.28 us
    psum x1 -> x0, blocking collectives: 281 us -> none  [body(): lax.psum((param_sums[0], param_sums[1], param_sums[2], param_sums[3], par...]
    dot_general x11 -> x0, matrix products: 107 us -> none  [the longest x3 28.6 us: contract_cols(): lax.dot_general(left, right, (((1,), (1,)), ((), ())), preferred_element_...]
    ppermute x0 -> x44, waiting for transfers between devices: none -> 100 us  [the longest x22 94.8 us: scatter_sum(): lax.ppermute(piece, axis, [(i, (i + shift) % size) for i in range(size)])]
    ppermute x0 -> x44, starting transfers between devices: none -> 75.9 us  [the longest x22 48.6 us: scatter_sum(): lax.ppermute(piece, axis, [(i, (i + shift) % size) for i in range(size)])]
    pallas_call x0 -> x3, Pallas kernels: none -> 73.1 us  [the longest x2 60.1 us: run_blocks(): pl.pallas_call(functools.partial(step_kernel, first), out_shape=(jax.Shap...]
    scatter-add x1 -> x0, other arithmetic: 50.5 us -> none  [body(): jnp.zeros((own_bricks, VOX, FEAT), jnp.float32).at[target_rows]]
    all_to_all x2 -> x3, waiting for transfers between devices: 98.4 us -> 48.4 us  [exchange(): return lax.all_to_all(values, AXES, split_axis=0, concat_axis=0, tiled=True)]
    scatter x2 -> x0, local copies, waits for them, and re-layouts: 24.4 us -> none  [the longest x1 23.3 us: body(): jnp.zeros((dev_count * capacity, VOX, FEAT), jnp.float32).at[slots]]
  transfers between devices with their start and end apart: 3 -> 47, of which waited for: 1 -> 11; matrix products, arithmetic and copies ran while one was open for 4% -> 13% of each run, Pallas kernels for 0% -> 12%
where the time goes in v1:
time: 402 us; the launch traced here: 397 us
  waiting for transfers between devices  149 us (37%)
  starting transfers between devices  97 us (24%)
  Pallas kernels  73.1 us (18%)
  local copies, waits for them, and re-layouts  36.7 us (9%)
  blocking collectives  21.1 us (5%)
  other arithmetic  19.5 us (5%)
    ppermute x22, waiting for transfers between devices, scatter_sum(): lax.ppermute(piece, axis, [(i, (i + shift) % size) for i in range(size)])  94.8 us
    pallas_call x2, Pallas kernels, run_blocks(): pl.pallas_call(functools.partial(step_kernel, first), out_shape=(jax.Shap...  60.1 us
    ppermute x22, starting transfers between devices, scatter_sum(): lax.ppermute(piece, axis, [(i, (i + shift) % size) for i in range(size)])  48.6 us
    all_to_all x3, waiting for transfers between devices, exchange(): return lax.all_to_all(values, AXES, split_axis=0, concat_axis=0, tiled=True)  48.4 us
    ppermute x22, starting transfers between devices, gather_all(): lax.ppermute(part, axis, [((i + shift) % size, i) for i in range(size)])  27.3 us
    unnamed x79, local copies, waits for them, and re-layouts  21.6 us
    all_to_all x1, blocking collectives, exchange(): return lax.all_to_all(values, AXES, split_axis=0, concat_axis=0, tiled=True)  21.1 us
    all_to_all x3, starting transfers between devices, exchange(): return lax.all_to_all(values, AXES, split_axis=0, concat_axis=0, tiled=True)  21.1 us
  transfers between devices with their start and end apart: 47, of which 11 were waited for; matrix products, arithmetic and copies ran while one was open for 13% of the time, Pallas kernels for 12%

profile of v1, /device:TPU:1, one launch (start us, length us, event | category | flops | bytes accessed | tf_op | source)
XLA Modules:
  0.0 397.2 jit_solution(8155330540458009694)
XLA Ops:
  1.6 0.9 select_reduce_fusion.5
  2.6 21.1 %all_to_all.20 = s32[128,1,2]{2,1,0:T(1,128)S(1)} all-to-all(s32[128,1,2]{2,1,0:T(1,128)S(1)} %copy.73), channel_id=1, replica_groups=mesh['view'=8,'space'=16] {'view','space'}, dimensions={0} | all-to-all | bytes 2048 | tf_op jit(solution)/shard_map/all_to_all | solution.py:346
  23.9 2.7 gather_fusion.1
  26.7 5.3 %all-to-all-start.2 = ((bf16[128,32,512]{2,1,0:T(8,128)(2,1)}), bf16[128,32,512]{2,1,0:T(8,128)(2,1)}, u32[]{:S(2)}, u32[]{:S(2)}) async-start(bf16[128,32,512]{2,1,0:T(8,128)(2,1)} %gather_fusion.1), calls=%async_computation.2 | async-start | bytes 8388608 | tf_op jit(solution)/shard_map/all_to_all | solution.py:346
  32.0 2.8 gather_fusion
  34.9 48.4 %all-to-all-done.2.bricks_hbm = bf16[128,32,512]{2,1,0:T(8,128)(2,1)} async-done(((bf16[128,32,512]{2,1,0:T(8,128)(2,1)}), bf16[128,32,512]{2,1,0:T(8,128)(2,1)}, u32[]{:S(2)}, u32[]{:S(2)}) %all-to-all-start.2) | async-done | bytes 4194336 | tf_op jit(solution)/shard_map/all_to_all | solution.py:346
  83.3 5.5 %all-to-all-start.1 = ((bf16[128,32,512]{2,1,0:T(8,128)(2,1)}), bf16[128,32,512]{2,1,0:T(8,128)(2,1)}, u32[]{:S(2)}, u32[]{:S(2)}) async-start(bf16[128,32,512]{2,1,0:T(8,128)(2,1)} %gather_fusion), calls=%async_computation.1 | async-start | bytes 8388608 | tf_op jit(solution)/shard_map/all_to_all | solution.py:346
  96.2 2.0 fusion.41
  99.9 1.7 compare_select_fusion.3.block_ref
  101.7 1.8 compare_select_fusion.2.slot_ref
  103.4 1.9 compare_select_fusion.1.block_ref
  105.4 1.8 compare_select_fusion.slot_ref
  107.8 48.7 %blocks_first.1 = (bf16[128,2,32,512]{3,2,1,0:T(8,128)(2,1)}, f32[3,136,128]{2,1,0:T(8,128)}, f32[1024,128]{1,0:T(8,128)}) custom-call(s32[1]{0:T(128)} %bitcast.15.count_ref, s32[128]{0:T(128)} %compare_select_fusion.1.block_ref, s32[128]{0:T(128)} %compare_select_fusion.slot_ref, bf16[128,128,512]{2,1,0:T(8,128)(2,1)} %weights_hbm.3, ...), custom_call_target="tpu_custom_call" | custom-call | flops 8960000000 | bytes 25600000 | tf_op jit(solution)/shard_map/blocks_first/pallas_call | solution.py:273
  156.5 11.4 %blocks_second.1 = (bf16[128,2,32,512]{3,2,1,0:T(8,128)(2,1)}, f32[3,136,128]{2,1,0:T(8,128)}, f32[1024,128]{1,0:T(8,128)}) custom-call(s32[1]{0:T(128)} %bitcast.5.count_ref, s32[128]{0:T(128)} %compare_select_fusion.3.block_ref, s32[128]{0:T(128)} %compare_select_fusion.2.slot_ref, ...), custom_call_target="tpu_custom_call", output_to_operand_aliasing={{0}: (18, {})} | custom-call | flops 1120000000 | bytes 3200000 | tf_op jit(solution)/shard_map/blocks_second/pallas_call | solution.py:273
  167.9 10.2 %all-to-all-start.3 = ((bf16[128,2,32,512]{3,2,1,0:T(8,128)(2,1)}), bf16[128,2,32,512]{3,2,1,0:T(8,128)(2,1)}, u32[]{:S(2)}, u32[]{:S(2)}) async-start(bf16[128,2,32,512]{3,2,1,0:T(8,128)(2,1)} %get-tuple-element.16), calls=%async_computation.3 | async-start | bytes 16777216 | tf_op jit(solution)/shard_map/all_to_all | solution.py:346
  178.4 5.5 %collective-permute-start.14 = (f32[64,128]{1,0:T(8,128)S(1)}, f32[64,128]{1,0:T(8,128)S(1)}, u32[]{:S(2)}, u32[]{:S(2)}) collective-permute-start(f32[64,128]{1,0:T(8,128)S(1)} %get-tuple-element.54), channel_id=1, source_target_pairs={{0,15},{1,0},{2,1},{3,2},{4,3},{5,4},{6,5},{7,6},{8,7},{9,8},{10,9... | collective-permute-start | bytes 98312 | tf_op jit(solution)/shard_map/ppermute | solution.py:355
  185.1 1.9 collective-permute-start.10
  187.0 85.9 %collective-permute-done.14 = f32[64,128]{1,0:T(8,128)S(1)} collective-permute-done((f32[64,128]{1,0:T(8,128)S(1)}, f32[64,128]{1,0:T(8,128)S(1)}, u32[]{:S(2)}, u32[]{:S(2)}) %collective-permute-start.14) | collective-permute-done | bytes 32800 | tf_op jit(solution)/shard_map/ppermute | solution.py:355
  272.9 8.3 %collective-permute-start.9 = (f32[64,128]{1,0:T(8,128)S(1)}, f32[64,128]{1,0:T(8,128)S(1)}, u32[]{:S(2)}, u32[]{:S(2)}) collective-permute-start(f32[64,128]{1,0:T(8,128)S(1)} %get-tuple-element.59), channel_id=1, source_target_pairs={{0,10},{1,11},{2,12},{3,13},{4,14},{5,15},{6,0},{7,1},{8,2},{9,3},... | collective-permute-start | bytes 98312 | tf_op jit(solution)/shard_map/ppermute | solution.py:355
  281.7 1.1 collective-permute-start.7
  282.8 2.0 collective-permute-start.6
  284.9 1.1 collective-permute-done.8
  286.1 2.3 collective-permute-start.3
  288.4 2.5 collective-permute-start.2
  293.1 1.5 collective-permute-done.2
  294.6 2.9 collective-permute-done.1
  299.3 4.9 %collective-permute-start.21 = (f32[8,128]{1,0:T(8,128)S(1)}, f32[8,128]{1,0:T(8,128)S(1)}, u32[]{:S(2)}, u32[]{:S(2)}) collective-permute-start(f32[8,128]{1,0:T(8,128)S(1)} %get-tuple-element.69), channel_id=1, source_target_pairs={{0,112},{16,0},{32,16},{48,32},{64,48},{80,64},{96,80},{112,96},{1... | collective-permute-start | bytes 12296 | tf_op jit(solution)/shard_map/ppermute | solution.py:355
  304.3 11.1 %collective-permute-start.20 = (f32[8,128]{1,0:T(8,128)S(1)}, f32[8,128]{1,0:T(8,128)S(1)}, u32[]{:S(2)}, u32[]{:S(2)}) collective-permute-start(f32[8,128]{1,0:T(8,128)S(1)} %get-tuple-element.70), channel_id=1, source_target_pairs={{0,96},{16,112},{32,0},{48,16},{64,32},{80,48},{96,64},{112,80},{1... | collective-permute-start | bytes 12296 | tf_op jit(solution)/shard_map/ppermute | solution.py:355
  316.1 3.5 collective-permute-start.17
  319.6 1.3 collective-permute-start.15
  320.9 2.5 collective-permute-done.16
  324.1 1.0 collective-permute-start.23
  325.7 1.9 collective-permute-start.25
  327.6 1.9 collective-permute-start.26
  329.5 1.1 collective-permute-start.28
  330.6 1.2 collective-permute-done.26
  331.8 1.3 collective-permute-done.27
  337.2 1.4 collective-permute-start.30
  338.7 2.8 collective-permute-start.33
  341.4 3.5 collective-permute-start.34
  346.9 2.6 collective-permute-start.36
  351.0 2.6 collective-permute-start.38
  354.3 1.4 collective-permute-start.39
  356.3 1.2 collective-permute-start.40
  358.2 3.0 collective-permute-start.41
  365.5 2.7 collective-permute-done.42
  379.4 1.1 dynamic-slice_multiply_fusion
  384.2 13.0 %collect.1 = f32[64,32,512]{2,1,0:T(8,128)} custom-call(s32[256]{0:T(256)} %reshape_reshape.7.ids_ref, bf16[128,2,32,512]{3,2,1,0:T(8,128)(2,1)} %all-to-all-done.3.grads_ref), custom_call_target="tpu_custom_call" | custom-call | flops 2097152 | bytes 4194304 | tf_op jit(solution)/shard_map/collect/pallas_call | solution.py:328
  (185 shorter events, 47.3 us)
Async XLA Ops:
  26.7 56.6 %all-to-all-start.2 = ((bf16[128,32,512]{2,1,0:T(8,128)(2,1)}), bf16[128,32,512]{2,1,0:T(8,128)(2,1)}, u32[]{:S(2)}, u32[]{:S(2)}) async-start(bf16[128,32,512]{2,1,0:T(8,128)(2,1)} %gather_fusion.1), calls=%async_computation.2 | async-start | bytes 8388608 | tf_op jit(solution)/shard_map/all_to_all | solution.py:346
  83.3 73.1 %all-to-all-start.1 = ((bf16[128,32,512]{2,1,0:T(8,128)(2,1)}), bf16[128,32,512]{2,1,0:T(8,128)(2,1)}, u32[]{:S(2)}, u32[]{:S(2)}) async-start(bf16[128,32,512]{2,1,0:T(8,128)(2,1)} %gather_fusion), calls=%async_computation.1 | async-start | bytes 8388608 | tf_op jit(solution)/shard_map/all_to_all | solution.py:346
  167.9 168.0 %copy-start.3 = (f32[3,136,128]{2,1,0:T(8,128)S(1)}, f32[3,136,128]{2,1,0:T(8,128)}, u32[]{:S(2)}) copy-start(f32[3,136,128]{2,1,0:T(8,128)} %get-tuple-element.17) | copy-start | bytes 626692
  167.9 216.3 %all-to-all-start.3 = ((bf16[128,2,32,512]{3,2,1,0:T(8,128)(2,1)}), bf16[128,2,32,512]{3,2,1,0:T(8,128)(2,1)}, u32[]{:S(2)}, u32[]{:S(2)}) async-start(bf16[128,2,32,512]{3,2,1,0:T(8,128)(2,1)} %get-tuple-element.16), calls=%async_computation.3 | async-start | bytes 16777216 | tf_op jit(solution)/shard_map/all_to_all | solution.py:346
  178.4 94.5 %collective-permute-start.14 = (f32[64,128]{1,0:T(8,128)S(1)}, f32[64,128]{1,0:T(8,128)S(1)}, u32[]{:S(2)}, u32[]{:S(2)}) collective-permute-start(f32[64,128]{1,0:T(8,128)S(1)} %get-tuple-element.54), channel_id=1, source_target_pairs={{0,15},{1,0},{2,1},{3,2},{4,3},{5,4},{6,5},{7,6},{8,7},{9,8},{10,9... | collective-permute-start | bytes 98312 | tf_op jit(solution)/shard_map/ppermute | solution.py:355
  183.9 97.3 %collective-permute-start.13 = (f32[64,128]{1,0:T(8,128)S(1)}, f32[64,128]{1,0:T(8,128)S(1)}, u32[]{:S(2)}, u32[]{:S(2)}) collective-permute-start(f32[64,128]{1,0:T(8,128)S(1)} %get-tuple-element.55), channel_id=1, source_target_pairs={{0,14},{1,15},{2,0},{3,1},{4,2},{5,3},{6,4},{7,5},{8,6},{9,7},{10,... | collective-permute-start | bytes 98312 | tf_op jit(solution)/shard_map/ppermute | solution.py:355
  184.4 97.2 %collective-permute-start.12 = (f32[64,128]{1,0:T(8,128)S(1)}, f32[64,128]{1,0:T(8,128)S(1)}, u32[]{:S(2)}, u32[]{:S(2)}) collective-permute-start(f32[64,128]{1,0:T(8,128)S(1)} %get-tuple-element.56), channel_id=1, source_target_pairs={{0,13},{1,14},{2,15},{3,0},{4,1},{5,2},{6,3},{7,4},{8,5},{9,6},{10... | collective-permute-start | bytes 98312 | tf_op jit(solution)/shard_map/ppermute | solution.py:355
  185.1 97.8 %collective-permute-start.11 = (f32[64,128]{1,0:T(8,128)S(1)}, f32[64,128]{1,0:T(8,128)S(1)}, u32[]{:S(2)}, u32[]{:S(2)}) collective-permute-start(f32[64,128]{1,0:T(8,128)S(1)} %get-tuple-element.57), channel_id=1, source_target_pairs={{0,12},{1,13},{2,14},{3,15},{4,0},{5,1},{6,2},{7,3},{8,4},{9,5},{1... | collective-permute-start | bytes 98312 | tf_op jit(solution)/shard_map/ppermute | solution.py:355
  185.1 99.8 %collective-permute-start.10 = (f32[64,128]{1,0:T(8,128)S(1)}, f32[64,128]{1,0:T(8,128)S(1)}, u32[]{:S(2)}, u32[]{:S(2)}) collective-permute-start(f32[64,128]{1,0:T(8,128)S(1)} %get-tuple-element.58), channel_id=1, source_target_pairs={{0,11},{1,12},{2,13},{3,14},{4,15},{5,0},{6,1},{7,2},{8,3},{9,4},{... | collective-permute-start | bytes 98312 | tf_op jit(solution)/shard_map/ppermute | solution.py:355
  272.9 11.9 %collective-permute-start.9 = (f32[64,128]{1,0:T(8,128)S(1)}, f32[64,128]{1,0:T(8,128)S(1)}, u32[]{:S(2)}, u32[]{:S(2)}) collective-permute-start(f32[64,128]{1,0:T(8,128)S(1)} %get-tuple-element.59), channel_id=1, source_target_pairs={{0,10},{1,11},{2,12},{3,13},{4,14},{5,15},{6,0},{7,1},{8,2},{9,3},... | collective-permute-start | bytes 98312 | tf_op jit(solution)/shard_map/ppermute | solution.py:355
  281.2 4.9 %collective-permute-start.8 = (f32[64,128]{1,0:T(8,128)S(1)}, f32[64,128]{1,0:T(8,128)S(1)}, u32[]{:S(2)}, u32[]{:S(2)}) collective-permute-start(f32[64,128]{1,0:T(8,128)S(1)} %get-tuple-element.60), channel_id=1, source_target_pairs={{0,9},{1,10},{2,11},{3,12},{4,13},{5,14},{6,15},{7,0},{8,1},{9,2},... | collective-permute-start | bytes 98312 | tf_op jit(solution)/shard_map/ppermute | solution.py:355
  281.7 6.7 %collective-permute-start.7 = (f32[64,128]{1,0:T(8,128)S(1)}, f32[64,128]{1,0:T(8,128)S(1)}, u32[]{:S(2)}, u32[]{:S(2)}) collective-permute-start(f32[64,128]{1,0:T(8,128)S(1)} %get-tuple-element.61), channel_id=1, source_target_pairs={{0,8},{1,9},{2,10},{3,11},{4,12},{5,13},{6,14},{7,15},{8,0},{9,1},... | collective-permute-start | bytes 98312 | tf_op jit(solution)/shard_map/ppermute | solution.py:355
  282.8 8.1 %collective-permute-start.6 = (f32[64,128]{1,0:T(8,128)S(1)}, f32[64,128]{1,0:T(8,128)S(1)}, u32[]{:S(2)}, u32[]{:S(2)}) collective-permute-start(f32[64,128]{1,0:T(8,128)S(1)} %get-tuple-element.62), channel_id=1, source_target_pairs={{0,7},{1,8},{2,9},{3,10},{4,11},{5,12},{6,13},{7,14},{8,15},{9,0},... | collective-permute-start | bytes 98312 | tf_op jit(solution)/shard_map/ppermute | solution.py:355
  284.8 6.8 %collective-permute-start.5 = (f32[64,128]{1,0:T(8,128)S(1)}, f32[64,128]{1,0:T(8,128)S(1)}, u32[]{:S(2)}, u32[]{:S(2)}) collective-permute-start(f32[64,128]{1,0:T(8,128)S(1)} %get-tuple-element.63), channel_id=1, source_target_pairs={{0,6},{1,7},{2,8},{3,9},{4,10},{5,11},{6,12},{7,13},{8,14},{9,15},... | collective-permute-start | bytes 98312 | tf_op jit(solution)/shard_map/ppermute | solution.py:355
  284.9 8.3 %collective-permute-start.4 = (f32[64,128]{1,0:T(8,128)S(1)}, f32[64,128]{1,0:T(8,128)}, u32[]{:S(2)}, u32[]{:S(2)}) collective-permute-start(f32[64,128]{1,0:T(8,128)S(1)} %get-tuple-element.64), channel_id=1, source_target_pairs={{0,5},{1,6},{2,7},{3,8},{4,9},{5,10},{6,11},{7,12},{8,13},{9,14},{... | collective-permute-start | bytes 98312 | tf_op jit(solution)/shard_map/ppermute | solution.py:355
  286.1 7.1 %collective-permute-start.3 = (f32[64,128]{1,0:T(8,128)S(1)}, f32[64,128]{1,0:T(8,128)}, u32[]{:S(2)}, u32[]{:S(2)}) collective-permute-start(f32[64,128]{1,0:T(8,128)S(1)} %get-tuple-element.65), channel_id=1, source_target_pairs={{0,4},{1,5},{2,6},{3,7},{4,8},{5,9},{6,10},{7,11},{8,12},{9,13},{1... | collective-permute-start | bytes 98312 | tf_op jit(solution)/shard_map/ppermute | solution.py:355
  288.4 6.2 %collective-permute-start.2 = (f32[64,128]{1,0:T(8,128)S(1)}, f32[64,128]{1,0:T(8,128)}, u32[]{:S(2)}, u32[]{:S(2)}) collective-permute-start(f32[64,128]{1,0:T(8,128)S(1)} %get-tuple-element.66), channel_id=1, source_target_pairs={{0,3},{1,4},{2,5},{3,6},{4,7},{5,8},{6,9},{7,10},{8,11},{9,12},{10... | collective-permute-start | bytes 98312 | tf_op jit(solution)/shard_map/ppermute | solution.py:355
  290.9 6.6 %collective-permute-start.1 = (f32[64,128]{1,0:T(8,128)S(1)}, f32[64,128]{1,0:T(8,128)}, u32[]{:S(2)}, u32[]{:S(2)}) collective-permute-start(f32[64,128]{1,0:T(8,128)S(1)} %get-tuple-element.67), channel_id=1, source_target_pairs={{0,2},{1,3},{2,4},{3,5},{4,6},{5,7},{6,8},{7,9},{8,10},{9,11},{10,... | collective-permute-start | bytes 98312 | tf_op jit(solution)/shard_map/ppermute | solution.py:355
  292.2 6.2 %collective-permute-start = (f32[64,128]{1,0:T(8,128)S(1)}, f32[64,128]{1,0:T(8,128)}, u32[]{:S(2)}, u32[]{:S(2)}) collective-permute-start(f32[64,128]{1,0:T(8,128)S(1)} %get-tuple-element.53), channel_id=1, source_target_pairs={{0,1},{1,2},{2,3},{3,4},{4,5},{5,6},{6,7},{7,8},{8,9},{9,10},{10,1... | collective-permute-start | bytes 98312 | tf_op jit(solution)/shard_map/ppermute | solution.py:355
  299.3 20.3 %collective-permute-start.21 = (f32[8,128]{1,0:T(8,128)S(1)}, f32[8,128]{1,0:T(8,128)S(1)}, u32[]{:S(2)}, u32[]{:S(2)}) collective-permute-start(f32[8,128]{1,0:T(8,128)S(1)} %get-tuple-element.69), channel_id=1, source_target_pairs={{0,112},{16,0},{32,16},{48,32},{64,48},{80,64},{96,80},{112,96},{1... | collective-permute-start | bytes 12296 | tf_op jit(solution)/shard_map/ppermute | solution.py:355
  304.3 15.4 %collective-permute-start.20 = (f32[8,128]{1,0:T(8,128)S(1)}, f32[8,128]{1,0:T(8,128)S(1)}, u32[]{:S(2)}, u32[]{:S(2)}) collective-permute-start(f32[8,128]{1,0:T(8,128)S(1)} %get-tuple-element.70), channel_id=1, source_target_pairs={{0,96},{16,112},{32,0},{48,16},{64,32},{80,48},{96,64},{112,80},{1... | collective-permute-start | bytes 12296 | tf_op jit(solution)/shard_map/ppermute | solution.py:355
  315.4 5.5 %collective-permute-start.19 = (f32[8,128]{1,0:T(8,128)S(1)}, f32[8,128]{1,0:T(8,128)S(1)}, u32[]{:S(2)}, u32[]{:S(2)}) collective-permute-start(f32[8,128]{1,0:T(8,128)S(1)} %get-tuple-element.71), channel_id=1, source_target_pairs={{0,80},{16,96},{32,112},{48,0},{64,16},{80,32},{96,48},{112,64},{1... | collective-permute-start | bytes 12296 | tf_op jit(solution)/shard_map/ppermute | solution.py:355
  315.4 5.5 %collective-permute-start.18 = (f32[8,128]{1,0:T(8,128)S(1)}, f32[8,128]{1,0:T(8,128)S(1)}, u32[]{:S(2)}, u32[]{:S(2)}) collective-permute-start(f32[8,128]{1,0:T(8,128)S(1)} %get-tuple-element.72), channel_id=1, source_target_pairs={{0,64},{16,80},{32,96},{48,112},{64,0},{80,16},{96,32},{112,48},{1... | collective-permute-start | bytes 12296 | tf_op jit(solution)/shard_map/ppermute | solution.py:355
  316.1 4.8 %collective-permute-start.17 = (f32[8,128]{1,0:T(8,128)S(1)}, f32[8,128]{1,0:T(8,128)S(1)}, u32[]{:S(2)}, u32[]{:S(2)}) collective-permute-start(f32[8,128]{1,0:T(8,128)S(1)} %get-tuple-element.73), channel_id=1, source_target_pairs={{0,48},{16,64},{32,80},{48,96},{64,112},{80,0},{96,16},{112,32},{1... | collective-permute-start | bytes 12296 | tf_op jit(solution)/shard_map/ppermute | solution.py:355
  319.6 3.9 collective-permute-start.16
  319.6 3.8 collective-permute-start.15
  323.5 5.9 %collective-permute-start.22 = (f32[8,128]{1,0:T(8,128)S(1)}, f32[8,128]{1,0:T(8,128)S(1)}, u32[]{:S(2)}, u32[]{:S(2)}) collective-permute-start(f32[8,128]{1,0:T(8,128)S(1)} %get-tuple-element.42), channel_id=1, source_target_pairs={{16,0},{32,16},{48,32},{64,48},{80,64},{96,80},{112,96},{0,112},{1... | collective-permute-start | bytes 12296 | tf_op jit(solution)/shard_map/ppermute | solution.py:363
  324.1 5.5 %collective-permute-start.23 = (f32[8,128]{1,0:T(8,128)S(1)}, f32[8,128]{1,0:T(8,128)S(1)}, u32[]{:S(2)}, u32[]{:S(2)}) collective-permute-start(f32[8,128]{1,0:T(8,128)S(1)} %get-tuple-element.42), channel_id=1, source_target_pairs={{32,0},{48,16},{64,32},{80,48},{96,64},{112,80},{0,96},{16,112},{3... | collective-permute-start | bytes 12296 | tf_op jit(solution)/shard_map/ppermute | solution.py:363
  325.1 5.6 %collective-permute-start.24 = (f32[8,128]{1,0:T(8,128)S(1)}, f32[8,128]{1,0:T(8,128)S(1)}, u32[]{:S(2)}, u32[]{:S(2)}) collective-permute-start(f32[8,128]{1,0:T(8,128)S(1)} %get-tuple-element.42), channel_id=1, source_target_pairs={{48,0},{64,16},{80,32},{96,48},{112,64},{0,80},{16,96},{32,112},{4... | collective-permute-start | bytes 12296 | tf_op jit(solution)/shard_map/ppermute | solution.py:363
  325.7 5.0 %collective-permute-start.25 = (f32[8,128]{1,0:T(8,128)S(1)}, f32[8,128]{1,0:T(8,128)S(1)}, u32[]{:S(2)}, u32[]{:S(2)}) collective-permute-start(f32[8,128]{1,0:T(8,128)S(1)} %get-tuple-element.42), channel_id=1, source_target_pairs={{64,0},{80,16},{96,32},{112,48},{0,64},{16,80},{32,96},{48,112},{6... | collective-permute-start | bytes 12296 | tf_op jit(solution)/shard_map/ppermute | solution.py:363
  327.6 4.2 %collective-permute-start.26 = (f32[8,128]{1,0:T(8,128)S(1)}, f32[8,128]{1,0:T(8,128)S(1)}, u32[]{:S(2)}, u32[]{:S(2)}) collective-permute-start(f32[8,128]{1,0:T(8,128)S(1)} %get-tuple-element.42), channel_id=1, source_target_pairs={{80,0},{96,16},{112,32},{0,48},{16,64},{32,80},{48,96},{64,112},{8... | collective-permute-start | bytes 12296 | tf_op jit(solution)/shard_map/ppermute | solution.py:363
  329.4 3.7 collective-permute-start.27
  329.5 3.6 collective-permute-start.28
  333.9 7.6 %collective-permute-start.29 = (f32[64,128]{1,0:T(8,128)S(1)}, f32[64,128]{1,0:T(8,128)S(1)}, u32[]{:S(2)}, u32[]{:S(2)}) collective-permute-start(f32[64,128]{1,0:T(8,128)S(1)} %get-tuple-element.40), channel_id=1, source_target_pairs={{1,0},{2,1},{3,2},{4,3},{5,4},{6,5},{7,6},{8,7},{9,8},{10,9},{11,1... | collective-permute-start | bytes 98312 | tf_op jit(solution)/shard_map/ppermute | solution.py:363
  337.2 8.4 %collective-permute-start.30 = (f32[64,128]{1,0:T(8,128)S(1)}, f32[64,128]{1,0:T(8,128)S(1)}, u32[]{:S(2)}, u32[]{:S(2)}) collective-permute-start(f32[64,128]{1,0:T(8,128)S(1)} %get-tuple-element.40), channel_id=1, source_target_pairs={{2,0},{3,1},{4,2},{5,3},{6,4},{7,5},{8,6},{9,7},{10,8},{11,9},{12,... | collective-permute-start | bytes 98312 | tf_op jit(solution)/shard_map/ppermute | solution.py:363
  338.7 8.2 %collective-permute-start.31 = (f32[64,128]{1,0:T(8,128)S(1)}, f32[64,128]{1,0:T(8,128)S(1)}, u32[]{:S(2)}, u32[]{:S(2)}) collective-permute-start(f32[64,128]{1,0:T(8,128)S(1)} %get-tuple-element.40), channel_id=1, source_target_pairs={{3,0},{4,1},{5,2},{6,3},{7,4},{8,5},{9,6},{10,7},{11,8},{12,9},{13... | collective-permute-start | bytes 98312 | tf_op jit(solution)/shard_map/ppermute | solution.py:363
  338.7 11.4 %collective-permute-start.32 = (f32[64,128]{1,0:T(8,128)S(1)}, f32[64,128]{1,0:T(8,128)S(1)}, u32[]{:S(2)}, u32[]{:S(2)}) collective-permute-start(f32[64,128]{1,0:T(8,128)S(1)} %get-tuple-element.40), channel_id=1, source_target_pairs={{4,0},{5,1},{6,2},{7,3},{8,4},{9,5},{10,6},{11,7},{12,8},{13,9},{1... | collective-permute-start | bytes 98312 | tf_op jit(solution)/shard_map/ppermute | solution.py:363
  338.7 12.4 %collective-permute-start.33 = (f32[64,128]{1,0:T(8,128)S(1)}, f32[64,128]{1,0:T(8,128)S(1)}, u32[]{:S(2)}, u32[]{:S(2)}) collective-permute-start(f32[64,128]{1,0:T(8,128)S(1)} %get-tuple-element.40), channel_id=1, source_target_pairs={{5,0},{6,1},{7,2},{8,3},{9,4},{10,5},{11,6},{12,7},{13,8},{14,9},{... | collective-permute-start | bytes 98312 | tf_op jit(solution)/shard_map/ppermute | solution.py:363
  341.4 12.8 %collective-permute-start.34 = (f32[64,128]{1,0:T(8,128)S(1)}, f32[64,128]{1,0:T(8,128)S(1)}, u32[]{:S(2)}, u32[]{:S(2)}) collective-permute-start(f32[64,128]{1,0:T(8,128)S(1)} %get-tuple-element.40), channel_id=1, source_target_pairs={{6,0},{7,1},{8,2},{9,3},{10,4},{11,5},{12,6},{13,7},{14,8},{15,9},... | collective-permute-start | bytes 98312 | tf_op jit(solution)/shard_map/ppermute | solution.py:363
  345.6 10.7 %collective-permute-start.35 = (f32[64,128]{1,0:T(8,128)S(1)}, f32[64,128]{1,0:T(8,128)S(1)}, u32[]{:S(2)}, u32[]{:S(2)}) collective-permute-start(f32[64,128]{1,0:T(8,128)S(1)} %get-tuple-element.40), channel_id=1, source_target_pairs={{7,0},{8,1},{9,2},{10,3},{11,4},{12,5},{13,6},{14,7},{15,8},{0,9},... | collective-permute-start | bytes 98312 | tf_op jit(solution)/shard_map/ppermute | solution.py:363
  346.9 11.3 %collective-permute-start.36 = (f32[64,128]{1,0:T(8,128)S(1)}, f32[64,128]{1,0:T(8,128)S(1)}, u32[]{:S(2)}, u32[]{:S(2)}) collective-permute-start(f32[64,128]{1,0:T(8,128)S(1)} %get-tuple-element.40), channel_id=1, source_target_pairs={{8,0},{9,1},{10,2},{11,3},{12,4},{13,5},{14,6},{15,7},{0,8},{1,9},... | collective-permute-start | bytes 98312 | tf_op jit(solution)/shard_map/ppermute | solution.py:363
  350.1 11.7 %collective-permute-start.37 = (f32[64,128]{1,0:T(8,128)S(1)}, f32[64,128]{1,0:T(8,128)S(1)}, u32[]{:S(2)}, u32[]{:S(2)}) collective-permute-start(f32[64,128]{1,0:T(8,128)S(1)} %get-tuple-element.40), channel_id=1, source_target_pairs={{9,0},{10,1},{11,2},{12,3},{13,4},{14,5},{15,6},{0,7},{1,8},{2,9},... | collective-permute-start | bytes 98312 | tf_op jit(solution)/shard_map/ppermute | solution.py:363
  351.0 11.8 %collective-permute-start.38 = (f32[64,128]{1,0:T(8,128)S(1)}, f32[64,128]{1,0:T(8,128)S(1)}, u32[]{:S(2)}, u32[]{:S(2)}) collective-permute-start(f32[64,128]{1,0:T(8,128)S(1)} %get-tuple-element.40), channel_id=1, source_target_pairs={{10,0},{11,1},{12,2},{13,3},{14,4},{15,5},{0,6},{1,7},{2,8},{3,9},... | collective-permute-start | bytes 98312 | tf_op jit(solution)/shard_map/ppermute | solution.py:363
  354.3 9.4 %collective-permute-start.39 = (f32[64,128]{1,0:T(8,128)S(1)}, f32[64,128]{1,0:T(8,128)S(1)}, u32[]{:S(2)}, u32[]{:S(2)}) collective-permute-start(f32[64,128]{1,0:T(8,128)S(1)} %get-tuple-element.40), channel_id=1, source_target_pairs={{11,0},{12,1},{13,2},{14,3},{15,4},{0,5},{1,6},{2,7},{3,8},{4,9},{... | collective-permute-start | bytes 98312 | tf_op jit(solution)/shard_map/ppermute | solution.py:363
  356.3 7.9 %collective-permute-start.40 = (f32[64,128]{1,0:T(8,128)S(1)}, f32[64,128]{1,0:T(8,128)S(1)}, u32[]{:S(2)}, u32[]{:S(2)}) collective-permute-start(f32[64,128]{1,0:T(8,128)S(1)} %get-tuple-element.40), channel_id=1, source_target_pairs={{12,0},{13,1},{14,2},{15,3},{0,4},{1,5},{2,6},{3,7},{4,8},{5,9},{6... | collective-permute-start | bytes 98312 | tf_op jit(solution)/shard_map/ppermute | solution.py:363
  358.2 6.7 %collective-permute-start.41 = (f32[64,128]{1,0:T(8,128)S(1)}, f32[64,128]{1,0:T(8,128)S(1)}, u32[]{:S(2)}, u32[]{:S(2)}) collective-permute-start(f32[64,128]{1,0:T(8,128)S(1)} %get-tuple-element.40), channel_id=1, source_target_pairs={{13,0},{14,1},{15,2},{0,3},{1,4},{2,5},{3,6},{4,7},{5,8},{6,9},{7,... | collective-permute-start | bytes 98312 | tf_op jit(solution)/shard_map/ppermute | solution.py:363
  361.8 6.4 %collective-permute-start.42 = (f32[64,128]{1,0:T(8,128)S(1)}, f32[64,128]{1,0:T(8,128)S(1)}, u32[]{:S(2)}, u32[]{:S(2)}) collective-permute-start(f32[64,128]{1,0:T(8,128)S(1)} %get-tuple-element.40), channel_id=1, source_target_pairs={{14,0},{15,1},{0,2},{1,3},{2,4},{3,5},{4,6},{5,7},{6,8},{7,9},{8,1... | collective-permute-start | bytes 98312 | tf_op jit(solution)/shard_map/ppermute | solution.py:363
  362.8 6.1 %collective-permute-start.43 = (f32[64,128]{1,0:T(8,128)S(1)}, f32[64,128]{1,0:T(8,128)S(1)}, u32[]{:S(2)}, u32[]{:S(2)}) collective-permute-start(f32[64,128]{1,0:T(8,128)S(1)} %get-tuple-element.40), channel_id=1, source_target_pairs={{15,0},{0,1},{1,2},{2,3},{3,4},{4,5},{5,6},{6,7},{7,8},{8,9},{9,10... | collective-permute-start | bytes 98312 | tf_op jit(solution)/shard_map/ppermute | solution.py:363
  (14 other events, 721.0 us)

commit v2 on v1

v2 whole, which is shorter than its diff:
```python
import functools

import jax
import jax.numpy as jnp
from jax import lax
from jax.experimental import pallas as pl
from jax.experimental.pallas import tpu as pltpu
from jax.sharding import PartitionSpec as P

FEAT = 32
VOX = 512
WIDTH = 256
BLOCK = 128
RAY_LEN = 32
GROUP = 8
GRAD_ROWS = 1024

AXES = ("view", "space")
step_len = 0.05
F32 = jnp.float32
BF16 = jnp.bfloat16


def dot_nn(left, right, precision=None):
    return lax.dot_general(
        left, right, (((1,), (0,)), ((), ())), precision=precision, preferred_element_type=F32
    )


def dot_nt(left, right, precision=None):
    return lax.dot_general(
        left, right, (((1,), (1,)), ((), ())), precision=precision, preferred_element_type=F32
    )


def dot_tn(left, right):
    return lax.dot_general(
        left, right, (((0,), (0,)), ((), ())), preferred_element_type=F32
    )


def lane_sums(values, matrix):
    return dot_nn(values, matrix, precision=lax.Precision.HIGHEST)


def render_grad(raw, live, goal, before, within, after):
    rows = live.shape[0]
    small = jnp.exp(-jnp.abs(raw[0]))
    sigma = jnp.maximum(raw[0], 0.0) + jnp.log1p(small)
    slope = jnp.where(raw[0] >= 0.0, 1.0, small) / (1.0 + small)
    shades = [jax.nn.sigmoid(channel) for channel in raw[1:]]
    depth = step_len * sigma * live
    faded = jnp.exp(-depth)
    trans = jnp.exp(depth - lane_sums(depth, before))
    weight = trans * (1.0 - faded)
    stacked = jnp.concatenate([weight * shade for shade in shades], axis=0)
    color = lane_sums(stacked, within)
    colors = [color[c * rows : (c + 1) * rows] for c in range(3)]
    miss = [colors[c] - goal[c] for c in range(3)]
    d_weight = miss[0] * shades[0] + miss[1] * shades[1] + miss[2] * shades[2]
    d_depth = d_weight * (trans * faded) - lane_sums(d_weight * weight, after)
    d_raw = [step_len * live * d_depth * slope]
    for c in range(3):
        d_raw.append(weight * miss[c] * shades[c] * (1.0 - shades[c]))
    return colors, d_raw


def lane_matrices():
    row = lax.broadcasted_iota(jnp.int32, (BLOCK, BLOCK), 0)
    col = lax.broadcasted_iota(jnp.int32, (BLOCK, BLOCK), 1)
    same = (row // RAY_LEN) == (col // RAY_LEN)
    before = (same & (row <= col)).astype(F32)
    after = (same & (row > col)).astype(F32)
    return before, same.astype(F32), after


def plan_kernel(owner_ref, brick_ref, wish_ref, lists_ref):
    amount = owner_ref.shape[0]

    def clear(i, state):
        wish_ref[2 * i] = -1
        wish_ref[2 * i + 1] = -1
        return state

    lax.fori_loop(0, wish_ref.shape[0] // 2, clear, 0, unroll=8)

    def place(i, state):
        firsts, seconds = state
        owner = owner_ref[i]
        rank = jnp.where(wish_ref[2 * owner] >= 0, 1, 0)
        wish_ref[2 * owner + rank] = brick_ref[i]
        lists_ref[0, 1 + firsts] = i
        lists_ref[1, 1 + seconds] = i
        return firsts + 1 - rank, seconds + rank

    counts = lax.fori_loop(0, amount, place, (0, 0), unroll=4)
    for rank in range(2):
        lists_ref[rank, 0] = counts[rank]
        for k in range(GROUP):
            lists_ref[rank, 1 + counts[rank] + k] = 0


def plan(owners, bricks, dev_count):
    smem = pl.BlockSpec(memory_space=pltpu.SMEM)
    return pl.pallas_call(
        plan_kernel,
        out_shape=(
            jax.ShapeDtypeStruct((dev_count * 2,), jnp.int32),
            jax.ShapeDtypeStruct((2, owners.shape[0] + 2 * GROUP), jnp.int32),
        ),
        in_specs=[smem, smem],
        out_specs=(smem, smem),
        name="plan",
    )(owners, bricks)


def step_kernel(
    first,
    lists_ref,
    owner_ref,
    b_out_ref,
    weights_hbm,
    bricks_hbm,
    rays_ref,
    w_in_ref,
    b_in_ref,
    w_hid_ref,
    b_hid_ref,
    w_out_ref,
    carried_ref,
    _,
    grads_hbm,
    color_ref,
    sums_ref,
    weights_buf,
    bricks_buf,
    grads_buf,
    rays_buf,
    raw_buf,
    d_raw_buf,
    step_buf,
    lanes_buf,
    w_in_t,
    w_hid_t,
    w_out_rows,
    b_one_col,
    b_two_col,
    acc_hid,
    acc_in,
    acc_out,
    acc_b_hid,
    acc_b_in,
    acc_b_out,
    parts_buf,
    weights_sem,
    bricks_sem,
    grads_sem,
    parts_sem,
):
    which = 0 if first else 1
    total = lists_ref[which, 0]
    steps = (total + GROUP - 1) // GROUP

    def fetch(step, side):
        for k in range(GROUP):
            block = lists_ref[which, 1 + step * GROUP + k]
            pltpu.make_async_copy(
                weights_hbm.at[block], weights_buf.at[side, k], weights_sem.at[side, k]
            ).start()
            pltpu.make_async_copy(
                bricks_hbm.at[owner_ref[block]], bricks_buf.at[side, k], bricks_sem.at[side, k]
            ).start()

    def arrive(side):
        for k in range(GROUP):
            pltpu.make_async_copy(
                weights_hbm.at[0], weights_buf.at[side, k], weights_sem.at[side, k]
            ).wait()
            pltpu.make_async_copy(
                bricks_hbm.at[0], bricks_buf.at[side, k], bricks_sem.at[side, k]
            ).wait()

    def place(owner):
        return grads_hbm.at[owner, pl.ds(which * BLOCK, BLOCK)]

    def send(step, side):
        for k in range(GROUP):
            at = step * GROUP + k

            @pl.when(at < total)
            def _():
                owner = owner_ref[lists_ref[which, 1 + at]]
                pltpu.make_async_copy(
                    grads_buf.at[side, k], place(owner), grads_sem.at[side, k]
                ).start()

    def settle(step, side):
        for k in range(GROUP):
            at = step * GROUP + k

            @pl.when((step >= 0) & (at < total))
            def _():
                pltpu.make_async_copy(
                    grads_buf.at[side, k], place(0), grads_sem.at[side, k]
                ).wait()

    @pl.when(steps > 0)
    def _():
        fetch(0, 0)

    for ref in (acc_hid, acc_in, acc_out, acc_b_hid, acc_b_in, acc_b_out, color_ref):
        ref[...] = jnp.zeros_like(ref)
    w_in_t[...] = w_in_ref[...].T
    w_hid_t[...] = w_hid_ref[...].T
    w_out_rows[...] = jnp.zeros_like(w_out_rows)
    w_out_rows[0:4, :] = w_out_ref[...]
    d_raw_buf[...] = jnp.zeros_like(d_raw_buf)
    b_one_col[...] = jnp.broadcast_to(b_in_ref[...], (BLOCK, WIDTH)).T
    b_two_col[...] = jnp.broadcast_to(b_hid_ref[...], (BLOCK, WIDTH)).T
    for at, matrix in enumerate(lane_matrices()):
        lanes_buf[at] = matrix
    ray = lax.broadcasted_iota(jnp.int32, (BLOCK // RAY_LEN, BLOCK), 0)
    lane = lax.broadcasted_iota(jnp.int32, (BLOCK // RAY_LEN, BLOCK), 1)
    repeat = (lane // RAY_LEN == ray).astype(F32)
    for c in range(4):
        rays_buf[c] = lane_sums(rays_ref[c], repeat)

    def one_step(step, state):
        side = step % 2
        arrive(side)

        @pl.when(step + 1 < steps)
        def _():
            fetch(step + 1, 1 - side)

        for k in range(GROUP):
            at = step * GROUP + k
            block = lists_ref[which, 1 + at]
            for c in range(3):
                step_buf[c, pl.ds(k, 1), :] = rays_buf[c, pl.ds(block, 1), :]
            used = jnp.where(at < total, rays_buf[3, pl.ds(block, 1), :], 0.0)
            step_buf[3, pl.ds(k, 1), :] = used
        position = lax.broadcasted_iota(jnp.int32, (GROUP, BLOCK), 1) % RAY_LEN
        live = (position.astype(F32) < step_buf[3]).astype(F32)

        feats = jnp.concatenate(
            [dot_nt(bricks_buf[side, k], weights_buf[side, k]) for k in range(GROUP)], axis=1
        ).astype(BF16)
        pre_one = dot_nn(w_in_t[...], feats) + b_one_col[:, 0:1]
        act_one = jnp.maximum(pre_one, 0.0).astype(BF16)
        pre_two = dot_nn(w_hid_t[...], act_one) + b_two_col[:, 0:1]
        act_two = jnp.maximum(pre_two, 0.0).astype(BF16)
        raw = dot_nn(w_out_rows[...], act_two)
        for k in range(GROUP):
            for c in range(4):
                raw_buf[c, k : k + 1, :] = raw[c : c + 1, k * BLOCK : (k + 1) * BLOCK]
        colors, d_raw = render_grad(
            [raw_buf[c] + b_out_ref[c] for c in range(4)],
            live,
            [step_buf[c] for c in range(3)],
            lanes_buf[0],
            lanes_buf[1],
            lanes_buf[2],
        )
        for k in range(GROUP):
            at = step * GROUP + k
            row = jnp.where(at < total, lists_ref[which, 1 + at], BLOCK)
            for c in range(3):
                color_ref[c, pl.ds(row, 1), :] = colors[c][k : k + 1]
            for c in range(4):
                d_raw_buf[c : c + 1, k * BLOCK : (k + 1) * BLOCK] = d_raw[c][k : k + 1]
        for c in range(4):
            acc_b_out[c] += d_raw[c]
        d_raw_b = d_raw_buf[...].astype(BF16)
        acc_out[...] += dot_nt(d_raw_b, act_two)
        d_two = jnp.where(pre_two > 0.0, dot_tn(w_out_rows[...], d_raw_b), 0.0)
        d_two_b = d_two.astype(BF16)
        acc_hid[...] += dot_nt(act_one, d_two_b)
        d_one = jnp.where(pre_one > 0.0, dot_nn(w_hid_ref[...], d_two_b), 0.0)
        d_one_b = d_one.astype(BF16)
        acc_in[...] += dot_nt(feats, d_one_b)
        b_two = acc_b_hid[...]
        b_one = acc_b_in[...]
        for k in range(GROUP):
            b_two += d_two[:, k * BLOCK : (k + 1) * BLOCK]
            b_one += d_one[:, k * BLOCK : (k + 1) * BLOCK]
        acc_b_hid[...] = b_two
        acc_b_in[...] = b_one
        d_feats = dot_nn(w_in_ref[...], d_one_b).astype(BF16)
        settle(step - 2, side)
        for k in range(GROUP):
            grad = dot_nn(d_feats[:, k * BLOCK : (k + 1) * BLOCK], weights_buf[side, k])
            grad = grad.astype(BF16)
            for v in range(VOX // BLOCK):
                grads_buf[side, k, v * FEAT : (v + 1) * FEAT] = grad[:, v * BLOCK : (v + 1) * BLOCK]
        send(step, side)
        return state

    lax.fori_loop(0, steps, one_step, 0)

    ones = jnp.ones((8, BLOCK), F32)

    def over_lanes(values):
        return dot_nt(ones, values, precision=lax.Precision.HIGHEST)

    half = WIDTH // 2
    sums_ref[0:256, :] = acc_hid[:, :half]
    sums_ref[256:512, :] = acc_hid[:, half:]
    sums_ref[512:544, :] = acc_in[:, :half]
    sums_ref[544:576, :] = acc_in[:, half:]
    sums_ref[576:584, :] = acc_out[:, :half]
    sums_ref[584:592, :] = acc_out[:, half:]
    b_hid_row = over_lanes(acc_b_hid[...])
    b_in_row = over_lanes(acc_b_in[...])
    sums_ref[592:600, :] = b_hid_row[:, :half]
    sums_ref[600:608, :] = b_hid_row[:, half:]
    sums_ref[608:616, :] = b_in_row[:, :half]
    sums_ref[616:624, :] = b_in_row[:, half:]
    sums_ref[624:GRAD_ROWS, :] = jnp.zeros((GRAD_ROWS - 624, BLOCK), F32)
    for c in range(4):
        sums_ref[624 + c : 625 + c, :] = jnp.sum(acc_b_out[c], axis=0, keepdims=True)

    if not first:
        sums_ref[...] += carried_ref[...]
        sums = sums_ref[...].reshape(GRAD_ROWS // 8, 8, BLOCK)
        high = sums.astype(BF16)
        parts_buf[:, 0:8, :] = high
        parts_buf[:, 8:16, :] = (sums - high.astype(F32)).astype(BF16)
        copy = pltpu.make_async_copy(
            parts_buf, grads_hbm.at[:, pl.ds(2 * BLOCK, 16)], parts_sem
        )
        copy.start()
        copy.wait()

    settle(steps - 2, steps % 2)
    settle(steps - 1, (steps + 1) % 2)


def run_blocks(first, lists, owners, weights, bricks, rays, params, carried, grads):
    vmem = pl.BlockSpec(memory_space=pltpu.VMEM)
    smem = pl.BlockSpec(memory_space=pltpu.SMEM)
    hbm = pl.BlockSpec(memory_space=pl.ANY)
    w_in, b_in, w_hid, b_hid, w_out, b_out = params
    amount = weights.shape[0] if first else weights.shape[0] // 8
    cost = pl.CostEstimate(
        flops=amount * 70_000_000, bytes_accessed=amount * 200_000, transcendentals=amount * 1000
    )
    return pl.pallas_call(
        functools.partial(step_kernel, first),
        out_shape=(
            jax.ShapeDtypeStruct((bricks.shape[0], 2 * BLOCK + 16, BLOCK), BF16),
            jax.ShapeDtypeStruct((3, BLOCK + 8, BLOCK), F32),
            jax.ShapeDtypeStruct((GRAD_ROWS, BLOCK), F32),
        ),
        in_specs=[smem, smem, smem, hbm, hbm] + [vmem] * 7 + [hbm],
        out_specs=(hbm, vmem, vmem),
        scratch_shapes=[
            pltpu.VMEM((2, GROUP, BLOCK, VOX), BF16),
            pltpu.VMEM((2, GROUP, FEAT, VOX), BF16),
            pltpu.VMEM((2, GROUP, BLOCK, BLOCK), BF16),
            pltpu.VMEM((4, BLOCK, BLOCK), F32),
            pltpu.VMEM((4, GROUP, BLOCK), F32),
            pltpu.VMEM((8, GROUP * BLOCK), F32),
            pltpu.VMEM((4, GROUP, BLOCK), F32),
            pltpu.VMEM((3, BLOCK, BLOCK), F32),
            pltpu.VMEM((WIDTH, FEAT), BF16),
            pltpu.VMEM((WIDTH, WIDTH), BF16),
            pltpu.VMEM((8, WIDTH), BF16),
            pltpu.VMEM((WIDTH, BLOCK), F32),
            pltpu.VMEM((WIDTH, BLOCK), F32),
            pltpu.VMEM((WIDTH, WIDTH), F32),
            pltpu.VMEM((FEAT, WIDTH), F32),
            pltpu.VMEM((8, WIDTH), F32),
            pltpu.VMEM((WIDTH, BLOCK), F32),
            pltpu.VMEM((WIDTH, BLOCK), F32),
            pltpu.VMEM((4, GROUP, BLOCK), F32),
            pltpu.VMEM((GRAD_ROWS // 8, 16, BLOCK), BF16),
            pltpu.SemaphoreType.DMA((2, GROUP)),
            pltpu.SemaphoreType.DMA((2, GROUP)),
            pltpu.SemaphoreType.DMA((2, GROUP)),
            pltpu.SemaphoreType.DMA,
        ],
        compiler_params=pltpu.CompilerParams(vmem_limit_bytes=60 << 20),
        input_output_aliases={} if first else {12: 0},
        cost_estimate=cost,
        name="blocks_first" if first else "blocks_second",
    )(
        lists,
        owners,
        b_out,
        weights,
        bricks,
        rays,
        w_in,
        b_in[None],
        w_hid,
        b_hid[None],
        w_out,
        carried,
        grads,
    )


TAKE = 8


def collect_kernel(ids_ref, grads_ref, out_ref):
    step = pl.program_id(0)

    @pl.when(step == 0)
    def _():
        out_ref[...] = jnp.zeros_like(out_ref)

    for k in range(TAKE):
        for r in range(2):
            brick = ids_ref[2 * (step * TAKE + k) + r]

            @pl.when(brick >= 0)
            def _():
                for v in range(VOX // BLOCK):
                    rows = pl.ds(r * BLOCK + v * FEAT, FEAT)
                    out_ref[brick, :, v * BLOCK : (v + 1) * BLOCK] += grads_ref[k, rows].astype(F32)


def collect(ids, grads, own):
    amount, rows, _ = grads.shape
    return pl.pallas_call(
        collect_kernel,
        out_shape=jax.ShapeDtypeStruct((own, FEAT, VOX), F32),
        grid_spec=pltpu.PrefetchScalarGridSpec(
            num_scalar_prefetch=1,
            grid=(amount // TAKE,),
            in_specs=[pl.BlockSpec((TAKE, rows, BLOCK), lambda i, ids: (i, 0, 0))],
            out_specs=pl.BlockSpec((own, FEAT, VOX), lambda i, ids: (0, 0, 0)),
        ),
        compiler_params=pltpu.CompilerParams(vmem_limit_bytes=60 << 20),
        cost_estimate=pl.CostEstimate(
            flops=amount * FEAT * VOX, bytes_accessed=amount * FEAT * VOX * 4, transcendentals=0
        ),
        name="collect",
    )(ids, grads)


def exchange(values):
    return lax.all_to_all(values, AXES, split_axis=0, concat_axis=0, tiled=True)


def body(
    brick_feats,
    interp_weights,
    block_owner,
    block_brick,
    sample_count,
    target,
    w_in,
    b_in,
    w_hid,
    b_hid,
    w_out,
    b_out,
):
    own_blocks = interp_weights.shape[0]
    own_bricks = brick_feats.shape[0]
    dev_count = lax.axis_size(AXES)
    owners = block_owner[:, 0]
    wish, lists = plan(owners, block_brick[:, 0], dev_count)
    asked = exchange(wish.reshape(dev_count, 1, 2)).reshape(dev_count, 2)

    bricks_t = jnp.swapaxes(brick_feats, 1, 2)
    fetched = [exchange(bricks_t[jnp.maximum(asked[:, r], 0)]) for r in range(2)]

    rays = jnp.concatenate([target, sample_count.astype(F32)[None]])
    rays = rays.reshape(4, own_blocks, BLOCK // RAY_LEN)
    params = (w_in, b_in, w_hid, b_hid, w_out, b_out)
    nothing = jnp.zeros((8, BLOCK), F32)
    grads, color_0, sums = run_blocks(
        True, lists, owners, interp_weights, fetched[0], rays, params, nothing, nothing
    )
    grads, color_1, _ = run_blocks(
        False, lists, owners, interp_weights, fetched[1], rays, params, sums, grads
    )
    returned = exchange(grads)

    parts = returned[:, 2 * BLOCK :].astype(F32)
    mine = jnp.sum(parts[:, :8] + parts[:, 8:], axis=0)
    totals = exchange(jnp.broadcast_to(mine[None], (dev_count, 8, BLOCK)))
    brick_grad = jnp.swapaxes(collect(asked.reshape(-1), returned, own_bricks), 1, 2)

    totals = totals.reshape(GRAD_ROWS, BLOCK) / (sample_count.shape[0] * dev_count)

    def joined(start, rows):
        return jnp.concatenate([totals[start : start + rows], totals[start + rows : start + 2 * rows]], axis=1)

    g_w_hid = joined(0, WIDTH)
    g_w_in = joined(2 * WIDTH, FEAT)
    g_w_out = joined(576, 8)[:4]
    g_b_hid = joined(592, 8)[0]
    g_b_in = joined(608, 8)[0]
    g_b_out = jnp.sum(totals[624:628], axis=1)
    color = (color_0 + color_1)[:, :own_blocks, ::RAY_LEN].reshape(3, -1)
    return (brick_grad, color, g_w_in, g_b_in, g_w_hid, g_b_hid, g_w_out, g_b_out)


def solution(mesh):
    shared = P(AXES, None, None)
    return jax.shard_map(
        body,
        mesh=mesh,
        in_specs=(
            shared,
            shared,
            P(AXES, None),
            P(AXES, None),
            P(AXES),
            P(None, AXES),
            P(),
            P(),
            P(),
            P(),
            P(),
            P(),
        ),
        out_specs=(shared, P(None, AXES), P(), P(), P(), P(), P(), P()),
        check_vma=False,
    )
```

time: 402 us -> 293 us (0.73)
  blocking collectives: 21.1 us -> 132 us
  waiting for transfers between devices: 149 us -> 50.8 us
  starting transfers between devices: 97 us -> 14.8 us
  local copies, waits for them, and re-layouts: 36.7 us -> 14.3 us
  other arithmetic: 19.5 us -> 4.42 us
    all_to_all x1 -> x2, blocking collectives: 21.1 us -> 132 us  [exchange(): return lax.all_to_all(values, AXES, split_axis=0, concat_axis=0, tiled=True)]
    ppermute x44 -> x0, waiting for transfers between devices: 100 us -> none  [the longest x22 94.8 us: scatter_sum(): lax.ppermute(piece, axis, [(i, (i + shift) % size) for i in range(size)])]
    ppermute x44 -> x0, starting transfers between devices: 75.9 us -> none  [the longest x22 48.6 us: scatter_sum(): lax.ppermute(piece, axis, [(i, (i + shift) % size) for i in range(size)])]
    unnamed x79 -> x15, local copies, waits for them, and re-layouts: 21.6 us -> 3.53 us
    select_n x4 -> x0, other arithmetic: 7.26 us -> none  [the longest x2 3.66 us: body(): blocks = jnp.where(empty, last, blocks)]
    all_to_all x3, starting transfers between devices: 21.1 us -> 14.8 us  [exchange(): return lax.all_to_all(values, AXES, split_axis=0, concat_axis=0, tiled=True)]
  transfers between devices with their start and end apart: 47 -> 3, of which waited for: 11 -> 2; matrix products, arithmetic and copies ran while one was open for 13% -> 2% of each run, Pallas kernels for 12% -> 21%
where the time goes in v2:
time: 293 us; the launch traced here: 292 us
  blocking collectives  132 us (45%)
  Pallas kernels  74.4 us (25%)
  waiting for transfers between devices  50.8 us (17%)
  starting transfers between devices  14.8 us (5%)
  local copies, waits for them, and re-layouts  14.3 us (5%)
  other arithmetic  4.42 us (2%)
    all_to_all x2, blocking collectives, exchange(): return lax.all_to_all(values, AXES, split_axis=0, concat_axis=0, tiled=True)  132 us
    pallas_call x2, Pallas kernels, run_blocks(): pl.pallas_call(functools.partial(step_kernel, first), out_shape=(jax.Shap...  58.6 us
    all_to_all x3, waiting for transfers between devices, exchange(): return lax.all_to_all(values, AXES, split_axis=0, concat_axis=0, tiled=True)  50.8 us
    all_to_all x3, starting transfers between devices, exchange(): return lax.all_to_all(values, AXES, split_axis=0, concat_axis=0, tiled=True)  14.8 us
    pallas_call x1, Pallas kernels, collect(): pl.pallas_call(collect_kernel, out_shape=jax.ShapeDtypeStruct((own, FEAT,...  13.1 us
  transfers between devices with their start and end apart: 3, of which 2 were waited for; matrix products, arithmetic and copies ran while one was open for 2% of the time, Pallas kernels for 21%

profile of v2, /device:TPU:1, one launch (start us, length us, event | category | flops | bytes accessed | tf_op | source)
XLA Modules:
  0.0 292.1 jit_solution(6483568777095080278)
XLA Ops:
  0.6 0.0 copy-start
  0.6 2.7 plan.1
  3.3 0.8 reshape.43
  4.2 21.1 %all_to_all.25 = s32[128,1,2]{2,1,0:T(1,128)S(1)} all-to-all(s32[128,1,2]{2,1,0:T(1,128)S(1)} %bitcast.36), channel_id=1, replica_groups=mesh['view'=8,'space'=16] {'view','space'}, dimensions={0} | all-to-all | bytes 2048 | tf_op jit(solution)/shard_map/all_to_all | solution.py:445
  25.3 0.2 fusion.1
  25.5 0.0 copy-done
  25.5 2.8 gather_fusion.1
  28.2 5.3 %all-to-all-start.2 = ((bf16[128,32,512]{2,1,0:T(8,128)(2,1)}), bf16[128,32,512]{2,1,0:T(8,128)(2,1)}, u32[]{:S(2)}, u32[]{:S(2)}) async-start(bf16[128,32,512]{2,1,0:T(8,128)(2,1)} %gather_fusion.1), calls=%async_computation.2 | async-start | bytes 8388608 | tf_op jit(solution)/shard_map/all_to_all | solution.py:445
  33.6 2.8 gather_fusion
  36.4 0.0 copy-start.6
  36.4 0.0 copy-start.5
  36.4 48.4 %all-to-all-done.2.bricks_hbm = bf16[128,32,512]{2,1,0:T(8,128)(2,1)} async-done(((bf16[128,32,512]{2,1,0:T(8,128)(2,1)}), bf16[128,32,512]{2,1,0:T(8,128)(2,1)}, u32[]{:S(2)}, u32[]{:S(2)}) %all-to-all-start.2) | async-done | bytes 4194336 | tf_op jit(solution)/shard_map/all_to_all | solution.py:445
  84.8 5.5 %all-to-all-start.1 = ((bf16[128,32,512]{2,1,0:T(8,128)(2,1)}), bf16[128,32,512]{2,1,0:T(8,128)(2,1)}, u32[]{:S(2)}, u32[]{:S(2)}) async-start(bf16[128,32,512]{2,1,0:T(8,128)(2,1)} %gather_fusion), calls=%async_computation.1 | async-start | bytes 8388608 | tf_op jit(solution)/shard_map/all_to_all | solution.py:445
  90.4 0.0 copy-done.6
  90.4 0.1 concatenate.24
  90.5 0.0 copy-done.5
  90.5 0.2 concatenate.23
  90.8 0.0 copy-start.2
  90.8 0.7 broadcast_in_dim.10.carried_ref._
  91.4 0.0 copy-done.2
  91.5 47.7 %blocks_first.1 = (bf16[128,272,128]{2,1,0:T(8,128)(2,1)}, f32[3,136,128]{2,1,0:T(8,128)}, f32[1024,128]{1,0:T(8,128)}) custom-call(s32[2,144]{1,0:T(2,128)} %get-tuple-element.16.lists_ref, s32[128]{0:T(128)} %bitcast.44, f32[4]{0:T(128)} %b_out_ref.3, bf16[128,128,512]{2,1,0:T(8,128)(2,1)} %weights_hbm.3, bf16[128,32,512]{2,1,0:T(8,128)(2,1)} %all-to-all-done.2.bricks_hbm, ...), custom_call_target="tpu_custom_call" | custom-call | flops 8960000000 | bytes 25600000 | tf_op jit(solution)/shard_map/blocks_first/pallas_call | solution.py:348
  139.2 2.4 all-to-all-done.1.bricks_hbm
  141.6 10.9 %blocks_second.1 = (bf16[128,272,128]{2,1,0:T(8,128)(2,1)}, f32[3,136,128]{2,1,0:T(8,128)}, f32[1024,128]{1,0:T(8,128)}) custom-call(s32[2,144]{1,0:T(2,128)} %get-tuple-element.16.lists_ref, s32[128]{0:T(128)} %bitcast.45, f32[4]{0:T(128)} %b_out_ref.3, bf16[128,128,512]{2,1,0:T(8,128)(2,1)} %weights_hbm.3, ...), custom_call_target="tpu_custom_call", output_to_operand_aliasing={{0}: (12, {})} | custom-call | flops 1120000000 | bytes 3200000 | tf_op jit(solution)/shard_map/blocks_second/pallas_call | solution.py:348
  152.5 111.4 %all_to_all.26.grads_ref = bf16[128,272,128]{2,1,0:T(8,128)(2,1)S(1)} all-to-all(bf16[128,272,128]{2,1,0:T(8,128)(2,1)} %get-tuple-element.19), channel_id=1, replica_groups=mesh['view'=8,'space'=16] {'view','space'}, dimensions={0} | all-to-all | bytes 17825792 | tf_op jit(solution)/shard_map/all_to_all | solution.py:445
  263.9 0.0 copy-start.1
  263.9 3.4 %copy-done.1 = bf16[128,272,128]{2,1,0:T(8,128)(2,1)} copy-done((bf16[128,272,128]{2,1,0:T(8,128)(2,1)}, bf16[128,272,128]{2,1,0:T(8,128)(2,1)S(1)}, u32[]{:S(2)}) %copy-start.1) | copy-done | bytes 8912920
  267.3 0.0 copy-start.3
  267.3 0.0 copy-start.4
  267.3 0.1 slice_convert_fusion
  267.4 0.1 fusion
  267.5 0.9 broadcast_in_dim.11
  268.4 4.0 %all-to-all-start.4 = ((f32[128,8,128]{2,1,0:T(8,128)}), f32[128,8,128]{2,1,0:T(8,128)S(1)}, u32[]{:S(2)}, u32[]{:S(2)}) async-start(f32[128,8,128]{2,1,0:T(8,128)} %broadcast_in_dim.11), calls=%async_computation.4 | async-start | bytes 1048576 | tf_op jit(solution)/shard_map/all_to_all | solution.py:445
  272.4 0.5 broadcast.28
  272.9 0.8 reduce.7
  273.7 0.7 reshape_reshape.3.ids_ref
  274.4 0.0 copy-done.3
  274.4 0.0 copy-done.4
  274.4 0.5 slice.92
  275.0 0.7 reshape.45
  275.7 13.1 %collect.1 = f32[64,32,512]{2,1,0:T(8,128)} custom-call(s32[256]{0:T(256)} %reshape_reshape.3.ids_ref, bf16[128,272,128]{2,1,0:T(8,128)(2,1)} %copy-done.1), custom_call_target="tpu_custom_call" | custom-call | flops 2097152 | bytes 8388608 | tf_op jit(solution)/shard_map/collect/pallas_call | solution.py:427
  288.9 0.0 all-to-all-done.4
  288.9 0.1 fusion.3
  289.0 0.6 slice_reduce_fusion
  289.6 0.6 pad_maximum_fusion.2
  290.2 0.7 pad_maximum_fusion
  290.9 0.6 pad_maximum_fusion.1
  291.6 0.6 pad_maximum_fusion.3
  (9 shorter events, 0.1 us)
Async XLA Ops:
  0.6 24.8 %copy-start = (bf16[64,512,32]{1,2,0:T(8,128)(2,1)S(1)}, bf16[64,512,32]{1,2,0:T(8,128)(2,1)}, u32[]{:S(2)}) copy-start(bf16[64,512,32]{1,2,0:T(8,128)(2,1)} %param.12) | copy-start | bytes 6291460
  28.2 56.6 %all-to-all-start.2 = ((bf16[128,32,512]{2,1,0:T(8,128)(2,1)}), bf16[128,32,512]{2,1,0:T(8,128)(2,1)}, u32[]{:S(2)}, u32[]{:S(2)}) async-start(bf16[128,32,512]{2,1,0:T(8,128)(2,1)} %gather_fusion.1), calls=%async_computation.2 | async-start | bytes 8388608 | tf_op jit(solution)/shard_map/all_to_all | solution.py:445
  36.4 54.0 %copy-start.6 = (s32[512]{0:T(512)S(1)}, s32[512]{0:T(512)}, u32[]{:S(2)}) copy-start(s32[512]{0:T(512)} %param.16) | copy-start | bytes 6148
  36.4 54.1 %copy-start.5 = (f32[3,512]{1,0:T(4,128)S(1)}, f32[3,512]{1,0:T(4,128)}, u32[]{:S(2)}) copy-start(f32[3,512]{1,0:T(4,128)} %param.17) | copy-start | bytes 18436
  84.8 56.7 %all-to-all-start.1 = ((bf16[128,32,512]{2,1,0:T(8,128)(2,1)}), bf16[128,32,512]{2,1,0:T(8,128)(2,1)}, u32[]{:S(2)}, u32[]{:S(2)}) async-start(bf16[128,32,512]{2,1,0:T(8,128)(2,1)} %gather_fusion), calls=%async_computation.1 | async-start | bytes 8388608 | tf_op jit(solution)/shard_map/all_to_all | solution.py:445
  90.8 0.7 copy-start.2
  263.9 3.4 %copy-start.1 = (bf16[128,272,128]{2,1,0:T(8,128)(2,1)}, bf16[128,272,128]{2,1,0:T(8,128)(2,1)S(1)}, u32[]{:S(2)}) copy-start(bf16[128,272,128]{2,1,0:T(8,128)(2,1)S(1)} %all_to_all.26.grads_ref) | copy-start | bytes 26738692
  267.3 7.1 %copy-start.3 = (f32[3,136,128]{2,1,0:T(8,128)S(1)}, f32[3,136,128]{2,1,0:T(8,128)}, u32[]{:S(2)}) copy-start(f32[3,136,128]{2,1,0:T(8,128)} %get-tuple-element.20) | copy-start | bytes 626692
  267.3 7.1 %copy-start.4 = (f32[3,136,128]{2,1,0:T(8,128)S(1)}, f32[3,136,128]{2,1,0:T(8,128)}, u32[]{:S(2)}) copy-start(f32[3,136,128]{2,1,0:T(8,128)} %get-tuple-element.21) | copy-start | bytes 626692
  268.4 20.5 %all-to-all-start.4 = ((f32[128,8,128]{2,1,0:T(8,128)}), f32[128,8,128]{2,1,0:T(8,128)S(1)}, u32[]{:S(2)}, u32[]{:S(2)}) async-start(f32[128,8,128]{2,1,0:T(8,128)} %broadcast_in_dim.11), calls=%async_computation.4 | async-start | bytes 1048576 | tf_op jit(solution)/shard_map/all_to_all | solution.py:445

commit v3 on v2

--- a/solution.py
+++ b/solution.py
@@ -6,6 +6,7 @@
 from jax.experimental import pallas as pl
 from jax.experimental.pallas import tpu as pltpu
 from jax.sharding import PartitionSpec as P
+
 
 FEAT = 32
 VOX = 512
@@ -14,6 +15,7 @@
 RAY_LEN = 32
 GROUP = 8
 GRAD_ROWS = 1024
+VMEM_LIMIT = 60 << 20
 
 AXES = ("view", "space")
 step_len = 0.05
@@ -128,14 +130,12 @@
     b_hid_ref,
     w_out_ref,
     carried_ref,
-    _,
     grads_hbm,
     color_ref,
     sums_ref,
     weights_buf,
     bricks_buf,
     grads_buf,
-    rays_buf,
     raw_buf,
     d_raw_buf,
     step_buf,
@@ -181,7 +181,7 @@
             ).wait()
 
     def place(owner):
-        return grads_hbm.at[owner, pl.ds(which * BLOCK, BLOCK)]
+        return grads_hbm.at[owner, pl.ds(0, BLOCK)]
 
     def send(step, side):
         for k in range(GROUP):
@@ -219,11 +219,6 @@
     b_two_col[...] = jnp.broadcast_to(b_hid_ref[...], (BLOCK, WIDTH)).T
     for at, matrix in enumerate(lane_matrices()):
         lanes_buf[at] = matrix
-    ray = lax.broadcasted_iota(jnp.int32, (BLOCK // RAY_LEN, BLOCK), 0)
-    lane = lax.broadcasted_iota(jnp.int32, (BLOCK // RAY_LEN, BLOCK), 1)
-    repeat = (lane // RAY_LEN == ray).astype(F32)
-    for c in range(4):
-        rays_buf[c] = lane_sums(rays_ref[c], repeat)
 
     def one_step(step, state):
         side = step % 2
@@ -237,8 +232,8 @@
             at = step * GROUP + k
             block = lists_ref[which, 1 + at]
             for c in range(3):
-                step_buf[c, pl.ds(k, 1), :] = rays_buf[c, pl.ds(block, 1), :]
-            used = jnp.where(at < total, rays_buf[3, pl.ds(block, 1), :], 0.0)
+                step_buf[c, pl.ds(k, 1), :] = rays_ref[c, pl.ds(block, 1), :]
+            used = jnp.where(at < total, rays_ref[3, pl.ds(block, 1), :], 0.0)
             step_buf[3, pl.ds(k, 1), :] = used
         position = lax.broadcasted_iota(jnp.int32, (GROUP, BLOCK), 1) % RAY_LEN
         live = (position.astype(F32) < step_buf[3]).astype(F32)
@@ -327,7 +322,7 @@
         parts_buf[:, 0:8, :] = high
         parts_buf[:, 8:16, :] = (sums - high.astype(F32)).astype(BF16)
         copy = pltpu.make_async_copy(
-            parts_buf, grads_hbm.at[:, pl.ds(2 * BLOCK, 16)], parts_sem
+            parts_buf, grads_hbm.at[:, pl.ds(BLOCK, 16)], parts_sem
         )
         copy.start()
         copy.wait()
@@ -336,7 +331,27 @@
     settle(steps - 1, (steps + 1) % 2)
 
 
-def run_blocks(first, lists, owners, weights, bricks, rays, params, carried, grads):
+def expand_kernel(rays_ref, out_ref):
+    ray = lax.broadcasted_iota(jnp.int32, (BLOCK // RAY_LEN, BLOCK), 0)
+    lane = lax.broadcasted_iota(jnp.int32, (BLOCK // RAY_LEN, BLOCK), 1)
+    repeat = (lane // RAY_LEN == ray).astype(F32)
+    for c in range(4):
+        out_ref[c] = lane_sums(rays_ref[c], repeat)
+
+
+def expand(rays):
+    channels, blocks, _ = rays.shape
+    return pl.pallas_call(
+        expand_kernel,
+        out_shape=jax.ShapeDtypeStruct((channels, blocks, BLOCK), F32),
+        in_specs=[pl.BlockSpec(memory_space=pltpu.VMEM)],
+        out_specs=pl.BlockSpec(memory_space=pltpu.VMEM),
+        cost_estimate=pl.CostEstimate(flops=1_000_000, bytes_accessed=300_000, transcendentals=0),
+        name="expand",
+    )(rays)
+
+
+def run_blocks(first, lists, owners, weights, bricks, rays, params, carried):
     vmem = pl.BlockSpec(memory_space=pltpu.VMEM)
     smem = pl.BlockSpec(memory_space=pltpu.SMEM)
     hbm = pl.BlockSpec(memory_space=pl.ANY)
@@ -348,17 +363,16 @@
     return pl.pallas_call(
         functools.partial(step_kernel, first),
         out_shape=(
-            jax.ShapeDtypeStruct((bricks.shape[0], 2 * BLOCK + 16, BLOCK), BF16),
+            jax.ShapeDtypeStruct((bricks.shape[0], BLOCK + (0 if first else 16), BLOCK), BF16),
             jax.ShapeDtypeStruct((3, BLOCK + 8, BLOCK), F32),
             jax.ShapeDtypeStruct((GRAD_ROWS, BLOCK), F32),
         ),
-        in_specs=[smem, smem, smem, hbm, hbm] + [vmem] * 7 + [hbm],
+        in_specs=[smem, smem, smem, hbm, hbm] + [vmem] * 7,
         out_specs=(hbm, vmem, vmem),
         scratch_shapes=[
             pltpu.VMEM((2, GROUP, BLOCK, VOX), BF16),
             pltpu.VMEM((2, GROUP, FEAT, VOX), BF16),
             pltpu.VMEM((2, GROUP, BLOCK, BLOCK), BF16),
-            pltpu.VMEM((4, BLOCK, BLOCK), F32),
             pltpu.VMEM((4, GROUP, BLOCK), F32),
             pltpu.VMEM((8, GROUP * BLOCK), F32),
             pltpu.VMEM((4, GROUP, BLOCK), F32),
@@ -380,8 +394,7 @@
             pltpu.SemaphoreType.DMA((2, GROUP)),
             pltpu.SemaphoreType.DMA,
         ],
-        compiler_params=pltpu.CompilerParams(vmem_limit_bytes=60 << 20),
-        input_output_aliases={} if first else {12: 0},
+        compiler_params=pltpu.CompilerParams(vmem_limit_bytes=VMEM_LIMIT),
         cost_estimate=cost,
         name="blocks_first" if first else "blocks_second",
     )(
@@ -397,48 +410,55 @@
         b_hid[None],
         w_out,
         carried,
-        grads,
-    )
-
-
-TAKE = 8
-
-
-def collect_kernel(ids_ref, grads_ref, out_ref):
+    )
+
+
+TAKE = 16
+
+
+def collect_kernel(first, ids_ref, grads_ref, carried_ref, out_ref):
     step = pl.program_id(0)
 
     @pl.when(step == 0)
     def _():
-        out_ref[...] = jnp.zeros_like(out_ref)
+        if first:
+            out_ref[...] = jnp.zeros_like(out_ref)
+        else:
+            out_ref[...] = carried_ref[...]
 
     for k in range(TAKE):
-        for r in range(2):
-            brick = ids_ref[2 * (step * TAKE + k) + r]
-
-            @pl.when(brick >= 0)
-            def _():
-                for v in range(VOX // BLOCK):
-                    rows = pl.ds(r * BLOCK + v * FEAT, FEAT)
-                    out_ref[brick, :, v * BLOCK : (v + 1) * BLOCK] += grads_ref[k, rows].astype(F32)
-
-
-def collect(ids, grads, own):
+        brick = ids_ref[step * TAKE + k]
+
+        @pl.when(brick >= 0)
+        def _():
+            for v in range(VOX // BLOCK):
+                rows = grads_ref[k, v * FEAT : (v + 1) * FEAT].astype(F32)
+                out_ref[brick, :, v * BLOCK : (v + 1) * BLOCK] += rows
+
+
+def collect(ids, grads, own, carried):
     amount, rows, _ = grads.shape
+    first = carried is None
+    if first:
+        carried = jnp.zeros((8, BLOCK), F32)
+        held = pl.BlockSpec((8, BLOCK), lambda i, ids: (0, 0))
+    else:
+        held = pl.BlockSpec((own, FEAT, VOX), lambda i, ids: (0, 0, 0), pipeline_mode=pl.Buffered(1))
     return pl.pallas_call(
-        collect_kernel,
+        functools.partial(collect_kernel, first),
         out_shape=jax.ShapeDtypeStruct((own, FEAT, VOX), F32),
         grid_spec=pltpu.PrefetchScalarGridSpec(
             num_scalar_prefetch=1,
             grid=(amount // TAKE,),
-            in_specs=[pl.BlockSpec((TAKE, rows, BLOCK), lambda i, ids: (i, 0, 0))],
+            in_specs=[pl.BlockSpec((TAKE, rows, BLOCK), lambda i, ids: (i, 0, 0)), held],
             out_specs=pl.BlockSpec((own, FEAT, VOX), lambda i, ids: (0, 0, 0)),
         ),
-        compiler_params=pltpu.CompilerParams(vmem_limit_bytes=60 << 20),
+        compiler_params=pltpu.CompilerParams(vmem_limit_bytes=VMEM_LIMIT),
         cost_estimate=pl.CostEstimate(
             flops=amount * FEAT * VOX, bytes_accessed=amount * FEAT * VOX * 4, transcendentals=0
         ),
-        name="collect",
-    )(ids, grads)
+        name="collect_first" if first else "collect_second",
+    )(ids, grads, carried)
 
 
 def exchange(values):
@@ -470,21 +490,24 @@
     fetched = [exchange(bricks_t[jnp.maximum(asked[:, r], 0)]) for r in range(2)]
 
     rays = jnp.concatenate([target, sample_count.astype(F32)[None]])
-    rays = rays.reshape(4, own_blocks, BLOCK // RAY_LEN)
+    rays = expand(rays.reshape(4, own_blocks, BLOCK // RAY_LEN))
     params = (w_in, b_in, w_hid, b_hid, w_out, b_out)
     nothing = jnp.zeros((8, BLOCK), F32)
-    grads, color_0, sums = run_blocks(
-        True, lists, owners, interp_weights, fetched[0], rays, params, nothing, nothing
-    )
-    grads, color_1, _ = run_blocks(
-        False, lists, owners, interp_weights, fetched[1], rays, params, sums, grads
-    )
-    returned = exchange(grads)
-
-    parts = returned[:, 2 * BLOCK :].astype(F32)
+    grads_0, color_0, sums = run_blocks(
+        True, lists, owners, interp_weights, fetched[0], rays, params, nothing
+    )
+    grads_1, color_1, _ = run_blocks(
+        False, lists, owners, interp_weights, fetched[1], rays, params, sums
+    )
+    returned_0 = exchange(grads_0)
+    returned_1 = exchange(grads_1)
+    partial = collect(asked[:, 0], returned_0, own_bricks, None)
+
+    parts = returned_1[:, BLOCK:].astype(F32)
     mine = jnp.sum(parts[:, :8] + parts[:, 8:], axis=0)
     totals = exchange(jnp.broadcast_to(mine[None], (dev_count, 8, BLOCK)))
-    brick_grad = jnp.swapaxes(collect(asked.reshape(-1), returned, own_bricks), 1, 2)
+    brick_grad = collect(asked[:, 1], returned_1, own_bricks, partial)
+    brick_grad = jnp.swapaxes(brick_grad, 1, 2)
 
     totals = totals.reshape(GRAD_ROWS, BLOCK) / (sample_count.shape[0] * dev_count)
 

time: 293 us -> 307 us (1.048)
  waiting for transfers between devices: 50.8 us -> 98.4 us
  blocking collectives: 132 us -> 90 us
  starting transfers between devices: 14.8 us -> 21 us
  Pallas kernels: 74.4 us -> 80.5 us
  local copies, waits for them, and re-layouts: 14.3 us -> 9.47 us
    all_to_all x3 -> x4, waiting for transfers between devices: 50.8 us -> 98.4 us  [exchange(): return lax.all_to_all(values, AXES, split_axis=0, concat_axis=0, tiled=True)]
    all_to_all x2, blocking collectives: 132 us -> 90 us  [exchange(): return lax.all_to_all(values, AXES, split_axis=0, concat_axis=0, tiled=True)]
    all_to_all x3 -> x4, starting transfers between devices: 14.8 us -> 21 us  [exchange(): return lax.all_to_all(values, AXES, split_axis=0, concat_axis=0, tiled=True)]
    pallas_call x1 -> x3, Pallas kernels: 13.1 us -> 19.3 us  [the longest x2 17.3 us: collect(): pl.pallas_call(functools.partial(collect_kernel, first), out_shape=jax.Sh...]
    unnamed x15 -> x12, local copies, waits for them, and re-layouts: 3.53 us -> 0.03 us
  transfers between devices with their start and end apart: 3 -> 4, of which waited for: 2 -> 2; matrix products, arithmetic and copies ran while one was open for 2% -> 2% of each run, Pallas kernels for 21% -> 22%
where the time goes in v3:
time: 307 us; the launch traced here: 306 us
  waiting for transfers between devices  98.4 us (32%)
  blocking collectives  90 us (29%)
  Pallas kernels  80.5 us (26%)
  starting transfers between devices  21 us (7%)
  local copies, waits for them, and re-layouts  9.47 us (3%)
  other arithmetic  5.97 us (2%)
    all_to_all x4, waiting for transfers between devices, exchange(): return lax.all_to_all(values, AXES, split_axis=0, concat_axis=0, tiled=True)  98.4 us
    all_to_all x2, blocking collectives, exchange(): return lax.all_to_all(values, AXES, split_axis=0, concat_axis=0, tiled=True)  90 us
    pallas_call x2, Pallas kernels, run_blocks(): pl.pallas_call(functools.partial(step_kernel, first), out_shape=(jax.Shap...  58.5 us
    all_to_all x4, starting transfers between devices, exchange(): return lax.all_to_all(values, AXES, split_axis=0, concat_axis=0, tiled=True)  21 us
    pallas_call x2, Pallas kernels, collect(): pl.pallas_call(functools.partial(collect_kernel, first), out_shape=jax.Sh...  17.3 us
  transfers between devices with their start and end apart: 4, of which 2 were waited for; matrix products, arithmetic and copies ran while one was open for 2% of the time, Pallas kernels for 22%

profile of v3, /device:TPU:1, one launch (start us, length us, event | category | flops | bytes accessed | tf_op | source)
XLA Modules:
  0.0 306.3 jit_solution(7030552777428296144)
XLA Ops:
  0.6 0.0 copy-start
  0.6 2.7 plan.1
  3.4 0.8 reshape.43
  4.2 21.1 %all_to_all.30 = s32[128,1,2]{2,1,0:T(1,128)S(1)} all-to-all(s32[128,1,2]{2,1,0:T(1,128)S(1)} %bitcast.36), channel_id=1, replica_groups=mesh['view'=8,'space'=16] {'view','space'}, dimensions={0} | all-to-all | bytes 2048 | tf_op jit(solution)/shard_map/all_to_all | solution.py:465
  25.3 0.7 slice_reduce_fusion
  26.0 0.0 copy-done
  26.0 2.7 gather_fusion.1
  28.7 5.3 %all-to-all-start.2 = ((bf16[128,32,512]{2,1,0:T(8,128)(2,1)}), bf16[128,32,512]{2,1,0:T(8,128)(2,1)}, u32[]{:S(2)}, u32[]{:S(2)}) async-start(bf16[128,32,512]{2,1,0:T(8,128)(2,1)} %gather_fusion.1), calls=%async_computation.2 | async-start | bytes 8388608 | tf_op jit(solution)/shard_map/all_to_all | solution.py:465
  34.1 2.8 gather_fusion
  36.9 0.0 copy-start.5
  36.9 0.0 copy-start.4
  36.9 48.4 %all-to-all-done.2.bricks_hbm = bf16[128,32,512]{2,1,0:T(8,128)(2,1)} async-done(((bf16[128,32,512]{2,1,0:T(8,128)(2,1)}), bf16[128,32,512]{2,1,0:T(8,128)(2,1)}, u32[]{:S(2)}, u32[]{:S(2)}) %all-to-all-start.2) | async-done | bytes 4194336 | tf_op jit(solution)/shard_map/all_to_all | solution.py:465
  85.3 5.5 %all-to-all-start.1 = ((bf16[128,32,512]{2,1,0:T(8,128)(2,1)}), bf16[128,32,512]{2,1,0:T(8,128)(2,1)}, u32[]{:S(2)}, u32[]{:S(2)}) async-start(bf16[128,32,512]{2,1,0:T(8,128)(2,1)} %gather_fusion), calls=%async_computation.1 | async-start | bytes 8388608 | tf_op jit(solution)/shard_map/all_to_all | solution.py:465
  90.9 0.0 copy-done.5
  90.9 0.1 concatenate.24
  91.0 0.0 copy-done.4
  91.0 0.2 concatenate.23
  91.2 0.7 pad_maximum_fusion.rays_ref
  92.0 2.0 expand.1.rays_ref
  94.0 0.6 broadcast_3_carried_ref.2.carried_ref
  94.6 47.7 %blocks_first.1 = (bf16[128,128,128]{2,1,0:T(8,128)(2,1)}, f32[3,136,128]{2,1,0:T(8,128)}, f32[1024,128]{1,0:T(8,128)}) custom-call(s32[2,144]{1,0:T(2,128)} %get-tuple-element.16.lists_ref, s32[128]{0:T(128)} %bitcast.44, f32[4]{0:T(128)} %b_out_ref.3, bf16[128,128,512]{2,1,0:T(8,128)(2,1)} %weights_hbm.3, bf16[128,32,512]{2,1,0:T(8,128)(2,1)} %all-to-all-done.2.bricks_hbm, ...), custom_call_target="tpu_custom_call" | custom-call | flops 8960000000 | bytes 25600000 | tf_op jit(solution)/shard_map/blocks_first/pallas_call | solution.py:363
  142.2 0.0 all-to-all-done.1.bricks_hbm
  142.2 10.9 %blocks_second.1 = (bf16[128,144,128]{2,1,0:T(8,128)(2,1)}, f32[3,136,128]{2,1,0:T(8,128)}, f32[1024,128]{1,0:T(8,128)}) custom-call(s32[2,144]{1,0:T(2,128)} %get-tuple-element.16.lists_ref, s32[128]{0:T(128)} %bitcast.45, f32[4]{0:T(128)} %b_out_ref.3, bf16[128,128,512]{2,1,0:T(8,128)(2,1)} %weights_hbm.3, ...), custom_call_target="tpu_custom_call" | custom-call | flops 1120000000 | bytes 3200000 | tf_op jit(solution)/shard_map/blocks_second/pallas_call | solution.py:363
  153.1 68.9 %all_to_all.31.grads_ref = bf16[128,144,128]{2,1,0:T(8,128)(2,1)} all-to-all(bf16[128,144,128]{2,1,0:T(8,128)(2,1)} %get-tuple-element.18), channel_id=1, replica_groups=mesh['view'=8,'space'=16] {'view','space'}, dimensions={0} | all-to-all | bytes 9437184 | tf_op jit(solution)/shard_map/all_to_all | solution.py:465
  222.1 5.1 %all-to-all-start.4 = ((bf16[128,128,128]{2,1,0:T(8,128)(2,1)}), bf16[128,128,128]{2,1,0:T(8,128)(2,1)}, u32[]{:S(2)}, u32[]{:S(2)}) async-start(bf16[128,128,128]{2,1,0:T(8,128)(2,1)} %get-tuple-element.19), calls=%async_computation.4 | async-start | bytes 8388608 | tf_op jit(solution)/shard_map/all_to_all | solution.py:465
  227.2 0.0 copy-start.2
  227.2 0.0 copy-start.3
  227.2 1.2 slice_convert_fusion
  228.4 0.1 fusion
  228.5 49.9 %all-to-all-done.4.grads_ref = bf16[128,128,128]{2,1,0:T(8,128)(2,1)} async-done(((bf16[128,128,128]{2,1,0:T(8,128)(2,1)}), bf16[128,128,128]{2,1,0:T(8,128)(2,1)}, u32[]{:S(2)}, u32[]{:S(2)}) %all-to-all-start.4) | async-done | bytes 4194336 | tf_op jit(solution)/shard_map/all_to_all | solution.py:465
  278.5 0.8 broadcast_in_dim.8
  279.3 5.1 %all-to-all-start.5 = ((f32[128,8,128]{2,1,0:T(8,128)}), f32[128,8,128]{2,1,0:T(8,128)S(1)}, u32[]{:S(2)}, u32[]{:S(2)}) async-start(f32[128,8,128]{2,1,0:T(8,128)} %broadcast_in_dim.8), calls=%async_computation.5 | async-start | bytes 1048576 | tf_op jit(solution)/shard_map/all_to_all | solution.py:465
  284.4 0.0 copy-done.2
  284.4 0.0 copy-done.3
  284.5 0.5 slice.94
  285.0 0.7 reshape.45
  285.7 8.2 %collect_first.1.carried_ref = f32[64,32,512]{2,1,0:T(8,128)} custom-call(s32[128]{0:T(128)} %get-tuple-element.22.ids_ref, bf16[128,128,128]{2,1,0:T(8,128)(2,1)} %all-to-all-done.4.grads_ref, f32[8,128]{1,0:T(8,128)} %broadcast_3_carried_ref.2.carried_ref), custom_call_target="tpu_custom_call" | custom-call | flops 2097152 | bytes 8388608 | tf_op jit(solution)/shard_map/collect_first/pallas_call | solution.py:447
  293.9 0.0 copy-start.1
  293.9 9.1 %collect_second.1 = f32[64,32,512]{2,1,0:T(8,128)} custom-call(s32[128]{0:T(128)} %get-tuple-element.25.ids_ref, bf16[128,144,128]{2,1,0:T(8,128)(2,1)} %all_to_all.31.grads_ref, f32[64,32,512]{2,1,0:T(8,128)} %collect_first.1.carried_ref), custom_call_target="tpu_custom_call" | custom-call | flops 2097152 | bytes 8388608 | tf_op jit(solution)/shard_map/collect_second/pallas_call | solution.py:447
  303.0 0.0 all-to-all-done.5
  303.0 0.1 fusion.1
  303.2 0.6 slice_reduce_fusion.2
  303.8 0.6 pad_maximum_fusion.3
  304.4 0.7 pad_maximum_fusion.1
  305.1 0.6 pad_maximum_fusion.2
  305.7 0.6 pad_maximum_fusion.4
  306.3 0.0 copy-done.1
  (7 shorter events, 0.1 us)
Async XLA Ops:
  0.6 25.3 %copy-start = (bf16[64,512,32]{1,2,0:T(8,128)(2,1)S(1)}, bf16[64,512,32]{1,2,0:T(8,128)(2,1)}, u32[]{:S(2)}) copy-start(bf16[64,512,32]{1,2,0:T(8,128)(2,1)} %param.12) | copy-start | bytes 6291460
  28.7 56.6 %all-to-all-start.2 = ((bf16[128,32,512]{2,1,0:T(8,128)(2,1)}), bf16[128,32,512]{2,1,0:T(8,128)(2,1)}, u32[]{:S(2)}, u32[]{:S(2)}) async-start(bf16[128,32,512]{2,1,0:T(8,128)(2,1)} %gather_fusion.1), calls=%async_computation.2 | async-start | bytes 8388608 | tf_op jit(solution)/shard_map/all_to_all | solution.py:465
  36.9 54.0 %copy-start.5 = (s32[512]{0:T(512)S(1)}, s32[512]{0:T(512)}, u32[]{:S(2)}) copy-start(s32[512]{0:T(512)} %param.16) | copy-start | bytes 6148
  36.9 54.1 %copy-start.4 = (f32[3,512]{1,0:T(4,128)S(1)}, f32[3,512]{1,0:T(4,128)}, u32[]{:S(2)}) copy-start(f32[3,512]{1,0:T(4,128)} %param.17) | copy-start | bytes 18436
  85.3 56.9 %all-to-all-start.1 = ((bf16[128,32,512]{2,1,0:T(8,128)(2,1)}), bf16[128,32,512]{2,1,0:T(8,128)(2,1)}, u32[]{:S(2)}, u32[]{:S(2)}) async-start(bf16[128,32,512]{2,1,0:T(8,128)(2,1)} %gather_fusion), calls=%async_computation.1 | async-start | bytes 8388608 | tf_op jit(solution)/shard_map/all_to_all | solution.py:465
  222.1 56.4 %all-to-all-start.4 = ((bf16[128,128,128]{2,1,0:T(8,128)(2,1)}), bf16[128,128,128]{2,1,0:T(8,128)(2,1)}, u32[]{:S(2)}, u32[]{:S(2)}) async-start(bf16[128,128,128]{2,1,0:T(8,128)(2,1)} %get-tuple-element.19), calls=%async_computation.4 | async-start | bytes 8388608 | tf_op jit(solution)/shard_map/all_to_all | solution.py:465
  227.2 57.2 %copy-start.2 = (f32[3,136,128]{2,1,0:T(8,128)S(1)}, f32[3,136,128]{2,1,0:T(8,128)}, u32[]{:S(2)}) copy-start(f32[3,136,128]{2,1,0:T(8,128)} %get-tuple-element.20) | copy-start | bytes 626692
  227.2 57.2 %copy-start.3 = (f32[3,136,128]{2,1,0:T(8,128)S(1)}, f32[3,136,128]{2,1,0:T(8,128)}, u32[]{:S(2)}) copy-start(f32[3,136,128]{2,1,0:T(8,128)} %get-tuple-element.21) | copy-start | bytes 626692
  279.3 23.7 %all-to-all-start.5 = ((f32[128,8,128]{2,1,0:T(8,128)}), f32[128,8,128]{2,1,0:T(8,128)S(1)}, u32[]{:S(2)}, u32[]{:S(2)}) async-start(f32[128,8,128]{2,1,0:T(8,128)} %broadcast_in_dim.8), calls=%async_computation.5 | async-start | bytes 1048576 | tf_op jit(solution)/shard_map/all_to_all | solution.py:465
  293.9 12.4 %copy-start.1 = (bf16[64,512,32]{1,2,0:T(8,128)(2,1)S(1)}, bf16[64,512,32]{1,2,0:T(8,128)(2,1)}, u32[]{:S(2)}) copy-start(bf16[64,512,32]{1,2,0:T(8,128)(2,1)} %param.12) | copy-start | bytes 6291460

commit v4 on v3

--- a/solution.py
+++ b/solution.py
@@ -13,9 +13,9 @@
 WIDTH = 256
 BLOCK = 128
 RAY_LEN = 32
-GROUP = 8
+GROUP = 16
 GRAD_ROWS = 1024
-VMEM_LIMIT = 60 << 20
+VMEM_LIMIT = 66_000_000
 
 AXES = ("view", "space")
 step_len = 0.05
@@ -79,18 +79,20 @@
 def plan_kernel(owner_ref, brick_ref, wish_ref, lists_ref):
     amount = owner_ref.shape[0]
 
+    half = wish_ref.shape[0] // 2
+
     def clear(i, state):
-        wish_ref[2 * i] = -1
-        wish_ref[2 * i + 1] = -1
+        wish_ref[i] = -1
+        wish_ref[half + i] = -1
         return state
 
-    lax.fori_loop(0, wish_ref.shape[0] // 2, clear, 0, unroll=8)
+    lax.fori_loop(0, half, clear, 0, unroll=8)
 
     def place(i, state):
         firsts, seconds = state
         owner = owner_ref[i]
-        rank = jnp.where(wish_ref[2 * owner] >= 0, 1, 0)
-        wish_ref[2 * owner + rank] = brick_ref[i]
+        rank = jnp.where(wish_ref[owner] >= 0, 1, 0)
+        wish_ref[half * rank + owner] = brick_ref[i]
         lists_ref[0, 1 + firsts] = i
         lists_ref[1, 1 + seconds] = i
         return firsts + 1 - rank, seconds + rank
@@ -118,6 +120,7 @@
 
 def step_kernel(
     first,
+    stride,
     lists_ref,
     owner_ref,
     b_out_ref,
@@ -158,7 +161,15 @@
     parts_sem,
 ):
     which = 0 if first else 1
+    parts = 1 if stride is None else 2
+    feats_each, rows_each = FEAT // parts, BLOCK // parts
     total = lists_ref[which, 0]
+
+    def mate(owner, part):
+        if stride is None:
+            return owner
+        return owner + (part - owner // stride % 2) * stride
+
     steps = (total + GROUP - 1) // GROUP
 
     def fetch(step, side):
@@ -167,21 +178,32 @@
             pltpu.make_async_copy(
                 weights_hbm.at[block], weights_buf.at[side, k], weights_sem.at[side, k]
             ).start()
-            pltpu.make_async_copy(
-                bricks_hbm.at[owner_ref[block]], bricks_buf.at[side, k], bricks_sem.at[side, k]
-            ).start()
+            owner = owner_ref[block]
+            for part in range(parts):
+                pltpu.make_async_copy(
+                    bricks_hbm.at[mate(owner, part)],
+                    bricks_buf.at[side, k, pl.ds(part * feats_each, feats_each)],
+                    bricks_sem.at[side, k, part],
+                ).start()
 
     def arrive(side):
         for k in range(GROUP):
             pltpu.make_async_copy(
                 weights_hbm.at[0], weights_buf.at[side, k], weights_sem.at[side, k]
             ).wait()
-            pltpu.make_async_copy(
-                bricks_hbm.at[0], bricks_buf.at[side, k], bricks_sem.at[side, k]
-            ).wait()
-
-    def place(owner):
-        return grads_hbm.at[owner, pl.ds(0, BLOCK)]
+            for part in range(parts):
+                pltpu.make_async_copy(
+                    bricks_hbm.at[0],
+                    bricks_buf.at[side, k, pl.ds(part * feats_each, feats_each)],
+                    bricks_sem.at[side, k, part],
+                ).wait()
+
+    def leave(side, k, part, owner):
+        return pltpu.make_async_copy(
+            grads_buf.at[side, k, pl.ds(part * rows_each, rows_each)],
+            grads_hbm.at[mate(owner, part), pl.ds(0, rows_each)],
+            grads_sem.at[side, k, part],
+        )
 
     def send(step, side):
         for k in range(GROUP):
@@ -190,9 +212,8 @@
             @pl.when(at < total)
             def _():
                 owner = owner_ref[lists_ref[which, 1 + at]]
-                pltpu.make_async_copy(
-                    grads_buf.at[side, k], place(owner), grads_sem.at[side, k]
-                ).start()
+                for part in range(parts):
+                    leave(side, k, part, owner).start()
 
     def settle(step, side):
         for k in range(GROUP):
@@ -200,9 +221,8 @@
 
             @pl.when((step >= 0) & (at < total))
             def _():
-                pltpu.make_async_copy(
-                    grads_buf.at[side, k], place(0), grads_sem.at[side, k]
-                ).wait()
+                for part in range(parts):
+                    leave(side, k, part, 0).wait()
 
     @pl.when(steps > 0)
     def _():
@@ -286,8 +306,13 @@
         for k in range(GROUP):
             grad = dot_nn(d_feats[:, k * BLOCK : (k + 1) * BLOCK], weights_buf[side, k])
             grad = grad.astype(BF16)
-            for v in range(VOX // BLOCK):
-                grads_buf[side, k, v * FEAT : (v + 1) * FEAT] = grad[:, v * BLOCK : (v + 1) * BLOCK]
+            for part in range(parts):
+                feat = part * feats_each
+                for v in range(VOX // BLOCK):
+                    row = part * rows_each + v * feats_each
+                    grads_buf[side, k, row : row + feats_each] = grad[
+                        feat : feat + feats_each, v * BLOCK : (v + 1) * BLOCK
+                    ]
         send(step, side)
         return state
 
@@ -322,7 +347,7 @@
         parts_buf[:, 0:8, :] = high
         parts_buf[:, 8:16, :] = (sums - high.astype(F32)).astype(BF16)
         copy = pltpu.make_async_copy(
-            parts_buf, grads_hbm.at[:, pl.ds(BLOCK, 16)], parts_sem
+            parts_buf, grads_hbm.at[:, pl.ds(rows_each, 16)], parts_sem
         )
         copy.start()
         copy.wait()
@@ -351,19 +376,21 @@
     )(rays)
 
 
-def run_blocks(first, lists, owners, weights, bricks, rays, params, carried):
+def run_blocks(first, lists, owners, weights, bricks, rays, params, carried, stride=None):
     vmem = pl.BlockSpec(memory_space=pltpu.VMEM)
     smem = pl.BlockSpec(memory_space=pltpu.SMEM)
     hbm = pl.BlockSpec(memory_space=pl.ANY)
     w_in, b_in, w_hid, b_hid, w_out, b_out = params
     amount = weights.shape[0] if first else weights.shape[0] // 8
+    parts = 1 if stride is None else 2
+    rows = BLOCK // parts + (0 if first else 16)
     cost = pl.CostEstimate(
         flops=amount * 70_000_000, bytes_accessed=amount * 200_000, transcendentals=amount * 1000
     )
     return pl.pallas_call(
-        functools.partial(step_kernel, first),
+        functools.partial(step_kernel, first, stride),
         out_shape=(
-            jax.ShapeDtypeStruct((bricks.shape[0], BLOCK + (0 if first else 16), BLOCK), BF16),
+            jax.ShapeDtypeStruct((bricks.shape[0], rows, BLOCK), BF16),
             jax.ShapeDtypeStruct((3, BLOCK + 8, BLOCK), F32),
             jax.ShapeDtypeStruct((GRAD_ROWS, BLOCK), F32),
         ),
@@ -390,13 +417,12 @@
             pltpu.VMEM((4, GROUP, BLOCK), F32),
             pltpu.VMEM((GRAD_ROWS // 8, 16, BLOCK), BF16),
             pltpu.SemaphoreType.DMA((2, GROUP)),
-            pltpu.SemaphoreType.DMA((2, GROUP)),
-            pltpu.SemaphoreType.DMA((2, GROUP)),
+            pltpu.SemaphoreType.DMA((2, GROUP, parts)),
+            pltpu.SemaphoreType.DMA((2, GROUP, parts)),
             pltpu.SemaphoreType.DMA,
         ],
         compiler_params=pltpu.CompilerParams(vmem_limit_bytes=VMEM_LIMIT),
         cost_estimate=cost,
-        name="blocks_first" if first else "blocks_second",
     )(
         lists,
         owners,
@@ -459,6 +485,91 @@
         ),
         name="collect_first" if first else "collect_second",
     )(ids, grads, carried)
+
+
+def collect_halves_kernel(ids_ref, grads_ref, carried_ref, out_ref, mate_ref):
+    step = pl.program_id(0)
+    own = out_ref.shape[0]
+    half = FEAT // 2
+    feat = pl.multiple_of(ids_ref[ids_ref.shape[0] - 1] * half, half)
+
+    @pl.when(step == 0)
+    def _():
+        out_ref[...] = carried_ref[...]
+        mate_ref[...] = jnp.zeros_like(mate_ref)
+
+    for k in range(TAKE):
+        brick = ids_ref[step * TAKE + k]
+
+        @pl.when((brick >= 0) & (brick < own))
+        def _():
+            for v in range(VOX // BLOCK):
+                rows = grads_ref[k, v * half : (v + 1) * half].astype(F32)
+                out_ref[brick, pl.ds(feat, half), v * BLOCK : (v + 1) * BLOCK] += rows
+
+        @pl.when(brick >= own)
+        def _():
+            for v in range(VOX // BLOCK):
+                rows = grads_ref[k, v * half : (v + 1) * half].astype(F32)
+                mate_ref[brick - own, :, v * BLOCK : (v + 1) * BLOCK] += rows
+
+
+def collect_halves(ids, grads, own, carried):
+    amount, rows, _ = grads.shape
+    half = FEAT // 2
+    return pl.pallas_call(
+        collect_halves_kernel,
+        out_shape=(
+            jax.ShapeDtypeStruct((own, FEAT, VOX), F32),
+            jax.ShapeDtypeStruct((own, half, VOX), F32),
+        ),
+        grid_spec=pltpu.PrefetchScalarGridSpec(
+            num_scalar_prefetch=1,
+            grid=(amount // TAKE,),
+            in_specs=[
+                pl.BlockSpec((TAKE, rows, BLOCK), lambda i, ids: (i, 0, 0)),
+                pl.BlockSpec(
+                    (own, FEAT, VOX), lambda i, ids: (0, 0, 0), pipeline_mode=pl.Buffered(1)
+                ),
+            ],
+            out_specs=(
+                pl.BlockSpec((own, FEAT, VOX), lambda i, ids: (0, 0, 0)),
+                pl.BlockSpec((own, half, VOX), lambda i, ids: (0, 0, 0)),
+            ),
+        ),
+        compiler_params=pltpu.CompilerParams(vmem_limit_bytes=VMEM_LIMIT),
+        cost_estimate=pl.CostEstimate(
+            flops=amount * FEAT * VOX, bytes_accessed=amount * FEAT * VOX * 4, transcendentals=0
+        ),
+        name="collect_halves",
+    )(ids, grads, carried)
+
+
+MERGE = 16
+
+
+def merge_kernel(core_ref, sums_ref, arrived_ref, out_ref):
+    half = FEAT // 2
+    feat = pl.multiple_of((1 - core_ref[0]) * half, half)
+    out_ref[...] = sums_ref[...]
+    out_ref[:, pl.ds(feat, half), :] += arrived_ref[...]
+
+
+def merge(core, sums, arrived):
+    own, half, _ = arrived.shape
+    whole = pl.BlockSpec((MERGE, FEAT, VOX), lambda i, core: (i, 0, 0))
+    return pl.pallas_call(
+        merge_kernel,
+        out_shape=jax.ShapeDtypeStruct(sums.shape, F32),
+        grid_spec=pltpu.PrefetchScalarGridSpec(
+            num_scalar_prefetch=1,
+            grid=(own // MERGE,),
+            in_specs=[whole, pl.BlockSpec((MERGE, half, VOX), lambda i, core: (i, 0, 0))],
+            out_specs=whole,
+        ),
+        compiler_params=pltpu.CompilerParams(vmem_limit_bytes=VMEM_LIMIT),
+        name="merge",
+    )(core, sums, arrived)
 
 
 def exchange(values):
@@ -483,30 +594,74 @@
     own_bricks = brick_feats.shape[0]
     dev_count = lax.axis_size(AXES)
     owners = block_owner[:, 0]
+    space = lax.axis_size("space")
+    me = lax.axis_index(AXES)
+    core = lax.axis_index("view") % 2
     wish, lists = plan(owners, block_brick[:, 0], dev_count)
-    asked = exchange(wish.reshape(dev_count, 1, 2)).reshape(dev_count, 2)
+    wishes = exchange(jnp.broadcast_to(wish.reshape(1, 2, dev_count), (dev_count, 2, dev_count)))
+    asked = [wishes[:, r, :] for r in range(2)]
+    mine = [lax.dynamic_index_in_dim(a, me, axis=1, keepdims=False) for a in asked]
+    other = me + (1 - 2 * core) * space
+    others = lax.dynamic_index_in_dim(asked[1], other, axis=1, keepdims=False)
+    others = jnp.where(others >= 0, others + own_bricks, -1)
+    halves = jnp.where(mine[1] >= 0, mine[1], others)
+    twice = (asked[1] >= 0).reshape(dev_count, dev_count // (2 * space), 2, space)
+    crowded = jnp.any(twice[:, :, 0] & twice[:, :, 1])
 
     bricks_t = jnp.swapaxes(brick_feats, 1, 2)
-    fetched = [exchange(bricks_t[jnp.maximum(asked[:, r], 0)]) for r in range(2)]
+    half = FEAT // 2
+    swap = [(v, v ^ 1) for v in range(lax.axis_size("view"))]
+
+    def part(which):
+        return lax.dynamic_slice_in_dim(bricks_t, which * half, half, axis=1)
+
+    chip_bricks = jnp.concatenate([part(core), lax.ppermute(part(1 - core), "view", swap)])
+    fetched_0 = exchange(bricks_t[jnp.maximum(mine[0], 0)])
+    sent_wholes = bricks_t[jnp.maximum(mine[1], 0)]
+    sent_halves = chip_bricks[jnp.maximum(halves, 0)]
+    sent_wholes, sent_halves = lax.optimization_barrier((sent_wholes, sent_halves))
 
     rays = jnp.concatenate([target, sample_count.astype(F32)[None]])
     rays = expand(rays.reshape(4, own_blocks, BLOCK // RAY_LEN))
     params = (w_in, b_in, w_hid, b_hid, w_out, b_out)
     nothing = jnp.zeros((8, BLOCK), F32)
-    grads_0, color_0, sums = run_blocks(
-        True, lists, owners, interp_weights, fetched[0], rays, params, nothing
+
+    def rest(split, fetched_0, sent_1, ids_1, core, lists, owners, weights, rays, ids_0):
+        stride = space if split else None
+        rows = BLOCK // 2 if split else BLOCK
+        fetched_1 = exchange(sent_1)
+        grads_0, color_0, sums = run_blocks(
+            True, lists, owners, weights, fetched_0, rays, params, nothing
+        )
+        grads_1, color_1, _ = run_blocks(
+            False, lists, owners, weights, fetched_1, rays, params, sums, stride
+        )
+        returned_0 = exchange(grads_0)
+        returned_1 = exchange(grads_1)
+        partial = collect(ids_0, returned_0, own_bricks, None)
+        parts = returned_1[:, rows:].astype(F32)
+        chunk = jnp.sum(parts[:, :8] + parts[:, 8:], axis=0)
+        totals = exchange(jnp.broadcast_to(chunk[None], (dev_count, 8, BLOCK)))
+        if split:
+            grad, spare = collect_halves(
+                jnp.concatenate([ids_1, core[None]]), returned_1, own_bricks, partial
+            )
+            grad = merge(core[None], grad, lax.ppermute(spare, "view", swap))
+        else:
+            grad = collect(ids_1, returned_1, own_bricks, partial)
+        color = (color_0 + color_1)[:, :own_blocks, ::RAY_LEN].reshape(3, -1)
+        return grad, color, totals
+
+    common = (lists, owners, interp_weights, rays, mine[0])
+    brick_grad, color, totals = lax.cond(
+        crowded,
+        lambda f, full, split, *c: rest(False, f, full, mine[1], core, *c),
+        lambda f, full, split, *c: rest(True, f, split, halves, core, *c),
+        fetched_0,
+        sent_wholes,
+        sent_halves,
+        *common,
     )
-    grads_1, color_1, _ = run_blocks(
-        False, lists, owners, interp_weights, fetched[1], rays, params, sums
-    )
-    returned_0 = exchange(grads_0)
-    returned_1 = exchange(grads_1)
-    partial = collect(asked[:, 0], returned_0, own_bricks, None)
-
-    parts = returned_1[:, BLOCK:].astype(F32)
-    mine = jnp.sum(parts[:, :8] + parts[:, 8:], axis=0)
-    totals = exchange(jnp.broadcast_to(mine[None], (dev_count, 8, BLOCK)))
-    brick_grad = collect(asked[:, 1], returned_1, own_bricks, partial)
     brick_grad = jnp.swapaxes(brick_grad, 1, 2)
 
     totals = totals.reshape(GRAD_ROWS, BLOCK) / (sample_count.shape[0] * dev_count)
@@ -520,7 +675,6 @@
     g_b_hid = joined(592, 8)[0]
     g_b_in = joined(608, 8)[0]
     g_b_out = jnp.sum(totals[624:628], axis=1)
-    color = (color_0 + color_1)[:, :own_blocks, ::RAY_LEN].reshape(3, -1)
     return (brick_grad, color, g_w_in, g_b_in, g_w_hid, g_b_hid, g_w_out, g_b_out)
 
 

time: 307 us -> 274 us (0.89)
  blocking collectives: 90 us -> 0 us
  starting transfers between devices: 21 us -> 45 us
  waiting for transfers between devices: 98.4 us -> 121 us
  local copies, waits for them, and re-layouts: 9.47 us -> 16 us
  other arithmetic: 5.97 us -> 10.6 us
    all_to_all x2 -> x0, blocking collectives: 90 us -> none  [exchange(): return lax.all_to_all(values, AXES, split_axis=0, concat_axis=0, tiled=True)]
    all_to_all x4 -> x6, waiting for transfers between devices: 98.4 us -> 121 us  [exchange(): return lax.all_to_all(values, AXES, split_axis=0, concat_axis=0, tiled=True)]
    all_to_all x4 -> x6, starting transfers between devices: 21 us -> 42.6 us  [exchange(): return lax.all_to_all(values, AXES, split_axis=0, concat_axis=0, tiled=True)]
    pallas_call x2 -> x1, Pallas kernels: 17.3 us -> 8.08 us  [collect(): pl.pallas_call(functools.partial(collect_kernel, first), out_shape=jax.Sh...]
    pallas_call x2 -> x4, Pallas kernels: 58.5 us -> 66.7 us  [the longest x2 51.9 us: run_blocks(): pl.pallas_call(functools.partial(step_kernel, first, stride), out_shape=(...]
    gather x2 -> x3, local copies, waits for them, and re-layouts: 5.57 us -> 9.44 us  [the longest x1 4.42 us: body(): fetched_0 = exchange(bricks_t[jnp.maximum(mine[0], 0)])]
  transfers between devices with their start and end apart: 4 -> 8, of which waited for: 2 -> 5; matrix products, arithmetic and copies ran while one was open for 2% -> 6% of each run, Pallas kernels for 22% -> 24%
where the time goes in v4:
time: 274 us; the launch traced here: 273 us
  waiting for transfers between devices  121 us (44%)
  Pallas kernels  78.7 us (29%)
  starting transfers between devices  45 us (16%)
  local copies, waits for them, and re-layouts  16 us (6%)
  other arithmetic  10.6 us (4%)
    all_to_all x6, waiting for transfers between devices, exchange(): return lax.all_to_all(values, AXES, split_axis=0, concat_axis=0, tiled=True)  121 us
    pallas_call x2, Pallas kernels, run_blocks(): pl.pallas_call(functools.partial(step_kernel, first, stride), out_shape=(...  51.9 us
    all_to_all x6, starting transfers between devices, exchange(): return lax.all_to_all(values, AXES, split_axis=0, concat_axis=0, tiled=True)  42.6 us
    pallas_call x1, Pallas kernels, collect_halves(): pl.pallas_call(collect_halves_kernel, out_shape=(jax.ShapeDtypeStruct((ow...  9.53 us
    pallas_call x1, Pallas kernels, collect(): pl.pallas_call(functools.partial(collect_kernel, first), out_shape=jax.Sh...  8.08 us
  transfers between devices with their start and end apart: 8, of which 5 were waited for; matrix products, arithmetic and copies ran while one was open for 6% of the time, Pallas kernels for 24%

profile of v4, /device:TPU:1, one launch (start us, length us, event | category | flops | bytes accessed | tf_op | source)
XLA Modules:
  0.0 272.8 jit_solution(8496617768151498862)
XLA Ops:
  0.6 2.6 plan.1
  3.2 1.4 broadcast_in_dim.36
  4.6 11.5 %all-to-all-start.8 = ((s32[128,2,128]{2,1,0:T(2,128)}), s32[128,2,128]{2,1,0:T(2,128)S(1)}, u32[]{:S(2)}, u32[]{:S(2)}) async-start(s32[128,2,128]{2,1,0:T(2,128)} %broadcast_in_dim.36), calls=%async_computation.8 | async-start | bytes 262144 | tf_op jit(solution)/shard_map/all_to_all | solution.py:576
  16.1 10.2 %all-to-all-done.8 = s32[128,2,128]{2,1,0:T(2,128)S(1)} async-done(((s32[128,2,128]{2,1,0:T(2,128)}), s32[128,2,128]{2,1,0:T(2,128)S(1)}, u32[]{:S(2)}, u32[]{:S(2)}) %all-to-all-start.8) | async-done | bytes 131104 | tf_op jit(solution)/shard_map/all_to_all | solution.py:576
  26.4 0.2 constant_dynamic-slice_fusion
  26.7 0.5 copy-done.11
  27.2 4.4 %gather_fusion.2 = bf16[128,32,512]{2,1,0:T(8,128)(2,1)} fusion(bf16[64,32,512]{2,1,0:T(8,128)(2,1)} %bitcast.45, s32[1024]{0:T(1024)S(1)} %pad_clamp_fusion), kind=kCustom, calls=%fused_computation.2 | custom fusion | bytes 8389120 | tf_op jit(solution)/shard_map/gather | solution.py:619
  31.6 5.1 %all-to-all-start.9 = ((bf16[128,32,512]{2,1,0:T(8,128)(2,1)}), bf16[128,32,512]{2,1,0:T(8,128)(2,1)}, u32[]{:S(2)}, u32[]{:S(2)}) async-start(bf16[128,32,512]{2,1,0:T(8,128)(2,1)} %gather_fusion.2), calls=%async_computation.9 | async-start | bytes 8388608 | tf_op jit(solution)/shard_map/all_to_all | solution.py:576
  36.8 1.2 dynamic-slice_bitcast_fusion.1
  38.0 1.3 collective-permute-start.1
  39.5 0.2 concatenate.30
  39.7 0.7 pad_maximum_fusion.1.rays_ref
  40.4 1.3 expand.1
  41.8 0.6 fusion.3
  43.1 0.5 maximum_bitcast_fusion.1
  43.6 0.6 pad_clamp_fusion.1
  44.2 2.8 %gather_fusion = bf16[128,32,512]{2,1,0:T(8,128)(2,1)} fusion(bf16[64,32,512]{2,1,0:T(8,128)(2,1)S(1)} %bitcast.46, s32[1024]{0:T(1024)S(1)} %get-tuple-element.174), kind=kCustom, calls=%fused_computation | custom fusion | bytes 8389120 | tf_op jit(solution)/shard_map/gather | solution.py:620
  47.0 0.5 fusion.6
  47.5 1.4 pad_maximum_fusion
  49.1 2.2 gather_fusion.1
  51.3 36.7 %all-to-all-done.9 = bf16[128,32,512]{2,1,0:T(8,128)(2,1)} async-done(((bf16[128,32,512]{2,1,0:T(8,128)(2,1)}), bf16[128,32,512]{2,1,0:T(8,128)(2,1)}, u32[]{:S(2)}, u32[]{:S(2)}) %all-to-all-start.9) | async-done | bytes 4194336 | tf_op jit(solution)/shard_map/all_to_all | solution.py:576
  88.2 179.8 %conditional.1 = (f32[64,32,512]{2,1,0:T(8,128)}, f32[3,512]{1,0:T(4,128)S(1)}, f32[1024,128]{1,0:T(8,128)}) conditional(s32[]{:T(128)} %convert_element_type.12, (s32[]{:T(128)}, s32[128]{0:T(128)S(1)}, s32[128,1,1]{0,2,1:T(1,128)S(1)}, bf16[128,16,512]{2,1,0:T(8,128)(2,1)}, f32[256]{0:T(256)S(1)}, /*index=5*/f32[256]{0:T(256)S(1)}, ...), branch_computations={%region_1.3_spmd, %region_3.5_spmd} | conditional | flops 10084770816 | bytes 87760656 | solution.py:656
  88.2 5.6 %all-to-all-start = ((bf16[128,16,512]{2,1,0:T(8,128)(2,1)}), bf16[128,16,512]{2,1,0:T(8,128)(2,1)}, u32[]{:S(2)}, u32[]{:S(2)}) async-start(bf16[128,16,512]{2,1,0:T(8,128)(2,1)} %get-tuple-element.83), calls=%async_computation | async-start | bytes 4194304 | tf_op jit(solution)/shard_map/cond/branch_0_fun/all_to_all | solution.py:576
  93.8 0.6 broadcast_3_carried_ref.0.carried_ref
  94.3 40.9 %branch_0_fun.2 = (bf16[128,128,128]{2,1,0:T(8,128)(2,1)}, f32[3,136,128]{2,1,0:T(8,128)}, f32[1024,128]{1,0:T(8,128)}) custom-call(s32[2,160]{1,0:T(2,128)S(1)} %get-tuple-element.79.lists_ref, s32[128]{0:T(128)S(1)} %get-tuple-element.80.owner_ref, f32[4]{0:T(128)S(1)} %get-tuple-element.81.b_out_ref, ...), custom_call_target="tpu_custom_call" | custom-call | flops 8960000000 | bytes 25600000 | tf_op jit(solution)/shard_map/cond/branch_0_fun/pallas_call | solution.py:390
  135.2 10.2 %all-to-all-start.2 = ((bf16[128,128,128]{2,1,0:T(8,128)(2,1)}), bf16[128,128,128]{2,1,0:T(8,128)(2,1)}, u32[]{:S(2)}, u32[]{:S(2)}) async-start(bf16[128,128,128]{2,1,0:T(8,128)(2,1)} %get-tuple-element.94), calls=%async_computation.2 | async-start | bytes 8388608 | tf_op jit(solution)/shard_map/cond/branch_0_fun/all_to_all | solution.py:576
  145.5 11.1 %branch_0_fun.3 = (bf16[128,80,128]{2,1,0:T(8,128)(2,1)}, f32[3,136,128]{2,1,0:T(8,128)}, f32[1024,128]{1,0:T(8,128)}) custom-call(s32[2,160]{1,0:T(2,128)S(1)} %get-tuple-element.79.lists_ref, s32[128]{0:T(128)S(1)} %get-tuple-element.80.owner_ref, f32[4]{0:T(128)S(1)} %get-tuple-element.81.b_out_ref, bf16[128,128,512]{2,1,0:T(8,128)(2,1)} %get-tuple-element.82.weights_hbm, ...), custom_call_target="tpu_custom_call" | custom-call | flops 1120000000 | bytes 3200000 | tf_op jit(solution)/shard_map/cond/branch_0_fun/pallas_call | solution.py:390
  156.6 40.1 %all-to-all-done.2.grads_ref = bf16[128,128,128]{2,1,0:T(8,128)(2,1)} async-done(((bf16[128,128,128]{2,1,0:T(8,128)(2,1)}), bf16[128,128,128]{2,1,0:T(8,128)(2,1)}, u32[]{:S(2)}, u32[]{:S(2)}) %all-to-all-start.2) | async-done | bytes 4194336 | tf_op jit(solution)/shard_map/cond/branch_0_fun/all_to_all | solution.py:576
  196.6 5.5 %all-to-all-start.1 = ((bf16[128,80,128]{2,1,0:T(8,128)(2,1)}), bf16[128,80,128]{2,1,0:T(8,128)(2,1)}, u32[]{:S(2)}, u32[]{:S(2)}) async-start(bf16[128,80,128]{2,1,0:T(8,128)(2,1)} %get-tuple-element.92), calls=%async_computation.1 | async-start | bytes 5242880 | tf_op jit(solution)/shard_map/cond/branch_0_fun/all_to_all | solution.py:576
  202.2 0.6 pad_add_fusion.ids_ref
  202.7 8.1 %collect_first.2.carried_ref = f32[64,32,512]{2,1,0:T(8,128)} custom-call(s32[128]{0:T(128)S(1)} %get-tuple-element.93.ids_ref, bf16[128,128,128]{2,1,0:T(8,128)(2,1)} %all-to-all-done.2.grads_ref, f32[8,128]{1,0:T(8,128)} %broadcast_3_carried_ref.0.carried_ref), custom_call_target="tpu_custom_call" | custom-call | flops 2097152 | bytes 8388608 | tf_op jit(solution)/shard_map/cond/branch_0_fun/collect_first/pallas_call | solution.py:473
  210.8 26.0 %all-to-all-done.1.grads_ref = bf16[128,80,128]{2,1,0:T(8,128)(2,1)} async-done(((bf16[128,80,128]{2,1,0:T(8,128)(2,1)}), bf16[128,80,128]{2,1,0:T(8,128)(2,1)}, u32[]{:S(2)}, u32[]{:S(2)}) %all-to-all-start.1) | async-done | bytes 2621472 | tf_op jit(solution)/shard_map/cond/branch_0_fun/all_to_all | solution.py:576
  236.8 9.5 %collect_halves.1 = (f32[64,32,512]{2,1,0:T(8,128)}, f32[64,16,512]{2,1,0:T(8,128)}) custom-call(s32[129]{0:T(256)} %pad_add_fusion.ids_ref, bf16[128,80,128]{2,1,0:T(8,128)(2,1)} %all-to-all-done.1.grads_ref, f32[64,32,512]{2,1,0:T(8,128)} %collect_first.2.carried_ref), custom_call_target="tpu_custom_call" | custom-call | flops 2097152 | bytes 8388608 | tf_op jit(solution)/shard_map/cond/branch_0_fun/collect_halves/pallas_call | solution.py:520
  246.3 1.2 collective-permute-start
  247.5 1.1 slice_convert_fusion
  248.8 0.8 broadcast_in_dim.15
  249.6 4.7 %all-to-all-start.3 = ((f32[128,8,128]{2,1,0:T(8,128)}), f32[128,8,128]{2,1,0:T(8,128)}, u32[]{:S(2)}, u32[]{:S(2)}) async-start(f32[128,8,128]{2,1,0:T(8,128)} %broadcast_in_dim.15), calls=%async_computation.3 | async-start | bytes 1048576 | tf_op jit(solution)/shard_map/cond/branch_0_fun/all_to_all | solution.py:576
  254.3 0.5 slice.52
  254.8 0.1 reshape.122
  255.0 5.2 %merge.1 = f32[64,32,512]{2,1,0:T(8,128)} custom-call(s32[1]{0:T(128)} %bitcast.core_ref, f32[64,32,512]{2,1,0:T(8,128)} %get-tuple-element.95.sums_ref, f32[64,16,512]{2,1,0:T(8,128)} %collective-permute-done.arrived_ref), custom_call_target="tpu_custom_call" | custom-call | tf_op jit(solution)/shard_map/cond/branch_0_fun/merge/pallas_call | solution.py:561
  260.2 7.8 %all-to-all-done.3 = f32[128,8,128]{2,1,0:T(8,128)} async-done(((f32[128,8,128]{2,1,0:T(8,128)}), f32[128,8,128]{2,1,0:T(8,128)}, u32[]{:S(2)}, u32[]{:S(2)}) %all-to-all-start.3) | async-done | bytes 524320 | tf_op jit(solution)/shard_map/cond/branch_0_fun/all_to_all | solution.py:576
  268.0 1.1 broadcast_multiply_fusion
  269.1 0.6 slice_reduce_fusion
  269.7 0.6 pad_maximum_fusion.4
  270.3 0.6 pad_maximum_fusion.5
  270.9 0.6 pad_maximum_fusion.6
  271.4 0.7 pad_maximum_fusion.2
  272.2 0.6 pad_maximum_fusion.3
  (52 shorter events, 0.7 us)
Async XLA Ops:
  4.6 21.7 %all-to-all-start.8 = ((s32[128,2,128]{2,1,0:T(2,128)}), s32[128,2,128]{2,1,0:T(2,128)S(1)}, u32[]{:S(2)}, u32[]{:S(2)}) async-start(s32[128,2,128]{2,1,0:T(2,128)} %broadcast_in_dim.36), calls=%async_computation.8 | async-start | bytes 262144 | tf_op jit(solution)/shard_map/all_to_all | solution.py:576
  26.7 0.5 copy-start.11
  31.6 5.2 %copy-start = (bf16[64,512,32]{1,2,0:T(8,128)(2,1)S(1)}, bf16[64,512,32]{1,2,0:T(8,128)(2,1)}, u32[]{:S(2)}) copy-start(bf16[64,512,32]{1,2,0:T(8,128)(2,1)} %param.14) | copy-start | bytes 6291460
  31.6 56.4 %all-to-all-start.9 = ((bf16[128,32,512]{2,1,0:T(8,128)(2,1)}), bf16[128,32,512]{2,1,0:T(8,128)(2,1)}, u32[]{:S(2)}, u32[]{:S(2)}) async-start(bf16[128,32,512]{2,1,0:T(8,128)(2,1)} %gather_fusion.2), calls=%async_computation.9 | async-start | bytes 8388608 | tf_op jit(solution)/shard_map/all_to_all | solution.py:576
  36.8 2.5 copy-start.17
  36.8 2.6 copy-start.9
  38.0 9.5 %collective-permute-start.1 = (bf16[64,16,512]{2,1,0:T(8,128)(2,1)}, bf16[64,16,512]{2,1,0:T(8,128)(2,1)}, u32[]{:S(2)}, u32[]{:S(2)}) collective-permute-start(bf16[64,16,512]{2,1,0:T(8,128)(2,1)} %get-tuple-element.159), channel_id=1, source_target_pairs={{0,16},{16,0},{32,48},{48,32},{64,80},{80,64},{96,112},{112,96},{1... | collective-permute-start | bytes 3145736 | tf_op jit(solution)/shard_map/ppermute | solution.py:618
  47.5 40.6 %copy-start.1 = (bf16[256,256]{1,0:T(8,128)(2,1)S(1)}, bf16[256,256]{1,0:T(8,128)(2,1)}, u32[]{:S(2)}) copy-start(bf16[256,256]{1,0:T(8,128)(2,1)} %param.22) | copy-start | bytes 393220
  47.5 40.6 %copy-start.6 = (bf16[32,256]{1,0:T(8,128)(2,1)S(1)}, bf16[32,256]{1,0:T(8,128)(2,1)}, u32[]{:S(2)}) copy-start(bf16[32,256]{1,0:T(8,128)(2,1)} %param.20) | copy-start | bytes 49156
  49.0 39.1 %copy-start.7 = (bf16[4,256]{1,0:T(4,128)(2,1)S(1)}, bf16[4,256]{1,0:T(4,128)(2,1)}, u32[]{:S(2)}) copy-start(bf16[4,256]{1,0:T(4,128)(2,1)} %param.24) | copy-start | bytes 6148
  49.0 39.1 %copy-start.8 = (s32[2,160]{1,0:T(2,128)S(1)}, s32[2,160]{1,0:T(2,128)}, u32[]{:S(2)}) copy-start(s32[2,160]{1,0:T(2,128)} %get-tuple-element.135) | copy-start | bytes 3844
  49.0 39.1 %copy-start.12 = (s32[128,1,1]{0,2,1:T(1,128)S(1)}, s32[128,1,1]{0,2,1:T(1,128)}, u32[]{:S(2)}) copy-start(s32[128,1,1]{0,2,1:T(1,128)} %copy-done.11) | copy-start | bytes 1540
  49.0 39.1 %copy-start.13 = (f32[256]{0:T(256)S(1)}, f32[256]{0:T(256)}, u32[]{:S(2)}) copy-start(f32[256]{0:T(256)} %param.21) | copy-start | bytes 3076
  49.0 39.1 %copy-start.14 = (f32[256]{0:T(256)S(1)}, f32[256]{0:T(256)}, u32[]{:S(2)}) copy-start(f32[256]{0:T(256)} %param.23) | copy-start | bytes 3076
  49.0 39.1 %copy-start.15 = (s32[128,1]{0,1:T(1,128)S(1)}, s32[128,1]{0,1:T(1,128)}, u32[]{:S(2)}) copy-start(s32[128,1]{0,1:T(1,128)} %param.16) | copy-start | bytes 1540
  49.0 39.1 %copy-start.16 = (f32[4]{0:T(128)S(1)}, f32[4]{0:T(128)}, u32[]{:S(2)}) copy-start(f32[4]{0:T(128)} %param.25) | copy-start | bytes 52
  49.1 39.1 %copy-start.18 = (s32[128]{0:T(128)S(1)}, s32[128]{0:T(128)}, u32[]{:S(2)}) copy-start(s32[128]{0:T(128)} %fusion.6) | copy-start | bytes 1540
  49.1 39.1 %copy-start.19 = (s32[128,1,1]{0,2,1:T(1,128)S(1)}, s32[128,1,1]{0,2,1:T(1,128)}, u32[]{:S(2)}) copy-start(s32[128,1,1]{0,2,1:T(1,128)} %get-tuple-element.157) | copy-start | bytes 1540
  88.2 47.0 %all-to-all-start = ((bf16[128,16,512]{2,1,0:T(8,128)(2,1)}), bf16[128,16,512]{2,1,0:T(8,128)(2,1)}, u32[]{:S(2)}, u32[]{:S(2)}) async-start(bf16[128,16,512]{2,1,0:T(8,128)(2,1)} %get-tuple-element.83), calls=%async_computation | async-start | bytes 4194304 | tf_op jit(solution)/shard_map/cond/branch_0_fun/all_to_all | solution.py:576
  135.2 61.4 %all-to-all-start.2 = ((bf16[128,128,128]{2,1,0:T(8,128)(2,1)}), bf16[128,128,128]{2,1,0:T(8,128)(2,1)}, u32[]{:S(2)}, u32[]{:S(2)}) async-start(bf16[128,128,128]{2,1,0:T(8,128)(2,1)} %get-tuple-element.94), calls=%async_computation.2 | async-start | bytes 8388608 | tf_op jit(solution)/shard_map/cond/branch_0_fun/all_to_all | solution.py:576
  196.6 40.1 %all-to-all-start.1 = ((bf16[128,80,128]{2,1,0:T(8,128)(2,1)}), bf16[128,80,128]{2,1,0:T(8,128)(2,1)}, u32[]{:S(2)}, u32[]{:S(2)}) async-start(bf16[128,80,128]{2,1,0:T(8,128)(2,1)} %get-tuple-element.92), calls=%async_computation.1 | async-start | bytes 5242880 | tf_op jit(solution)/shard_map/cond/branch_0_fun/all_to_all | solution.py:576
  210.8 43.5 %copy-start.2 = (f32[3,136,128]{2,1,0:T(8,128)S(1)}, f32[3,136,128]{2,1,0:T(8,128)}, u32[]{:S(2)}) copy-start(f32[3,136,128]{2,1,0:T(8,128)} %get-tuple-element.97) | copy-start | bytes 626692 | tf_op jit(solution)/shard_map/cond
  210.8 43.5 %copy-start.3 = (f32[3,136,128]{2,1,0:T(8,128)S(1)}, f32[3,136,128]{2,1,0:T(8,128)}, u32[]{:S(2)}) copy-start(f32[3,136,128]{2,1,0:T(8,128)} %get-tuple-element.98) | copy-start | bytes 626692 | tf_op jit(solution)/shard_map/cond
  246.3 8.7 %collective-permute-start = (f32[64,16,512]{2,1,0:T(8,128)}, f32[64,16,512]{2,1,0:T(8,128)}, u32[]{:S(2)}, u32[]{:S(2)}) collective-permute-start(f32[64,16,512]{2,1,0:T(8,128)} %get-tuple-element.96), channel_id=1, source_target_pairs={{0,16},{16,0},{32,48},{48,32},{64,80},{80,64},{96,112},{112,96},{1... | collective-permute-start | bytes 6291464 | tf_op jit(solution)/shard_map/cond/branch_0_fun/ppermute | solution.py:649
  249.6 18.4 %all-to-all-start.3 = ((f32[128,8,128]{2,1,0:T(8,128)}), f32[128,8,128]{2,1,0:T(8,128)}, u32[]{:S(2)}, u32[]{:S(2)}) async-start(f32[128,8,128]{2,1,0:T(8,128)} %broadcast_in_dim.15), calls=%async_computation.3 | async-start | bytes 1048576 | tf_op jit(solution)/shard_map/cond/branch_0_fun/all_to_all | solution.py:576
  268.0 4.8 %copy-start.10 = (f32[3,512]{1,0:T(4,128)}, f32[3,512]{1,0:T(4,128)S(1)}, u32[]{:S(2)}) copy-start(f32[3,512]{1,0:T(4,128)S(1)} %get-tuple-element.126) | copy-start | bytes 18436

commit v5 on v4

--- a/solution.py
+++ b/solution.py
@@ -572,6 +572,51 @@
     )(core, sums, arrived)
 
 
+def add_up_kernel(parts_ref, out_ref):
+    parts = parts_ref[...].astype(F32)
+    total = jnp.sum(parts[:, :8] + parts[:, 8:], axis=0, keepdims=True)
+    out_ref[...] = jnp.broadcast_to(total, out_ref.shape)
+
+
+def add_up(returned, rows):
+    devices = returned.shape[0]
+    return pl.pallas_call(
+        add_up_kernel,
+        out_shape=jax.ShapeDtypeStruct((devices, 8, BLOCK), F32),
+        grid=(1,),
+        in_specs=[pl.BlockSpec((devices, 16, BLOCK), lambda i: (0, rows // 16, 0))],
+        out_specs=pl.BlockSpec((devices, 8, BLOCK), lambda i: (0, 0, 0)),
+        name="add_up",
+    )(returned)
+
+
+def unpack_kernel(
+    scale, totals_ref, w_in_ref, b_in_ref, w_hid_ref, b_hid_ref, w_out_ref, b_out_ref
+):
+    half = WIDTH // 2
+    for side in range(2):
+        lanes = slice(side * half, (side + 1) * half)
+        w_hid_ref[:, lanes] = totals_ref[side * 256 : side * 256 + 256, :] * scale
+        w_in_ref[:, lanes] = totals_ref[512 + side * 32 : 544 + side * 32, :] * scale
+        w_out_ref[:, lanes] = totals_ref[576 + side * 8 : 580 + side * 8, :] * scale
+        b_hid_ref[:, lanes] = totals_ref[592 + side * 8 : 593 + side * 8, :] * scale
+        b_in_ref[:, lanes] = totals_ref[608 + side * 8 : 609 + side * 8, :] * scale
+    for c in range(4):
+        b_out_ref[c] = jnp.sum(totals_ref[624 + c : 625 + c, :]) * scale
+
+
+def unpack(totals, scale):
+    vmem = pl.BlockSpec(memory_space=pltpu.VMEM)
+    shapes = ((FEAT, WIDTH), (1, WIDTH), (WIDTH, WIDTH), (1, WIDTH), (4, WIDTH), (4,))
+    return pl.pallas_call(
+        functools.partial(unpack_kernel, scale),
+        out_shape=tuple(jax.ShapeDtypeStruct(shape, F32) for shape in shapes),
+        in_specs=[vmem],
+        out_specs=(vmem,) * 5 + (pl.BlockSpec(memory_space=pltpu.SMEM),),
+        name="unpack",
+    )(totals)
+
+
 def exchange(values):
     return lax.all_to_all(values, AXES, split_axis=0, concat_axis=0, tiled=True)
 
@@ -639,9 +684,7 @@
         returned_0 = exchange(grads_0)
         returned_1 = exchange(grads_1)
         partial = collect(ids_0, returned_0, own_bricks, None)
-        parts = returned_1[:, rows:].astype(F32)
-        chunk = jnp.sum(parts[:, :8] + parts[:, 8:], axis=0)
-        totals = exchange(jnp.broadcast_to(chunk[None], (dev_count, 8, BLOCK)))
+        totals = exchange(add_up(returned_1, rows))
         if split:
             grad, spare = collect_halves(
                 jnp.concatenate([ids_1, core[None]]), returned_1, own_bricks, partial
@@ -650,7 +693,7 @@
         else:
             grad = collect(ids_1, returned_1, own_bricks, partial)
         color = (color_0 + color_1)[:, :own_blocks, ::RAY_LEN].reshape(3, -1)
-        return grad, color, totals
+        return lax.optimization_barrier((grad, color, totals))
 
     common = (lists, owners, interp_weights, rays, mine[0])
     brick_grad, color, totals = lax.cond(
@@ -664,18 +707,11 @@
     )
     brick_grad = jnp.swapaxes(brick_grad, 1, 2)
 
-    totals = totals.reshape(GRAD_ROWS, BLOCK) / (sample_count.shape[0] * dev_count)
-
-    def joined(start, rows):
-        return jnp.concatenate([totals[start : start + rows], totals[start + rows : start + 2 * rows]], axis=1)
-
-    g_w_hid = joined(0, WIDTH)
-    g_w_in = joined(2 * WIDTH, FEAT)
-    g_w_out = joined(576, 8)[:4]
-    g_b_hid = joined(592, 8)[0]
-    g_b_in = joined(608, 8)[0]
-    g_b_out = jnp.sum(totals[624:628], axis=1)
-    return (brick_grad, color, g_w_in, g_b_in, g_w_hid, g_b_hid, g_w_out, g_b_out)
+    scale = 1.0 / (sample_count.shape[0] * dev_count)
+    g_w_in, g_b_in, g_w_hid, g_b_hid, g_w_out, g_b_out = unpack(
+        totals.reshape(GRAD_ROWS, BLOCK), scale
+    )
+    return (brick_grad, color, g_w_in, g_b_in[0], g_w_hid, g_b_hid[0], g_w_out, g_b_out)
 
 
 def solution(mesh):

time: 274 us -> 271 us (0.989)
  other arithmetic: 10.6 us -> 4.58 us
  Pallas kernels: 78.7 us -> 82.5 us
    pallas_call x0 -> x2, Pallas kernels: none -> 3.81 us  [the longest x1 2.03 us: add_up(): pl.pallas_call(add_up_kernel, out_shape=jax.ShapeDtypeStruct((devices, 8,...]
    concatenate x5 -> x0, other arithmetic: 3.06 us -> none  [joined(): jnp.concatenate([totals[start:start + rows], totals[start + rows:start +...]
  transfers between devices with their start and end apart: 8 -> 8, of which waited for: 5 -> 5; matrix products, arithmetic and copies ran while one was open for 6% -> 5% of each run, Pallas kernels for 24% -> 25%
where the time goes in v5:
time: 271 us; the launch traced here: 270 us
  waiting for transfers between devices  121 us (45%)
  Pallas kernels  82.5 us (30%)
  starting transfers between devices  45 us (17%)
  local copies, waits for them, and re-layouts  15.1 us (6%)
  other arithmetic  4.58 us (2%)
    all_to_all x6, waiting for transfers between devices, exchange(): return lax.all_to_all(values, AXES, split_axis=0, concat_axis=0, tiled=True)  121 us
    pallas_call x2, Pallas kernels, run_blocks(): pl.pallas_call(functools.partial(step_kernel, first, stride), out_shape=(...  52 us
    all_to_all x6, starting transfers between devices, exchange(): return lax.all_to_all(values, AXES, split_axis=0, concat_axis=0, tiled=True)  42.6 us
    pallas_call x1, Pallas kernels, collect_halves(): pl.pallas_call(collect_halves_kernel, out_shape=(jax.ShapeDtypeStruct((ow...  9.55 us
    pallas_call x1, Pallas kernels, collect(): pl.pallas_call(functools.partial(collect_kernel, first), out_shape=jax.Sh...  8.08 us
  transfers between devices with their start and end apart: 8, of which 5 were waited for; matrix products, arithmetic and copies ran while one was open for 5% of the time, Pallas kernels for 25%

profile of v5, /device:TPU:1, one launch (start us, length us, event | category | flops | bytes accessed | tf_op | source)
XLA Modules:
  0.0 269.8 jit_solution(13554485946682396200)
XLA Ops:
  0.6 2.6 plan.1
  3.2 1.4 broadcast_in_dim.39
  4.6 11.5 %all-to-all-start.8 = ((s32[128,2,128]{2,1,0:T(2,128)}), s32[128,2,128]{2,1,0:T(2,128)S(1)}, u32[]{:S(2)}, u32[]{:S(2)}) async-start(s32[128,2,128]{2,1,0:T(2,128)} %broadcast_in_dim.39), calls=%async_computation.8 | async-start | bytes 262144 | tf_op jit(solution)/shard_map/all_to_all | solution.py:621
  16.1 10.2 %all-to-all-done.8 = s32[128,2,128]{2,1,0:T(2,128)S(1)} async-done(((s32[128,2,128]{2,1,0:T(2,128)}), s32[128,2,128]{2,1,0:T(2,128)S(1)}, u32[]{:S(2)}, u32[]{:S(2)}) %all-to-all-start.8) | async-done | bytes 131104 | tf_op jit(solution)/shard_map/all_to_all | solution.py:621
  26.3 0.1 fusion.5
  26.4 0.2 constant_dynamic-slice_fusion
  26.6 0.1 copy.33
  26.7 0.5 copy-done.11
  27.2 4.4 %gather_fusion.2 = bf16[128,32,512]{2,1,0:T(8,128)(2,1)} fusion(bf16[64,32,512]{2,1,0:T(8,128)(2,1)} %bitcast.44, s32[1024]{0:T(1024)S(1)} %pad_clamp_fusion), kind=kCustom, calls=%fused_computation.2 | custom fusion | bytes 8389120 | tf_op jit(solution)/shard_map/gather | solution.py:664
  31.6 5.1 %all-to-all-start.9 = ((bf16[128,32,512]{2,1,0:T(8,128)(2,1)}), bf16[128,32,512]{2,1,0:T(8,128)(2,1)}, u32[]{:S(2)}, u32[]{:S(2)}) async-start(bf16[128,32,512]{2,1,0:T(8,128)(2,1)} %gather_fusion.2), calls=%async_computation.9 | async-start | bytes 8388608 | tf_op jit(solution)/shard_map/all_to_all | solution.py:621
  36.7 0.0 copy-start.17
  36.8 0.0 copy-start.9
  36.8 1.2 dynamic-slice_bitcast_fusion.1
  38.0 1.3 collective-permute-start.1
  39.3 0.1 concatenate.16
  39.4 0.2 concatenate.15
  39.6 0.7 pad_maximum_fusion.1.rays_ref
  40.3 1.3 expand.1
  41.7 0.1 copy.31
  41.8 0.6 fusion.1
  43.1 0.5 maximum_bitcast_fusion.1
  43.6 0.6 pad_clamp_fusion.1
  44.2 2.8 %gather_fusion = bf16[128,32,512]{2,1,0:T(8,128)(2,1)} fusion(bf16[64,32,512]{2,1,0:T(8,128)(2,1)S(1)} %bitcast.45, s32[1024]{0:T(1024)S(1)} %get-tuple-element.175), kind=kCustom, calls=%fused_computation | custom fusion | bytes 8389120 | tf_op jit(solution)/shard_map/gather | solution.py:665
  47.0 0.5 fusion.4
  47.5 1.4 pad_maximum_fusion
  48.9 0.0 copy-start.7
  49.1 2.2 gather_fusion.1
  51.3 36.7 %all-to-all-done.9 = bf16[128,32,512]{2,1,0:T(8,128)(2,1)} async-done(((bf16[128,32,512]{2,1,0:T(8,128)(2,1)}), bf16[128,32,512]{2,1,0:T(8,128)(2,1)}, u32[]{:S(2)}, u32[]{:S(2)}) %all-to-all-start.9) | async-done | bytes 4194336 | tf_op jit(solution)/shard_map/all_to_all | solution.py:621
  88.1 179.7 %conditional.1 = (f32[64,32,512]{2,1,0:T(8,128)}, f32[3,512]{1,0:T(4,128)S(1)}, f32[128,8,128]{2,1,0:T(8,128)}) conditional(s32[]{:T(128)} %convert_element_type.6, (s32[]{:T(128)}, s32[128]{0:T(128)S(1)}, s32[128,1,1]{0,2,1:T(1,128)S(1)}, bf16[128,16,512]{2,1,0:T(8,128)(2,1)}, f32[256]{0:T(256)S(1)}, /*index=5*/f32[256]{0:T(256)S(1)}, ...), branch_computations={%region_1.2_spmd, %region_2.3_spmd} | conditional | flops 10084247552 | bytes 84606736 | solution.py:699
  88.1 5.6 %all-to-all-start.4 = ((bf16[128,16,512]{2,1,0:T(8,128)(2,1)}), bf16[128,16,512]{2,1,0:T(8,128)(2,1)}, u32[]{:S(2)}, u32[]{:S(2)}) async-start(bf16[128,16,512]{2,1,0:T(8,128)(2,1)} %get-tuple-element.82), calls=%async_computation.4 | async-start | bytes 4194304 | tf_op jit(solution)/shard_map/cond/branch_0_fun/all_to_all | solution.py:621
  93.7 0.6 broadcast_3_carried_ref.0.carried_ref
  94.3 40.9 %branch_0_fun.2 = (bf16[128,128,128]{2,1,0:T(8,128)(2,1)}, f32[3,136,128]{2,1,0:T(8,128)}, f32[1024,128]{1,0:T(8,128)}) custom-call(s32[2,160]{1,0:T(2,128)S(1)} %get-tuple-element.78.lists_ref, s32[128]{0:T(128)S(1)} %get-tuple-element.79.owner_ref, f32[4]{0:T(128)S(1)} %get-tuple-element.80.b_out_ref, ...), custom_call_target="tpu_custom_call" | custom-call | flops 8960000000 | bytes 25600000 | tf_op jit(solution)/shard_map/cond/branch_0_fun/pallas_call | solution.py:390
  135.2 10.2 %all-to-all-start.6 = ((bf16[128,128,128]{2,1,0:T(8,128)(2,1)}), bf16[128,128,128]{2,1,0:T(8,128)(2,1)}, u32[]{:S(2)}, u32[]{:S(2)}) async-start(bf16[128,128,128]{2,1,0:T(8,128)(2,1)} %get-tuple-element.93), calls=%async_computation.6 | async-start | bytes 8388608 | tf_op jit(solution)/shard_map/cond/branch_0_fun/all_to_all | solution.py:621
  145.4 11.1 %branch_0_fun.3 = (bf16[128,80,128]{2,1,0:T(8,128)(2,1)}, f32[3,136,128]{2,1,0:T(8,128)}, f32[1024,128]{1,0:T(8,128)}) custom-call(s32[2,160]{1,0:T(2,128)S(1)} %get-tuple-element.78.lists_ref, s32[128]{0:T(128)S(1)} %get-tuple-element.79.owner_ref, f32[4]{0:T(128)S(1)} %get-tuple-element.80.b_out_ref, bf16[128,128,512]{2,1,0:T(8,128)(2,1)} %get-tuple-element.81.weights_hbm, ...), custom_call_target="tpu_custom_call" | custom-call | flops 1120000000 | bytes 3200000 | tf_op jit(solution)/shard_map/cond/branch_0_fun/pallas_call | solution.py:390
  156.5 40.0 %all-to-all-done.6.grads_ref = bf16[128,128,128]{2,1,0:T(8,128)(2,1)} async-done(((bf16[128,128,128]{2,1,0:T(8,128)(2,1)}), bf16[128,128,128]{2,1,0:T(8,128)(2,1)}, u32[]{:S(2)}, u32[]{:S(2)}) %all-to-all-start.6) | async-done | bytes 4194336 | tf_op jit(solution)/shard_map/cond/branch_0_fun/all_to_all | solution.py:621
  196.6 5.5 %all-to-all-start.5 = ((bf16[128,80,128]{2,1,0:T(8,128)(2,1)}), bf16[128,80,128]{2,1,0:T(8,128)(2,1)}, u32[]{:S(2)}, u32[]{:S(2)}) async-start(bf16[128,80,128]{2,1,0:T(8,128)(2,1)} %get-tuple-element.91), calls=%async_computation.5 | async-start | bytes 5242880 | tf_op jit(solution)/shard_map/cond/branch_0_fun/all_to_all | solution.py:621
  202.1 0.6 pad_add_fusion.ids_ref
  202.7 8.1 %collect_first.2.carried_ref = f32[64,32,512]{2,1,0:T(8,128)} custom-call(s32[128]{0:T(128)S(1)} %get-tuple-element.92.ids_ref, bf16[128,128,128]{2,1,0:T(8,128)(2,1)} %all-to-all-done.6.grads_ref, f32[8,128]{1,0:T(8,128)} %broadcast_3_carried_ref.0.carried_ref), custom_call_target="tpu_custom_call" | custom-call | flops 2097152 | bytes 8388608 | tf_op jit(solution)/shard_map/cond/branch_0_fun/collect_first/pallas_call | solution.py:473
  210.7 26.0 %all-to-all-done.5.grads_ref.parts_ref = bf16[128,80,128]{2,1,0:T(8,128)(2,1)} async-done(((bf16[128,80,128]{2,1,0:T(8,128)(2,1)}), bf16[128,80,128]{2,1,0:T(8,128)(2,1)}, u32[]{:S(2)}, u32[]{:S(2)}) %all-to-all-start.5) | async-done | bytes 2621472 | tf_op jit(solution)/shard_map/cond/branch_0_fun/all_to_all | solution.py:621
  236.7 9.5 %collect_halves.1 = (f32[64,32,512]{2,1,0:T(8,128)}, f32[64,16,512]{2,1,0:T(8,128)}) custom-call(s32[129]{0:T(256)} %pad_add_fusion.ids_ref, bf16[128,80,128]{2,1,0:T(8,128)(2,1)} %all-to-all-done.5.grads_ref.parts_ref, f32[64,32,512]{2,1,0:T(8,128)} %collect_first.2.carried_ref), custom_call_target="tpu_custom_call" | custom-call | flops 2097152 | bytes 8388608 | tf_op jit(solution)/shard_map/cond/branch_0_fun/collect_halves/pallas_call | solution.py:520
  246.2 1.2 collective-permute-start
  247.4 2.0 add_up.2
  249.5 4.7 %all-to-all-start.7 = ((f32[128,8,128]{2,1,0:T(8,128)}), f32[128,8,128]{2,1,0:T(8,128)}, u32[]{:S(2)}, u32[]{:S(2)}) async-start(f32[128,8,128]{2,1,0:T(8,128)} %add_up.2), calls=%async_computation.7 | async-start | bytes 1048576 | tf_op jit(solution)/shard_map/cond/branch_0_fun/all_to_all | solution.py:621
  254.2 0.5 slice.12
  254.7 0.1 reshape.117
  254.9 5.2 %merge.1 = f32[64,32,512]{2,1,0:T(8,128)} custom-call(s32[1]{0:T(128)} %bitcast.core_ref, f32[64,32,512]{2,1,0:T(8,128)} %get-tuple-element.94.sums_ref, f32[64,16,512]{2,1,0:T(8,128)} %collective-permute-done.arrived_ref), custom_call_target="tpu_custom_call" | custom-call | tf_op jit(solution)/shard_map/cond/branch_0_fun/merge/pallas_call | solution.py:561
  260.1 7.7 %all-to-all-done.7 = f32[128,8,128]{2,1,0:T(8,128)} async-done(((f32[128,8,128]{2,1,0:T(8,128)}), f32[128,8,128]{2,1,0:T(8,128)}, u32[]{:S(2)}, u32[]{:S(2)}) %all-to-all-start.7) | async-done | bytes 524320 | tf_op jit(solution)/shard_map/cond/branch_0_fun/all_to_all | solution.py:621
  267.8 1.8 unpack.1
  (41 shorter events, 0.2 us)
Async XLA Ops:
  4.6 21.7 %all-to-all-start.8 = ((s32[128,2,128]{2,1,0:T(2,128)}), s32[128,2,128]{2,1,0:T(2,128)S(1)}, u32[]{:S(2)}, u32[]{:S(2)}) async-start(s32[128,2,128]{2,1,0:T(2,128)} %broadcast_in_dim.39), calls=%async_computation.8 | async-start | bytes 262144 | tf_op jit(solution)/shard_map/all_to_all | solution.py:621
  26.7 0.5 copy-start.11
  31.6 5.2 %copy-start = (bf16[64,512,32]{1,2,0:T(8,128)(2,1)S(1)}, bf16[64,512,32]{1,2,0:T(8,128)(2,1)}, u32[]{:S(2)}) copy-start(bf16[64,512,32]{1,2,0:T(8,128)(2,1)} %param.14) | copy-start | bytes 6291460
  31.6 56.4 %all-to-all-start.9 = ((bf16[128,32,512]{2,1,0:T(8,128)(2,1)}), bf16[128,32,512]{2,1,0:T(8,128)(2,1)}, u32[]{:S(2)}, u32[]{:S(2)}) async-start(bf16[128,32,512]{2,1,0:T(8,128)(2,1)} %gather_fusion.2), calls=%async_computation.9 | async-start | bytes 8388608 | tf_op jit(solution)/shard_map/all_to_all | solution.py:621
  36.7 2.5 copy-start.17
  36.8 2.6 copy-start.9
  38.0 9.5 %collective-permute-start.1 = (bf16[64,16,512]{2,1,0:T(8,128)(2,1)}, bf16[64,16,512]{2,1,0:T(8,128)(2,1)}, u32[]{:S(2)}, u32[]{:S(2)}) collective-permute-start(bf16[64,16,512]{2,1,0:T(8,128)(2,1)} %get-tuple-element.170), channel_id=1, source_target_pairs={{0,16},{16,0},{32,48},{48,32},{64,80},{80,64},{96,112},{112,96},{1... | collective-permute-start | bytes 3145736 | tf_op jit(solution)/shard_map/ppermute | solution.py:663
  47.5 40.5 %copy-start.1 = (bf16[256,256]{1,0:T(8,128)(2,1)S(1)}, bf16[256,256]{1,0:T(8,128)(2,1)}, u32[]{:S(2)}) copy-start(bf16[256,256]{1,0:T(8,128)(2,1)} %param.22) | copy-start | bytes 393220
  47.5 40.5 %copy-start.6 = (bf16[32,256]{1,0:T(8,128)(2,1)S(1)}, bf16[32,256]{1,0:T(8,128)(2,1)}, u32[]{:S(2)}) copy-start(bf16[32,256]{1,0:T(8,128)(2,1)} %param.20) | copy-start | bytes 49156
  48.9 39.1 %copy-start.7 = (bf16[4,256]{1,0:T(4,128)(2,1)S(1)}, bf16[4,256]{1,0:T(4,128)(2,1)}, u32[]{:S(2)}) copy-start(bf16[4,256]{1,0:T(4,128)(2,1)} %param.24) | copy-start | bytes 6148
  49.0 39.1 %copy-start.8 = (s32[2,160]{1,0:T(2,128)S(1)}, s32[2,160]{1,0:T(2,128)}, u32[]{:S(2)}) copy-start(s32[2,160]{1,0:T(2,128)} %get-tuple-element.140) | copy-start | bytes 3844
  49.0 39.1 %copy-start.12 = (s32[128,1,1]{0,2,1:T(1,128)S(1)}, s32[128,1,1]{0,2,1:T(1,128)}, u32[]{:S(2)}) copy-start(s32[128,1,1]{0,2,1:T(1,128)} %copy-done.11) | copy-start | bytes 1540
  49.0 39.1 %copy-start.13 = (f32[256]{0:T(256)S(1)}, f32[256]{0:T(256)}, u32[]{:S(2)}) copy-start(f32[256]{0:T(256)} %param.21) | copy-start | bytes 3076
  49.0 39.1 %copy-start.14 = (f32[256]{0:T(256)S(1)}, f32[256]{0:T(256)}, u32[]{:S(2)}) copy-start(f32[256]{0:T(256)} %param.23) | copy-start | bytes 3076
  49.0 39.1 %copy-start.15 = (s32[128,1]{0,1:T(1,128)S(1)}, s32[128,1]{0,1:T(1,128)}, u32[]{:S(2)}) copy-start(s32[128,1]{0,1:T(1,128)} %param.16) | copy-start | bytes 1540
  49.0 39.1 %copy-start.16 = (f32[4]{0:T(128)S(1)}, f32[4]{0:T(128)}, u32[]{:S(2)}) copy-start(f32[4]{0:T(128)} %param.25) | copy-start | bytes 52
  49.0 39.1 %copy-start.18 = (s32[128]{0:T(128)S(1)}, s32[128]{0:T(128)}, u32[]{:S(2)}) copy-start(s32[128]{0:T(128)} %fusion.4) | copy-start | bytes 1540
  49.0 39.1 %copy-start.19 = (s32[128,1,1]{0,2,1:T(1,128)S(1)}, s32[128,1,1]{0,2,1:T(1,128)}, u32[]{:S(2)}) copy-start(s32[128,1,1]{0,2,1:T(1,128)} %get-tuple-element.168) | copy-start | bytes 1540
  88.1 47.0 %all-to-all-start.4 = ((bf16[128,16,512]{2,1,0:T(8,128)(2,1)}), bf16[128,16,512]{2,1,0:T(8,128)(2,1)}, u32[]{:S(2)}, u32[]{:S(2)}) async-start(bf16[128,16,512]{2,1,0:T(8,128)(2,1)} %get-tuple-element.82), calls=%async_computation.4 | async-start | bytes 4194304 | tf_op jit(solution)/shard_map/cond/branch_0_fun/all_to_all | solution.py:621
  135.2 61.4 %all-to-all-start.6 = ((bf16[128,128,128]{2,1,0:T(8,128)(2,1)}), bf16[128,128,128]{2,1,0:T(8,128)(2,1)}, u32[]{:S(2)}, u32[]{:S(2)}) async-start(bf16[128,128,128]{2,1,0:T(8,128)(2,1)} %get-tuple-element.93), calls=%async_computation.6 | async-start | bytes 8388608 | tf_op jit(solution)/shard_map/cond/branch_0_fun/all_to_all | solution.py:621
  196.6 40.1 %all-to-all-start.5 = ((bf16[128,80,128]{2,1,0:T(8,128)(2,1)}), bf16[128,80,128]{2,1,0:T(8,128)(2,1)}, u32[]{:S(2)}, u32[]{:S(2)}) async-start(bf16[128,80,128]{2,1,0:T(8,128)(2,1)} %get-tuple-element.91), calls=%async_computation.5 | async-start | bytes 5242880 | tf_op jit(solution)/shard_map/cond/branch_0_fun/all_to_all | solution.py:621
  210.7 43.4 %copy-start.2 = (f32[3,136,128]{2,1,0:T(8,128)S(1)}, f32[3,136,128]{2,1,0:T(8,128)}, u32[]{:S(2)}) copy-start(f32[3,136,128]{2,1,0:T(8,128)} %get-tuple-element.96) | copy-start | bytes 626692 | tf_op jit(solution)/shard_map/cond
  210.7 43.4 %copy-start.3 = (f32[3,136,128]{2,1,0:T(8,128)S(1)}, f32[3,136,128]{2,1,0:T(8,128)}, u32[]{:S(2)}) copy-start(f32[3,136,128]{2,1,0:T(8,128)} %get-tuple-element.97) | copy-start | bytes 626692 | tf_op jit(solution)/shard_map/cond
  246.2 8.6 %collective-permute-start = (f32[64,16,512]{2,1,0:T(8,128)}, f32[64,16,512]{2,1,0:T(8,128)}, u32[]{:S(2)}, u32[]{:S(2)}) collective-permute-start(f32[64,16,512]{2,1,0:T(8,128)} %get-tuple-element.95), channel_id=1, source_target_pairs={{0,16},{16,0},{32,48},{48,32},{64,80},{80,64},{96,112},{112,96},{1... | collective-permute-start | bytes 6291464 | tf_op jit(solution)/shard_map/cond/branch_0_fun/ppermute | solution.py:692
  249.5 18.4 %all-to-all-start.7 = ((f32[128,8,128]{2,1,0:T(8,128)}), f32[128,8,128]{2,1,0:T(8,128)}, u32[]{:S(2)}, u32[]{:S(2)}) async-start(f32[128,8,128]{2,1,0:T(8,128)} %add_up.2), calls=%async_computation.7 | async-start | bytes 1048576 | tf_op jit(solution)/shard_map/cond/branch_0_fun/all_to_all | solution.py:621
  267.8 1.8 copy-start.10
